TPU v7x, 128 devices: a whole 4x4x4 slice. The times are simulated.
128 devices in a mesh: req: 32 (over x, z, core), tp: 4 (over y).
Axes of the slice: x: 4, y: 4, z: 4, core: 2. Of those that a mesh axis runs over, the one named last changes fastest.
Arguments:
- tokens: bfloat16 [65536, 1024], P('req'), may hold values from -6 to 6
- attn_gain: bfloat16 [1024], replicated, may hold values from 0.5 to 1.5
- w_query: bfloat16 [1024, 1024], P(None, 'tp'), may hold values from -1 to 1
- w_key: bfloat16 [1024, 1024], P(None, 'tp'), may hold values from -1 to 1
- w_value: bfloat16 [1024, 1024], P(None, 'tp'), may hold values from -0.1875 to 0.1875
- persist_key: bfloat16 [16, 1024], P(None, 'tp'), may hold values from -250 to 250
- persist_value: bfloat16 [16, 1024], P(None, 'tp'), may hold values from -6 to 6
- log_forget: float32 [65536, 8], P('req', 'tp'), may hold values from -0.75 to 0
- mem_gain: float32 [1024], P('tp'), may hold values from 0.5 to 1.5
- w_out: bfloat16 [1024, 1024], P('tp'), may hold values from -0.1875 to 0.1875
- ffn_gain: bfloat16 [1024], replicated, may hold values from 0.5 to 1.5
- w_gate: bfloat16 [1024, 2816], P(None, 'tp'), may hold values from -0.1875 to 0.1875
- w_up: bfloat16 [1024, 2816], P(None, 'tp'), may hold values from -0.1875 to 0.1875
- w_down: bfloat16 [2816, 1024], P('tp'), may hold values from -0.109375 to 0.109375
- doc_ids: int32 [65536], P('req'), may hold values from 0 to 512, never falling along the last dimension, each value on 1 to 32768 neighbouring positions
- page_owner: int32 [512], P('req'), may hold values from 0 to 31, as said below
- page_slot: int32 [512], P('req'), may hold values from 0 to 15
Outputs:
- layer_out: bfloat16 [65536, 1024], P('req')
- kv_cache: bfloat16 [512, 128, 2048], P('req', None, 'tp')
Inputs may be any that keep to these rules, and one draw needn't show every extreme that they name: `page_owner`: the pages of one index of req going to one owner number at most 1, and every owner receives exactly 16 pages, one for each of its slots.
All inputs are finite; a program needn't handle non-finite values.
Results may differ from a plain program's by a relative error of at most 0.015.
Values may be sent and summed in bfloat16 or wider, within the bound.
No kernel may reach another device: no remote copies, remote signals or barrier semaphores. Data moves between devices by JAX's collectives and lax.ppermute only.
A program may use at most 128 MiB of HBM per device.

v0:
```python
import functools
import math

import jax
import jax.numpy as jnp
from jax import lax
from jax.experimental import pallas as pl
from jax.experimental.pallas import tpu as pltpu
from jax.sharding import PartitionSpec as P

HD = 128
SEG = 1024
PAGE = 128
CH = 256
ROWS = 256
F32 = jnp.float32
BF = jnp.bfloat16
ANY = pl.ANY


def rms(x, eps):
    return x * lax.rsqrt(jnp.mean(x * x, axis=-1, keepdims=True) + eps)


def dot(a, b):
    return jnp.dot(a, b, preferred_element_type=F32)


def dot_t(a, b):
    return lax.dot_general(a, b, (((1,), (1,)), ((), ())), preferred_element_type=F32)


def dot_l(a, b):
    return lax.dot_general(a, b, (((0,), (0,)), ((), ())), preferred_element_type=F32)


def tri(n, lower=True):
    r = lax.broadcasted_iota(jnp.int32, (n, n), 0)
    c = lax.broadcasted_iota(jnp.int32, (n, n), 1)
    return (r >= c) if lower else (r <= c)


def split3(x):
    hi = x.astype(BF).astype(F32)
    mid = (x - hi).astype(BF).astype(F32)
    return hi, mid, x - hi - mid


def running(info):
    parts = jnp.concatenate(split3(info), axis=0).astype(BF)
    c = dot(parts, tri(info.shape[1], False).astype(F32).astype(BF))
    c = c[0:8] + c[8:16] + c[16:24]
    return jnp.where(lax.broadcasted_iota(jnp.int32, info.shape, 0) == 0, info, c)


def normed(tok, gain, out):
    g = gain[...].astype(F32)
    for b in range(CH // 32):
        r = slice(b * 32, (b + 1) * 32)
        out[r, :] = (rms(tok[r, :].astype(F32), 1e-5) * g).astype(BF)


def project_kernel(owner, tok0, tok1, tok2, gain, wq, wk, wv, row, codes, q_out, kv_out, ku_out, min_out, pay_out, cr_out, cc_out, sent, st, misc, buf, n0, n1, sem):
    i = pl.program_id(0)
    here = CH // PAGE
    last_sem = 2 * here

    @pl.when(i == 0)
    def _():
        st[...] = jnp.zeros_like(st)
        misc[...] = jnp.full_like(misc, -1.0)
        misc[0:2, :] = jnp.zeros((2, 128), F32)
        pltpu.make_async_copy(codes, sent.at[:, pl.ds(PAGE, 8), :], sem.at[last_sem]).start()
        normed(tok0, gain, n0)

    copies = []
    for j, (now, tok, later) in enumerate(((n0, tok1, n1), (n1, tok2, n0))):
        r = slice(j * CH, (j + 1) * CH)
        n = now[...]
        k = dot(n, wk[...]).astype(BF)
        v = dot(n, wv[...]).astype(BF)
        q_out[r, :] = dot(n, wq[...]).astype(BF)
        for h in range(2):
            s = slice(h * HD, (h + 1) * HD)
            kv_out[r, 2 * h * HD : (2 * h + 1) * HD] = k[:, s]
            kv_out[r, (2 * h + 1) * HD : (2 * h + 2) * HD] = v[:, s]
            for p in range(here):
                w = slice(p * PAGE, (p + 1) * PAGE)
                buf[j * here + p, :, 2 * h * HD : (2 * h + 1) * HD] = k[w, s]
                buf[j * here + p, :, (2 * h + 1) * HD : (2 * h + 2) * HD] = v[w, s]
        for p in range(here):
            m = j * here + p
            c = pltpu.make_async_copy(buf.at[m], sent.at[owner[i * 2 * here + m], pl.ds(0, PAGE), :], sem.at[m])
            c.start()
            copies.append(c)
        normed(tok, gain, later)
        cr = running(row[:, r])
        cc = cr.T
        cr_out[:, r] = cr
        cc_out[r, :] = cc
        last = cr[0:1, CH - 1 : CH]
        same = (cc[:, 0:1] == last).astype(F32)
        last_row = jnp.broadcast_to(last, (1, 128))
        cont = (last_row == misc[2:3, :]).astype(F32)
        for h in range(2):
            s = slice(h * HD, (h + 1) * HD)
            ku = rms(k[:, s].astype(F32), 1e-6) * (1.0 / math.sqrt(HD))
            ku_out[r, s] = ku.astype(BF)
            end_h = cr[1 + h : 2 + h, CH - 1 : CH]
            w = jnp.exp(end_h - cc[:, 1 + h : 2 + h]) * same
            add = dot_l((ku * w).astype(BF), v[:, s])
            end_row = jnp.broadcast_to(end_h, (1, 128))
            old = st[h]
            min_out[j, h] = old
            st[h] = old * (jnp.exp(end_row) * cont) + add
            misc[h : h + 1, :] = misc[h : h + 1, :] + end_row
        misc[2:3, :] = last_row

    @pl.when(i == pl.num_programs(0) - 1)
    def _():
        write_payload(pay_out, st, misc[0:1, :], misc[1:2, :], misc[2:3, :])
        pltpu.make_async_copy(codes, sent.at[:, pl.ds(PAGE, 8), :], sem.at[last_sem]).wait()

    for c in copies:
        c.wait()


def write_payload(out, st, l0, l1, last):
    hi = jnp.floor(last * (1.0 / 256.0))
    rows = [*split3(l0), *split3(l1), hi, last - hi * 256.0]
    tail = jnp.concatenate(rows, axis=0).astype(BF)
    for i in range(out.shape[0]):
        for h in range(2):
            out[i, h * HD : (h + 1) * HD, :] = st[h].astype(BF)
        out[i, 2 * HD : 2 * HD + 8, :] = tail


def read_payload(ref, j):
    s = ref[j, 2 * HD : 2 * HD + 8, :].astype(F32)
    l0 = s[0:1] + s[1:2] + s[2:3]
    l1 = s[3:4] + s[4:5] + s[5:6]
    return l0, l1, s[6:7] * 256.0 + s[7:8]


def project(owner, tokens, gain, wq, wk, wv, row, codes):
    t, d = tokens.shape
    tile = 512
    n = t // tile
    c = tile // CH
    full = lambda a: pl.BlockSpec(a.shape, lambda i, o: (0,) * a.ndim)
    rows = lambda w: pl.BlockSpec((tile, w), lambda i, o: (i, 0))
    lanes = pl.BlockSpec((8, tile), lambda i, o: (0, i))
    gs = pltpu.PrefetchScalarGridSpec(
        num_scalar_prefetch=1,
        grid=(n,),
        in_specs=[
            pl.BlockSpec((CH, d), lambda i, o: (0, 0)),
            pl.BlockSpec((CH, d), lambda i, o: (2 * i + 1, 0)),
            pl.BlockSpec((CH, d), lambda i, o: (jnp.minimum(2 * i + 2, 2 * n - 1), 0)),
            full(gain), full(wq), full(wk), full(wv), lanes, full(codes),
        ],
        out_specs=[
            rows(256),
            rows(512),
            rows(256),
            pl.BlockSpec((c, 2, HD, HD), lambda i, o: (i, 0, 0, 0)),
            pl.BlockSpec((8, 264, 128), lambda i, o: (0, 0, 0)),
            lanes,
            rows(8),
            pl.BlockSpec(memory_space=ANY),
        ],
        scratch_shapes=[
            pltpu.VMEM((2, HD, HD), F32),
            pltpu.VMEM((8, 128), F32),
            pltpu.VMEM((tile // PAGE, PAGE, 512), BF),
            pltpu.VMEM((CH, d), BF),
            pltpu.VMEM((CH, d), BF),
            pltpu.SemaphoreType.DMA((tile // PAGE + 1,)),
        ],
    )
    return pl.pallas_call(
        project_kernel,
        grid_spec=gs,
        out_shape=[
            jax.ShapeDtypeStruct((t, 256), BF),
            jax.ShapeDtypeStruct((t, 512), BF),
            jax.ShapeDtypeStruct((t, 256), BF),
            jax.ShapeDtypeStruct((t // CH, 2, HD, HD), F32),
            jax.ShapeDtypeStruct((8, 264, 128), BF),
            jax.ShapeDtypeStruct((8, t), F32),
            jax.ShapeDtypeStruct((t, 8), F32),
            jax.ShapeDtypeStruct((codes.shape[0], PAGE + 8, 512), BF),
        ],
        name="project",
    )(owner, tokens, tokens, tokens, gain, wq, wk, wv, row, codes)


def combine_kernel(place, got, e_out, info_out, pay_out, st):
    g = place[0]
    st[...] = jnp.zeros_like(st)
    e_out[...] = jnp.zeros_like(e_out)
    cur = jnp.full((1, 128), -1.0, F32)
    t0 = t1 = jnp.zeros((1, 128), F32)
    i0, i1, il = t0, t1, cur
    for j in range(8):
        @pl.when(g == j)
        def _():
            e_out[...] = st[...]

        here = g == j
        i0, i1, il = jnp.where(here, t0, i0), jnp.where(here, t1, i1), jnp.where(here, cur, il)
        l0, l1, last = read_payload(got, j)
        cont = (cur == last).astype(F32)
        for h, l in ((0, l0), (1, l1)):
            st[h] = st[h] * (jnp.exp(l) * cont) + got[j, h * HD : (h + 1) * HD, :].astype(F32)
        t0, t1, cur = t0 + l0, t1 + l1, last
    info_out[...] = jnp.concatenate([i0, i1, il, jnp.zeros((5, 128), F32)], axis=0)
    write_payload(pay_out, st, t0, t1, cur)


def combine(place, got):
    vm = pl.BlockSpec(memory_space=pltpu.VMEM)
    return pl.pallas_call(
        combine_kernel,
        in_specs=[pl.BlockSpec(memory_space=pltpu.SMEM), vm],
        out_specs=[vm, vm, vm],
        out_shape=[
            jax.ShapeDtypeStruct((2, HD, HD), F32),
            jax.ShapeDtypeStruct((8, 128), F32),
            jax.ShapeDtypeStruct((4, 264, 128), BF),
        ],
        scratch_shapes=[pltpu.VMEM((2, HD, HD), F32)],
        name="combine",
    )(place, got)


def attend_kernel(q, k, v, pk, pv, col, row, out):
    scale = 1.0 / math.sqrt(HD)
    c = scale * math.log2(math.e)
    mask = tri(CH)
    for i in range(SEG // CH):
        r = slice(i * CH, (i + 1) * CH)
        qi = q[r, :]
        doc = col[r, 0:1]
        sp = dot_t(qi, pk[...])
        sd = dot_t(qi, k[r, :])
        sd = jnp.where(mask & (doc == row[0:1, r]), sd, -1e30)
        m = jnp.maximum(jnp.max(sp, axis=-1, keepdims=True), jnp.max(sd, axis=-1, keepdims=True))
        if i:
            e = slice(0, i * CH)
            so = dot_t(qi, k[e, :])
            so = jnp.where(doc == row[0:1, e], so, -1e30)
            m = jnp.maximum(m, jnp.max(so, axis=-1, keepdims=True))
        wp = jnp.exp2((sp - m) * c)
        wd = jnp.exp2((sd - m) * c)
        total = jnp.sum(wp, axis=-1, keepdims=True) + jnp.sum(wd, axis=-1, keepdims=True)
        acc = dot(wp.astype(BF), pv[...]) + dot(wd.astype(BF), v[r, :])
        if i:
            wo = jnp.exp2((so - m) * c)
            total = total + jnp.sum(wo, axis=-1, keepdims=True)
            acc = acc + dot(wo.astype(BF), v[e, :])
        out[r, :] = acc / total


def attend(q, kv, pk, pv, col, row, seg, h0=0, heads=2):
    return pl.pallas_call(
        attend_kernel,
        grid=(heads,),
        in_specs=[
            pl.BlockSpec((SEG, HD), lambda h: (seg, h + h0)),
            pl.BlockSpec((SEG, HD), lambda h: (seg, 2 * (h + h0))),
            pl.BlockSpec((SEG, HD), lambda h: (seg, 2 * (h + h0) + 1)),
            pl.BlockSpec((16, HD), lambda h: (0, h + h0)),
            pl.BlockSpec((16, HD), lambda h: (0, h + h0)),
            pl.BlockSpec((SEG, 8), lambda h: (seg, 0)),
            pl.BlockSpec((8, SEG), lambda h: (0, seg)),
        ],
        out_specs=pl.BlockSpec((SEG, HD), lambda h: (0, h)),
        out_shape=jax.ShapeDtypeStruct((SEG, heads * HD), F32),
        name="attend",
        cost_estimate=pl.CostEstimate(flops=700_000_000 * heads, transcendentals=0, bytes_accessed=2_000_000 * heads),
    )(q, kv, kv, pk, pv, col, row)


def recall_kernel(half, place, bound, q, ku, kv, mi, e1, info, got, col, row, rows, at0, at1, gain, out, pst, pdoc):
    b = pl.program_id(0)
    chunk = 2 * b + half

    @pl.when(b == 0)
    def _():
        x, g = place[1], place[0]
        st = [jnp.zeros((HD, HD), F32)] * 2
        cur = jnp.full((1, 128), -1.0, F32)
        pst[...] = jnp.zeros_like(pst)
        il = cur
        for j in range(4):
            here = x == j
            il = jnp.where(here, cur, il)
            for h in range(2):
                pst[h] = jnp.where(here, st[h], pst[h])
            l0, l1, last = read_payload(got, j)
            cont = (cur == last).astype(F32)
            for h, l in ((0, l0), (1, l1)):
                st[h] = st[h] * (jnp.exp(l) * cont) + got[j, h * HD : (h + 1) * HD, :].astype(F32)
            cur = last
        glast = info[2:3, :]
        first = g == 0
        ok = jnp.where(first, 1.0, (il == glast).astype(F32))
        for h in range(2):
            pst[h] = pst[h] * (jnp.exp(info[h : h + 1, :]) * ok) + e1[h]
        pdoc[0:1, :] = jnp.where(first, il, glast)

    mask = tri(CH)
    pos = lax.broadcasted_iota(jnp.int32, rows.shape, 1)
    ends = (pos < chunk * CH) & (lax.rem(pos, CH) == CH - 1)
    pre = jnp.sum(jnp.where(ends, rows[...], 0.0), axis=1, keepdims=True)
    doc = col[:, 0:1]
    pdoc_row = pdoc[0:1, :]
    carried = jnp.where(chunk == 0, pdoc_row, bound[chunk])
    joined = (carried == pdoc_row).astype(F32)
    live = (doc == carried[:, 0:1]).astype(F32)
    ok = mask & (doc == row[0:1, :])
    for h in range(2):
        s = slice(h * HD, (h + 1) * HD)
        qh = q[:, s]
        cc = col[:, 1 + h : 2 + h]
        dec = jnp.exp(jnp.where(ok, cc - row[1 + h : 2 + h, :], -1e30))
        inner = (dot_t(qh, ku[:, s]) * dec).astype(BF)
        rec = dot(inner, kv[:, (2 * h + 1) * HD : (2 * h + 2) * HD])
        f = jnp.exp(jnp.broadcast_to(pre[1 + h : 2 + h, :], (1, 128))) * joined
        m = mi[0, h] + pst[h] * f
        rec = rec + dot(qh, m.astype(BF)) * (jnp.exp(cc) * live)
        qw = qh.astype(F32)
        rec = rec * (lax.rsqrt(jnp.mean(qw * qw, axis=-1, keepdims=True) + 1e-6) * (1.0 / math.sqrt(HD)))
        at = jnp.where(chunk < SEG // CH, at0[:, s], at1[:, s])
        out[0, :, s] = (at + rms(rec, 1e-5) * gain[:, s]).astype(BF)


def recall(half, place, bound, q, ku, kv, mi, e1, info, got, col, row, at0, at1, gain):
    ch = lambda w: pl.BlockSpec((CH, w), lambda b, p, d: (2 * b + half, 0))
    full = lambda a: pl.BlockSpec(a.shape, lambda b, p, d: (0,) * a.ndim)
    per = SEG // CH
    gs = pltpu.PrefetchScalarGridSpec(
        num_scalar_prefetch=2,
        grid=(4,),
        in_specs=[
            ch(256),
            ch(256),
            ch(512),
            pl.BlockSpec((1, 2, HD, HD), lambda b, p, d: (2 * b + half, 0, 0, 0)),
            full(e1),
            full(info),
            full(got),
            ch(8),
            pl.BlockSpec((8, CH), lambda b, p, d: (0, 2 * b + half)),
            full(row),
            pl.BlockSpec((CH, 256), lambda b, p, d: (jnp.minimum(2 * b + half, per - 1), 0)),
            pl.BlockSpec((CH, 256), lambda b, p, d: (jnp.maximum(2 * b + half - per, 0), 0)),
            full(gain),
        ],
        out_specs=pl.BlockSpec((1, CH, 256), lambda b, p, d: (lax.rem(b - p[2] + 4, 4), 0, 0)),
        scratch_shapes=[pltpu.VMEM((2, HD, HD), F32), pltpu.VMEM((8, 128), F32)],
    )
    return pl.pallas_call(
        functools.partial(recall_kernel, half),
        grid_spec=gs,
        out_shape=jax.ShapeDtypeStruct((4, CH, 256), BF),
        name="recall",
        cost_estimate=pl.CostEstimate(flops=400_000_000, transcendentals=0, bytes_accessed=4_000_000),
    )(place, bound, q, ku, kv, mi, e1, info, got, col, row, row, at0, at1, gain)


def ffn_kernel(place, tok, gain, h0, h1, h2, h3, *rest):
    own = rest[0:4]
    gu = (rest[4:8], rest[8:12])
    do = (rest[12:15], rest[15:18])
    out, wgu, wd, wo, norm, acc, sem = rest[18:]
    core = place[3]
    count = [0]
    waits = {}

    def copy(key, src, dst):
        c = pltpu.make_async_copy(src, dst, sem.at[count[0]])
        count[0] += 1
        waits.setdefault(key, []).append(c)
        c.start()

    def fetch(kind, group):
        key = (kind, group)
        if group == 0:
            if kind == "out":
                copy(key, own[3], wo.at[0])
            elif kind == "up":
                copy(key, own[0], wgu.at[0, 0])
                copy(key, own[1], wgu.at[1, 0])
            else:
                copy(key, own[2], wd.at[0])
            return
        spots = (1, 2) if group == 1 else (3,)
        for which in range(2):
            at = core if which == 0 else 1 - core
            if kind == "up":
                pos = jnp.where(at == 0, place[1], place[4])
                span = pl.ds(spots[0], len(spots))
                for i, hop in enumerate((0, 3, 1, 2)):
                    p = lax.rem(pos + hop, 4)
                    copy(key, gu[which][i].at[pl.ds(spots[0] - 1, len(spots))], wgu.at[at, span, pl.ds(p * 176, 176), :])
                continue
            for i in spots:
                if kind == "down":
                    copy(key, do[which][i - 1].at[pl.ds(0, 352), :], wd.at[i, pl.ds(at * 352, 352), :])
                else:
                    copy(key, do[which][i - 1].at[pl.ds(352, 128), :], wo.at[i, pl.ds(at * 128, 128), :])

    def ready(kind, group):
        for c in waits[(kind, group)]:
            c.wait()

    for group in range(3):
        fetch("out", group)
    fetch("up", 0)
    fetch("down", 0)
    total = tok[...].astype(F32)
    for i, (h, group) in enumerate(((h0, 0), (h1, 1), (h3, None), (h2, 2))):
        if group is not None:
            ready("out", group)
        total = total + dot(h[...], wo[i])
    for group in (1, 2):
        fetch("up", group)
        fetch("down", group)
    resid = total.astype(BF).astype(F32)
    acc[...] = resid
    norm[...] = (rms(resid, 1e-5) * gain[...].astype(F32)).astype(BF)

    def step(i, carry):
        for index, group in ((0, 0), (1, 1), (3, 2)):
            @pl.when(i == index)
            def _():
                ready("up", group)
                ready("down", group)

        n = norm[...]
        g = dot_t(n, wgu[0, i])
        u = dot_t(n, wgu[1, i])
        hid = (g / (1.0 + jnp.exp(-g)) * u).astype(BF)
        acc[...] += dot(hid, wd[i])
        return carry

    lax.fori_loop(0, 4, step, 0)
    out[...] = acc[...].astype(BF)


def ffn(half, place, tokens, gain, heads, own, gu, gux, do, dox):
    d = tokens.shape[1]
    full = lambda a: pl.BlockSpec(a.shape, lambda i, p: (0,) * a.ndim)
    anys = pl.BlockSpec(memory_space=ANY)
    ws = [*own, *gu, *gux, *do, *dox]
    gs = pltpu.PrefetchScalarGridSpec(
        num_scalar_prefetch=1,
        grid=(1,),
        in_specs=[pl.BlockSpec((ROWS, d), lambda i, p: (2 * p[2] + half, 0)), full(gain)]
        + [full(h) for h in heads]
        + [anys] * len(ws),
        out_specs=pl.BlockSpec((ROWS, d), lambda i, p: (0, 0)),
        scratch_shapes=[
            pltpu.VMEM((2, 4, 704, 1024), BF),
            pltpu.VMEM((4, 704, 1024), BF),
            pltpu.VMEM((4, 256, 1024), BF),
            pltpu.VMEM((ROWS, d), BF),
            pltpu.VMEM((ROWS, d), F32),
            pltpu.SemaphoreType.DMA((32,)),
        ],
    )
    return pl.pallas_call(
        ffn_kernel,
        grid_spec=gs,
        out_shape=jax.ShapeDtypeStruct((ROWS, d), BF),
        name="ffn",
    )(place, tokens, gain, *heads, *ws)


def staged(ins, bufs, outs, sem):
    n = len(ins)
    first = [pltpu.make_async_copy(ins[i], bufs[i], sem.at[i]) for i in range(n)]
    second = [pltpu.make_async_copy(bufs[i], outs[i], sem.at[n + i]) for i in range(n)]
    for c in first:
        c.start()
    for a, b in zip(first, second):
        a.wait()
        b.start()
    for c in second:
        c.wait()


def place_kernel(source, got, out, buf, sem):
    n = out.shape[0]
    staged(
        [got.at[source[s], pl.ds(0, PAGE), :] for s in range(n)],
        [buf.at[s] for s in range(n)],
        [out.at[s] for s in range(n)],
        sem,
    )


def place_pages(source, got, count):
    anys = pl.BlockSpec(memory_space=ANY)
    shape = (count, PAGE, got.shape[2])
    return pl.pallas_call(
        place_kernel,
        in_specs=[pl.BlockSpec(memory_space=pltpu.SMEM), anys],
        out_specs=anys,
        out_shape=jax.ShapeDtypeStruct(shape, BF),
        scratch_shapes=[pltpu.VMEM(shape, BF), pltpu.SemaphoreType.DMA((2 * count,))],
        name="place",
    )(source, got)


def join_kernel(spots, place, *refs):
    pieces, out, bufs, sem = refs[: len(spots)], refs[-2 - len(spots)], refs[-1 - len(spots) : -1], refs[-1]
    y = place[2]
    outs = []
    for d, row, n in spots:
        outs.append(out.at[pl.ds(lax.rem(y + d, 4) * (2 * ROWS) + row, n), :])
    staged(pieces, bufs, outs, sem)


def join(place, pieces, spots, into=None):
    anys = pl.BlockSpec(memory_space=ANY)
    rest = [] if into is None else [into]
    width = pieces[0].shape[1]
    return pl.pallas_call(
        functools.partial(join_kernel, spots),
        in_specs=[pl.BlockSpec(memory_space=pltpu.SMEM)] + [anys] * (len(pieces) + len(rest)),
        out_specs=anys,
        out_shape=jax.ShapeDtypeStruct((8 * ROWS, width), BF),
        scratch_shapes=[pltpu.VMEM(p.shape, BF) for p in pieces] + [pltpu.SemaphoreType.DMA((2 * len(pieces),))],
        input_output_aliases={} if into is None else {1 + len(pieces): 0},
        name="join",
    )(place, *pieces, *rest)


def on_device(
    tokens, attn_gain, w_query, w_key, w_value, persist_key, persist_value, log_forget, mem_gain,
    w_out, ffn_gain, w_gate, w_up, w_down, doc_ids, page_owner, page_slot,
):
    count = tokens.shape[0]
    reqs = lax.axis_size("req")
    req, y = lax.axis_index("req"), lax.axis_index("tp")
    core, x, z = req % 2, req // 8, (req // 2) % 4
    place = jnp.stack([req % 8, x, y, core, z]).astype(jnp.int32)
    shift = lambda a, d: lax.ppermute(a, "tp", [(i, (i + d) % 4) for i in range(4)])
    swap = lambda a: lax.ppermute(a, "req", [(i, i ^ 1) for i in range(reqs)])
    tie = lambda *a: lax.optimization_barrier(a)

    def around(a, d):
        def to(i):
            xx, zz, c = i // 8, (i // 2) % 4, i % 2
            if c == 0:
                xx = (xx + d) % 4
            else:
                zz = (zz + d) % 4
            return xx * 8 + zz * 2 + c

        return lax.ppermute(a, "req", [(i, to(i)) for i in range(reqs)])

    gate, up = w_gate.T, w_up.T
    at = jnp.where(core == 0, x, z)
    cut = lambda w, i, n: lax.dynamic_slice_in_dim(w, i * n, n, 0)
    piece = jnp.where(core == 0, cut(gate, at, 176), cut(up, at, 176))
    s1, s3, s2 = [shift(piece, d) for d in (1, 3, 2)]
    half_do = jnp.concatenate([cut(w_down, core, 352), cut(w_out, core, 128)])
    do1, do3, do2 = [shift(half_do, d) for d in (1, 3, 2)]

    doc = doc_ids.astype(F32)
    row = jnp.concatenate([doc[None], log_forget.T, jnp.zeros((5, count), F32)])
    bound = jnp.concatenate([jnp.full((1,), -1.0, F32), doc[CH - 1 : -1 : CH]])

    hit = page_owner[None, :] == jnp.arange(reqs)[:, None]
    code = jnp.sum(jnp.where(hit, page_slot[None, :] + 1, 0), axis=1).astype(BF)
    codes = jnp.broadcast_to(code[:, None, None], (reqs, 8, 512))
    q, kv, ku, mi, pay, row, col, outgoing = project(
        page_owner, tokens, attn_gain[None], w_query, w_key, w_value, row, codes
    )

    group8 = [[i * 8 + k for k in range(8)] for i in range(reqs // 8)]
    group4 = [[i * 8 + k for i in range(reqs // 8)] for k in range(8)]
    spread = lambda a, g: lax.all_to_all(a, "req", 0, 0, tiled=True, axis_index_groups=g)
    got8 = spread(pay, group8)

    at0 = attend(q, kv, persist_key, persist_value, col, row, 0)
    at0, got8 = tie(at0, got8)
    e1, info, pay4 = combine(place, got8)
    got4 = spread(pay4, group4)
    q1, at0, s1, s2, s3, _ = tie(q, at0, s1, s2, s3, pay4)
    at1 = attend(q1, kv, persist_key, persist_value, col, row, 1)
    at1, got4, s1, s2, s3, do1, do3 = tie(at1, got4, s1, s2, s3, do1, do3)
    near = jnp.stack([s1, s3, s2])
    far = [around(near, d) for d in (1, 3, 2)]

    gain = mem_gain[None]
    own_w = (gate, up, w_down, w_out)
    mem = lambda half: recall(half, place, bound, q, ku, kv, mi, e1, info, got4, col, row, at0, at1, gain)
    send = lambda out: [out[0]] + [shift(out[d], d) for d in (1, 3, 2)]
    out0 = mem(0)
    heads0 = send(out0)
    out1 = mem(1)
    out1, do2, *heads0 = tie(out1, do2, *heads0)
    heads1 = send(out1)
    outgoing, near, out1, *far = tie(outgoing, near, out1, *far)
    arrived = lax.all_to_all(outgoing, "req", 0, 0, tiled=True)
    gu, do = [near, *far], [do1, do3, do2]
    gux, dox = [swap(a) for a in gu], [swap(a) for a in do]
    slots = arrived[:, PAGE, 0].astype(F32)
    wanted = slots[None, :] == (jnp.arange(count // PAGE) + 1).astype(F32)[:, None]
    source = jnp.sum(jnp.where(wanted, jnp.arange(reqs)[None, :], 0), axis=1).astype(jnp.int32)
    kv_cache = place_pages(jnp.clip(source, 0, reqs - 1), arrived, count // PAGE)

    feed = lambda half, heads: ffn(
        half, place, tokens, ffn_gain[None], (heads[0], heads[1], heads[3], heads[2]), own_w, gu, gux, do, dox
    )
    R, H = ROWS, ROWS // 2
    own0 = feed(0, heads0)
    own0, *heads1 = tie(own0, *heads1)
    a0, b0 = shift(own0, 1), shift(own0, -1)
    own1 = feed(1, heads1)
    a1, b1 = shift(own1, 1), shift(own1, -1)
    lo0, hi0 = shift(a0[:H], 1), shift(b0[H:], -1)
    joined = join(place, [own0, a0, b0, own1], ((0, 0, R), (3, 0, R), (1, 0, R), (0, R, R)))
    a1, b1, joined, kv_cache = tie(a1, b1, joined, kv_cache)
    lo1, hi1 = shift(a1[:H], 1), shift(b1[H:], -1)
    joined = join(place, [a1, b1, lo0, hi0], ((3, R, R), (1, R, R), (2, 0, H), (2, H, H)), joined)
    lo1, hi1, joined = tie(lo1, hi1, joined)
    layer_out = join(place, [lo1, hi1], ((2, R, H), (2, R + H, H)), joined)
    return layer_out, kv_cache


def solution(mesh):
    return jax.shard_map(
        on_device,
        mesh=mesh,
        in_specs=(
            P("req", None), P(), P(None, "tp"), P(None, "tp"), P(None, "tp"), P(None, "tp"), P(None, "tp"),
            P("req", "tp"), P("tp"), P("tp", None), P(), P(None, "tp"), P(None, "tp"), P("tp", None),
            P("req"), P("req"), P("req"),
        ),
        out_specs=(P("req", None), P("req", None, "tp")),
        check_vma=False,
    )
```

profile of v0, /device:TPU:32, one launch (start us, length us, event | category | flops | bytes accessed | tf_op | source)
XLA Modules:
  0.0 175.1 jit_solution(11133988709546071604)
XLA Ops:
  0.7 1.0 constant_dynamic-slice_fusion
  1.7 1.2 constant_dynamic-slice_fusion.1
  2.9 1.0 pad_maximum_fusion.1
  3.9 3.0 %collective-permute-start.4 = (bf16[480,1024]{1,0:T(8,128)(2,1)}, bf16[480,1024]{1,0:T(8,128)(2,1)S(1)}, u32[]{:S(2)}, u32[]{:S(2)}) collective-permute-start(bf16[480,1024]{1,0:T(8,128)(2,1)} %pad_maximum_fusion.1), channel_id=1, source_target_pairs={{0,3},{1,0},{2,1},{3,2},{4,7},{5,4},{6,5},{7,6},{8,11},{9,8},{10,9... | collective-permute-start | bytes 2949128 | tf_op jit(solution)/shard_map/ppermute | solution.py:551
  7.0 0.6 broadcast_in_dim.53.gain
  7.7 0.7 maximum_maximum_fusion.row
  8.4 0.8 broadcast_in_dim.58.codes
  9.2 12.9 %project.1 = (bf16[2048,256]{1,0:T(8,128)(2,1)}, bf16[2048,512]{1,0:T(8,128)(2,1)}, bf16[2048,256]{1,0:T(8,128)(2,1)}, f32[8,2,128,128]{3,2,1,0:T(8,128)}, bf16[...) custom-call(s32[16]{0:T(128)} %owner.1, ...), custom_call_target="tpu_custom_call" | custom-call | tf_op jit(solution)/shard_map/project/pallas_call | solution.py:181
  22.1 5.4 %all-to-all-start = ((bf16[8,264,128]{2,1,0:T(8,128)(2,1)}), bf16[8,264,128]{2,1,0:T(8,128)(2,1)S(1)}, u32[]{:S(2)}, u32[]{:S(2)}) async-start(bf16[8,264,128]{2,1,0:T(8,128)(2,1)} %get-tuple-element.56), calls=%async_computation | async-start | bytes 1081344 | tf_op jit(solution)/shard_map/all_to_all | solution.py:587
  27.5 1.2 select_bitcast_fusion
  28.7 3.3 %collective-permute-start.2 = (bf16[176,1024]{1,0:T(8,128)(2,1)S(1)}, bf16[176,1024]{1,0:T(8,128)(2,1)S(1)}, u32[]{:S(2)}, u32[]{:S(2)}) collective-permute-start(bf16[176,1024]{1,0:T(8,128)(2,1)S(1)} %select_bitcast_fusion), channel_id=1, source_target_pairs={{0,3},{1,0},{2,1},{3,2},{4,7},{5,4},{6,5},{7,6},{8,11},{9,8},{10,9... | collective-permute-start | bytes 1081352 | tf_op jit(solution)/shard_map/ppermute | solution.py:551
  32.0 0.9 collective-permute-start
  33.0 0.6 stack.35.place
  33.6 6.3 %attend.2.at0 = f32[1024,256]{1,0:T(8,128)} custom-call(bf16[2048,256]{1,0:T(8,128)(2,1)} %get-tuple-element.62.q, bf16[2048,512]{1,0:T(8,128)(2,1)} %get-tuple-element.52.k.v.kv, bf16[2048,512]{1,0:T(8,128)(2,1)} %get-tuple-element.52.k.v.kv, bf16[16,256]{1,0:T(8,128)(2,1)} %pk.3, bf16[16,256]{1,0:T(8,128)(2,1)} %pv.3, f32[2048,8]{1,0:T(8,128)} %get-tuple-element.54.col, ...), custom_call_target="tpu_custom_call" | custom-call | flops 1400000000 | bytes 4000000 | tf_op jit(solution)/shard_map/attend/pallas_call | solution.py:266
  39.9 0.8 copy-done.13
  40.7 2.0 %combine.1 = (f32[2,128,128]{2,1,0:T(8,128)}, f32[8,128]{1,0:T(8,128)}, bf16[4,264,128]{2,1,0:T(8,128)(2,1)}) custom-call(s32[5]{0:T(128)} %stack.35.place, bf16[8,264,128]{2,1,0:T(8,128)(2,1)} %copy-done.13), custom_call_target="tpu_custom_call" | custom-call | tf_op jit(solution)/shard_map/combine/pallas_call | solution.py:223
  42.7 4.4 %all-to-all-start.1 = ((bf16[4,264,128]{2,1,0:T(8,128)(2,1)}), bf16[4,264,128]{2,1,0:T(8,128)(2,1)S(1)}, u32[]{:S(2)}, u32[]{:S(2)}) async-start(bf16[4,264,128]{2,1,0:T(8,128)(2,1)} %get-tuple-element.61), calls=%async_computation.1 | async-start | bytes 540672 | tf_op jit(solution)/shard_map/all_to_all | solution.py:587
  47.1 0.6 collective-permute-done.2
  47.7 2.1 %collective-permute-start.5 = (bf16[480,1024]{1,0:T(8,128)(2,1)}, bf16[480,1024]{1,0:T(8,128)(2,1)}, u32[]{:S(2)}, u32[]{:S(2)}) collective-permute-start(bf16[480,1024]{1,0:T(8,128)(2,1)} %pad_maximum_fusion.1), channel_id=1, source_target_pairs={{0,2},{1,3},{2,0},{3,1},{4,6},{5,7},{6,4},{7,5},{8,10},{9,11},{10,... | collective-permute-start | bytes 2949128 | tf_op jit(solution)/shard_map/ppermute | solution.py:551
  49.8 1.5 collective-permute-done
  51.3 6.3 %attend.3.at1 = f32[1024,256]{1,0:T(8,128)} custom-call(bf16[2048,256]{1,0:T(8,128)(2,1)} %get-tuple-element.62.q, bf16[2048,512]{1,0:T(8,128)(2,1)} %get-tuple-element.52.k.v.kv, bf16[2048,512]{1,0:T(8,128)(2,1)} %get-tuple-element.52.k.v.kv, bf16[16,256]{1,0:T(8,128)(2,1)} %pk.3, bf16[16,256]{1,0:T(8,128)(2,1)} %pv.3, f32[2048,8]{1,0:T(8,128)} %get-tuple-element.54.col, ...), custom_call_target="tpu_custom_call" | custom-call | flops 1400000000 | bytes 4000000 | tf_op jit(solution)/shard_map/attend/pallas_call | solution.py:266
  57.7 0.9 copy-done.7
  59.0 1.3 pad_maximum_fusion.rest_4_
  60.3 3.2 %collective-permute-start.11 = (bf16[3,176,1024]{2,1,0:T(8,128)(2,1)S(1)}, bf16[3,176,1024]{2,1,0:T(8,128)(2,1)S(1)}, u32[]{:S(2)}, u32[]{:S(2)}) collective-permute-start(bf16[3,176,1024]{2,1,0:T(8,128)(2,1)S(1)} %pad_maximum_fusion.rest_4_), channel_id=1, source_target_pairs={{0,64},{4,20},{8,72},{12,28},{16,80},{20,4},{24,88},{28,12},{32,96... | collective-permute-start | bytes 3244040 | tf_op jit(solution)/shard_map/ppermute | solution.py:564
  63.5 1.1 collective-permute-start.10
  64.6 0.9 collective-permute-start.9
  65.6 0.6 pad_maximum_fusion.2.bound
  66.2 6.6 %recall.3 = bf16[4,256,256]{2,1,0:T(8,128)(2,1)} custom-call(s32[5]{0:T(128)} %stack.35.place, f32[8]{0:T(128)} %pad_maximum_fusion.2.bound, bf16[2048,256]{1,0:T(8,128)(2,1)} %get-tuple-element.62.q, bf16[2048,256]{1,0:T(8,128)(2,1)} %get-tuple-element.51.ku, bf16[2048,512]{1,0:T(8,128)(2,1)} %get-tuple-element.52.k.v.kv, ...), custom_call_target="tpu_custom_call" | custom-call | flops 400000000 | bytes 4000000 | tf_op jit(solution)/shard_map/recall/pallas_call | solution.py:364
  72.7 1.9 %slice_bitcast_fusion = (bf16[256,256]{1,0:T(8,128)(2,1)S(1)}, bf16[256,256]{1,0:T(8,128)(2,1)}, bf16[256,256]{1,0:T(8,128)(2,1)}, bf16[256,256]{1,0:T(8,128)(2,1)}) fusion(bf16[4,256,256]{2,1,0:T(8,128)(2,1)} %recall.3), kind=kLoop, calls=%fused_computation.3 | loop fusion | bytes 1048576 | tf_op jit(solution)/shard_map/squeeze | solution.py:603
  74.6 0.6 collective-permute-start.8
  75.2 3.1 %collective-permute-start.7 = (bf16[256,256]{1,0:T(8,128)(2,1)}, bf16[256,256]{1,0:T(8,128)(2,1)S(1)}, u32[]{:S(2)}, u32[]{:S(2)}) collective-permute-start(bf16[256,256]{1,0:T(8,128)(2,1)} %get-tuple-element.103), channel_id=1, source_target_pairs={{0,3},{1,0},{2,1},{3,2},{4,7},{5,4},{6,5},{7,6},{8,11},{9,8},{10,9... | collective-permute-start | bytes 393224 | tf_op jit(solution)/shard_map/ppermute | solution.py:551
  78.3 3.4 %collective-permute-done.8.h2 = bf16[256,256]{1,0:T(8,128)(2,1)S(1)} collective-permute-done((bf16[256,256]{1,0:T(8,128)(2,1)S(1)}, bf16[256,256]{1,0:T(8,128)(2,1)S(1)}, u32[]{:S(2)}, u32[]{:S(2)}) %collective-permute-start.8) | collective-permute-done | bytes 131104 | tf_op jit(solution)/shard_map/ppermute | solution.py:551
  82.2 6.5 %recall.2 = bf16[4,256,256]{2,1,0:T(8,128)(2,1)} custom-call(s32[5]{0:T(128)} %stack.35.place, f32[8]{0:T(128)} %pad_maximum_fusion.2.bound, bf16[2048,256]{1,0:T(8,128)(2,1)} %get-tuple-element.62.q, bf16[2048,256]{1,0:T(8,128)(2,1)} %get-tuple-element.51.ku, bf16[2048,512]{1,0:T(8,128)(2,1)} %get-tuple-element.52.k.v.kv, ...), custom_call_target="tpu_custom_call" | custom-call | flops 400000000 | bytes 4000000 | tf_op jit(solution)/shard_map/recall/pallas_call | solution.py:364
  89.4 7.0 %all-to-all-start.2 = ((bf16[32,136,512]{2,1,0:T(8,128)(2,1)}), bf16[32,136,512]{2,1,0:T(8,128)(2,1)}, u32[]{:S(2)}, u32[]{:S(2)}) async-start(bf16[32,136,512]{2,1,0:T(8,128)(2,1)} %get-tuple-element.90), calls=%async_computation.2 | async-start | bytes 8912896 | tf_op jit(solution)/shard_map/all_to_all | solution.py:610
  97.7 1.6 collective-permute-done.16.rest_15_
  99.4 0.8 copy-done.9
  100.3 1.8 %collective-permute-done.17.rest_16_ = bf16[480,1024]{1,0:T(8,128)(2,1)S(1)} collective-permute-done((bf16[480,1024]{1,0:T(8,128)(2,1)}, bf16[480,1024]{1,0:T(8,128)(2,1)S(1)}, u32[]{:S(2)}, u32[]{:S(2)}) %collective-permute-start.17) | collective-permute-done | bytes 983072 | tf_op jit(solution)/shard_map/ppermute | solution.py:552
  102.1 0.9 copy-done.10
  103.2 1.8 %slice_bitcast_fusion.4 = (bf16[256,256]{1,0:T(8,128)(2,1)}, bf16[256,256]{1,0:T(8,128)(2,1)}, bf16[256,256]{1,0:T(8,128)(2,1)S(1)}, bf16[256,256]{1,0:T(8,128)(2,1)}) fusion(bf16[4,256,256]{2,1,0:T(8,128)(2,1)} %recall.2), kind=kLoop, calls=%fused_computation.7 | loop fusion | bytes 1048576 | tf_op jit(solution)/shard_map/squeeze | solution.py:603
  105.0 3.0 %collective-permute-done.18.rest_17_ = bf16[480,1024]{1,0:T(8,128)(2,1)S(1)} collective-permute-done((bf16[480,1024]{1,0:T(8,128)(2,1)}, bf16[480,1024]{1,0:T(8,128)(2,1)S(1)}, u32[]{:S(2)}, u32[]{:S(2)}) %collective-permute-start.18) | collective-permute-done | bytes 983072 | tf_op jit(solution)/shard_map/ppermute | solution.py:552
  108.0 1.7 collective-permute-start.21
  109.7 2.0 %collective-permute-start.20 = (bf16[256,256]{1,0:T(8,128)(2,1)}, bf16[256,256]{1,0:T(8,128)(2,1)S(1)}, u32[]{:S(2)}, u32[]{:S(2)}) collective-permute-start(bf16[256,256]{1,0:T(8,128)(2,1)} %get-tuple-element.99), channel_id=1, source_target_pairs={{0,3},{1,0},{2,1},{3,2},{4,7},{5,4},{6,5},{7,6},{8,11},{9,8},{10,9... | collective-permute-start | bytes 393224 | tf_op jit(solution)/shard_map/ppermute | solution.py:551
  111.8 0.6 broadcast_in_dim.52.gain
  112.7 0.7 copy-done.5
  113.8 12.9 %ffn.2.refs_0_ = bf16[256,1024]{1,0:T(8,128)(2,1)} custom-call(s32[5]{0:T(128)} %stack.35.place, bf16[2048,1024]{1,0:T(8,128)(2,1)} %tok.3, bf16[1,1024]{1,0:T(2,128)(2,1)} %broadcast_in_dim.52.gain, bf16[256,256]{1,0:T(8,128)(2,1)} %get-tuple-element.69.h0, bf16[256,256]{1,0:T(8,128)(2,1)} %collective-permute-done.6.h1, bf16[256,256]{1,0:T(8,128)(2,1)} %copy-done.23, ...), custom_call_target="tpu_custom_call" | custom-call | tf_op jit(solution)/shard_map/ffn/pallas_call | solution.py:474
  126.7 3.2 %collective-permute-start.25 = (bf16[256,1024]{1,0:T(8,128)(2,1)}, bf16[256,1024]{1,0:T(8,128)(2,1)S(1)}, u32[]{:S(2)}, u32[]{:S(2)}) collective-permute-start(bf16[256,1024]{1,0:T(8,128)(2,1)} %ffn.2.refs_0_), channel_id=1, source_target_pairs={{0,3},{1,0},{2,1},{3,2},{4,7},{5,4},{6,5},{7,6},{8,11},{9,8},{10,9... | collective-permute-start | bytes 1572872 | tf_op jit(solution)/shard_map/ppermute | solution.py:551
  130.0 12.9 %ffn.3.refs_3_ = bf16[256,1024]{1,0:T(8,128)(2,1)} custom-call(s32[5]{0:T(128)} %stack.35.place, bf16[2048,1024]{1,0:T(8,128)(2,1)} %tok.3, bf16[1,1024]{1,0:T(2,128)(2,1)} %broadcast_in_dim.52.gain, bf16[256,256]{1,0:T(8,128)(2,1)} %get-tuple-element.85.h0, bf16[256,256]{1,0:T(8,128)(2,1)} %copy-done.27, bf16[256,256]{1,0:T(8,128)(2,1)} %copy-done.25, ...), custom_call_target="tpu_custom_call" | custom-call | tf_op jit(solution)/shard_map/ffn/pallas_call | solution.py:474
  142.8 3.3 %collective-permute-start.23 = (bf16[256,1024]{1,0:T(8,128)(2,1)}, bf16[256,1024]{1,0:T(8,128)(2,1)S(1)}, u32[]{:S(2)}, u32[]{:S(2)}) collective-permute-start(bf16[256,1024]{1,0:T(8,128)(2,1)} %ffn.3.refs_3_), channel_id=1, source_target_pairs={{0,3},{1,0},{2,1},{3,2},{4,7},{5,4},{6,5},{7,6},{8,11},{9,8},{10,9... | collective-permute-start | bytes 1572872 | tf_op jit(solution)/shard_map/ppermute | solution.py:551
  146.2 3.3 %collective-permute-start.29 = (bf16[128,1024]{1,0:T(8,128)(2,1)S(1)}, bf16[128,1024]{1,0:T(8,128)(2,1)S(1)}, u32[]{:S(2)}, u32[]{:S(2)}) collective-permute-start(bf16[128,1024]{1,0:T(8,128)(2,1)S(1)} %slice.62), channel_id=1, source_target_pairs={{0,3},{1,0},{2,1},{3,2},{4,7},{5,4},{6,5},{7,6},{8,11},{9,8},{10,9... | collective-permute-start | bytes 786440 | tf_op jit(solution)/shard_map/ppermute | solution.py:551
  149.6 0.7 copy-done.17
  150.3 3.1 %join.3.refs_4_ = bf16[2048,1024]{1,0:T(8,128)(2,1)} custom-call(s32[5]{0:T(128)} %stack.35.place, bf16[256,1024]{1,0:T(8,128)(2,1)} %ffn.2.refs_0_, bf16[256,1024]{1,0:T(8,128)(2,1)} %copy-done.17, bf16[256,1024]{1,0:T(8,128)(2,1)} %copy-done.16, bf16[256,1024]{1,0:T(8,128)(2,1)} %ffn.3.refs_3_), custom_call_target="tpu_custom_call" | custom-call | tf_op jit(solution)/shard_map/join/pallas_call | solution.py:531
  153.4 2.0 %all-to-all-done.2.got = bf16[32,136,512]{2,1,0:T(8,128)(2,1)} async-done(((bf16[32,136,512]{2,1,0:T(8,128)(2,1)}), bf16[32,136,512]{2,1,0:T(8,128)(2,1)}, u32[]{:S(2)}, u32[]{:S(2)}) %all-to-all-start.2) | async-done | bytes 4456480 | tf_op jit(solution)/shard_map/all_to_all | solution.py:610
  155.3 1.2 fusion
  156.7 0.6 broadcast_clamp_fusion.source
  157.3 3.2 %place.1 = bf16[16,128,512]{2,1,0:T(8,128)(2,1)} custom-call(s32[16]{0:T(128)} %broadcast_clamp_fusion.source, bf16[32,136,512]{2,1,0:T(8,128)(2,1)} %all-to-all-done.2.got), custom_call_target="tpu_custom_call" | custom-call | tf_op jit(solution)/shard_map/place/pallas_call | solution.py:508
  160.5 1.9 %collective-permute-done.22.refs_0_ = bf16[256,1024]{1,0:T(8,128)(2,1)S(1)} collective-permute-done((bf16[256,1024]{1,0:T(8,128)(2,1)}, bf16[256,1024]{1,0:T(8,128)(2,1)S(1)}, u32[]{:S(2)}, u32[]{:S(2)}) %collective-permute-start.22) | collective-permute-done | bytes 524320 | tf_op jit(solution)/shard_map/ppermute | solution.py:551
  162.6 3.2 %collective-permute-start.27 = (bf16[128,1024]{1,0:T(8,128)(2,1)S(1)}, bf16[128,1024]{1,0:T(8,128)(2,1)S(1)}, u32[]{:S(2)}, u32[]{:S(2)}) collective-permute-start(bf16[128,1024]{1,0:T(8,128)(2,1)S(1)} %slice.53), channel_id=1, source_target_pairs={{0,3},{1,0},{2,1},{3,2},{4,7},{5,4},{6,5},{7,6},{8,11},{9,8},{10,9... | collective-permute-start | bytes 786440 | tf_op jit(solution)/shard_map/ppermute | solution.py:551
  165.8 1.0 collective-permute-done.28.refs_2_
  166.8 0.7 copy-done.20
  167.5 2.9 %join.4.refs_2_ = bf16[2048,1024]{1,0:T(8,128)(2,1)} custom-call(s32[5]{0:T(128)} %stack.35.place, bf16[256,1024]{1,0:T(8,128)(2,1)} %copy-done.15, bf16[256,1024]{1,0:T(8,128)(2,1)} %copy-done.14, bf16[128,1024]{1,0:T(8,128)(2,1)} %copy-done.20, bf16[128,1024]{1,0:T(8,128)(2,1)} %copy-done.19, ...), custom_call_target="tpu_custom_call", output_to_operand_aliasing={{}: (5, {})} | custom-call | tf_op jit(solution)/shard_map/join/pallas_call | solution.py:531
  170.4 0.7 collective-permute-done.26.refs_0_
  171.1 0.7 copy-done.21
  171.8 0.7 copy-done.22
  172.5 2.4 %join.5 = bf16[2048,1024]{1,0:T(8,128)(2,1)} custom-call(s32[5]{0:T(128)} %stack.35.place, bf16[128,1024]{1,0:T(8,128)(2,1)} %copy-done.21, bf16[128,1024]{1,0:T(8,128)(2,1)} %copy-done.22, bf16[2048,1024]{1,0:T(8,128)(2,1)} %join.4.refs_2_), custom_call_target="tpu_custom_call", output_to_operand_aliasing={{}: (3, {})} | custom-call | tf_op jit(solution)/shard_map/join/pallas_call | solution.py:531
  (110 shorter events, 4.5 us)
Async XLA Ops:
  1.6 5.3 %copy-start.33 = (s32[16]{0:T(128)S(1)}, s32[16]{0:T(128)}, u32[]{:S(2)}) copy-start(s32[16]{0:T(128)} %param.33) | copy-start | bytes 196
  1.6 5.3 %copy-start.32 = (s32[16]{0:T(128)S(1)}, s32[16]{0:T(128)}, u32[]{:S(2)}) copy-start(s32[16]{0:T(128)} %owner.1) | copy-start | bytes 196
  1.7 5.4 %copy-start.30 = (bf16[1024]{0:T(1024)(128)(2,1)S(1)}, bf16[1024]{0:T(1024)(128)(2,1)}, u32[]{:S(2)}) copy-start(bf16[1024]{0:T(1024)(128)(2,1)} %param.18) | copy-start | bytes 6148
  1.7 6.0 %copy-start.29 = (s32[2048]{0:T(1024)S(1)}, s32[2048]{0:T(1024)}, u32[]{:S(2)}) copy-start(s32[2048]{0:T(1024)} %param.31) | copy-start | bytes 24580
  1.7 6.0 %copy-start.28 = (f32[2048,2]{0,1:T(2,128)S(1)}, f32[2048,2]{0,1:T(2,128)}, u32[]{:S(2)}) copy-start(f32[2048,2]{0,1:T(2,128)} %param.24) | copy-start | bytes 49156
  3.9 53.7 %collective-permute-start.4 = (bf16[480,1024]{1,0:T(8,128)(2,1)}, bf16[480,1024]{1,0:T(8,128)(2,1)S(1)}, u32[]{:S(2)}, u32[]{:S(2)}) collective-permute-start(bf16[480,1024]{1,0:T(8,128)(2,1)} %pad_maximum_fusion.1), channel_id=1, source_target_pairs={{0,3},{1,0},{2,1},{3,2},{4,7},{5,4},{6,5},{7,6},{8,11},{9,8},{10,9... | collective-permute-start | bytes 2949128 | tf_op jit(solution)/shard_map/ppermute | solution.py:551
  6.9 50.7 %collective-permute-start.3 = (bf16[480,1024]{1,0:T(8,128)(2,1)}, bf16[480,1024]{1,0:T(8,128)(2,1)S(1)}, u32[]{:S(2)}, u32[]{:S(2)}) collective-permute-start(bf16[480,1024]{1,0:T(8,128)(2,1)} %pad_maximum_fusion.1), channel_id=1, source_target_pairs={{0,1},{1,2},{2,3},{3,0},{4,5},{5,6},{6,7},{7,4},{8,9},{9,10},{10,1... | collective-permute-start | bytes 2949128 | tf_op jit(solution)/shard_map/ppermute | solution.py:551
  22.1 17.8 %all-to-all-start = ((bf16[8,264,128]{2,1,0:T(8,128)(2,1)}), bf16[8,264,128]{2,1,0:T(8,128)(2,1)S(1)}, u32[]{:S(2)}, u32[]{:S(2)}) async-start(bf16[8,264,128]{2,1,0:T(8,128)(2,1)} %get-tuple-element.56), calls=%async_computation | async-start | bytes 1081344 | tf_op jit(solution)/shard_map/all_to_all | solution.py:587
  28.7 19.0 %collective-permute-start.2 = (bf16[176,1024]{1,0:T(8,128)(2,1)S(1)}, bf16[176,1024]{1,0:T(8,128)(2,1)S(1)}, u32[]{:S(2)}, u32[]{:S(2)}) collective-permute-start(bf16[176,1024]{1,0:T(8,128)(2,1)S(1)} %select_bitcast_fusion), channel_id=1, source_target_pairs={{0,3},{1,0},{2,1},{3,2},{4,7},{5,4},{6,5},{7,6},{8,11},{9,8},{10,9... | collective-permute-start | bytes 1081352 | tf_op jit(solution)/shard_map/ppermute | solution.py:551
  32.0 17.8 %collective-permute-start.1 = (bf16[176,1024]{1,0:T(8,128)(2,1)S(1)}, bf16[176,1024]{1,0:T(8,128)(2,1)}, u32[]{:S(2)}, u32[]{:S(2)}) collective-permute-start(bf16[176,1024]{1,0:T(8,128)(2,1)S(1)} %select_bitcast_fusion), channel_id=1, source_target_pairs={{0,2},{1,3},{2,0},{3,1},{4,6},{5,7},{6,4},{7,5},{8,10},{9,11},{10,... | collective-permute-start | bytes 1081352 | tf_op jit(solution)/shard_map/ppermute | solution.py:551
  32.0 19.2 %collective-permute-start = (bf16[176,1024]{1,0:T(8,128)(2,1)S(1)}, bf16[176,1024]{1,0:T(8,128)(2,1)}, u32[]{:S(2)}, u32[]{:S(2)}) collective-permute-start(bf16[176,1024]{1,0:T(8,128)(2,1)S(1)} %select_bitcast_fusion), channel_id=1, source_target_pairs={{0,1},{1,2},{2,3},{3,0},{4,5},{5,6},{6,7},{7,4},{8,9},{9,10},{10,1... | collective-permute-start | bytes 1081352 | tf_op jit(solution)/shard_map/ppermute | solution.py:551
  39.9 0.8 copy-start.13
  42.7 14.9 %all-to-all-start.1 = ((bf16[4,264,128]{2,1,0:T(8,128)(2,1)}), bf16[4,264,128]{2,1,0:T(8,128)(2,1)S(1)}, u32[]{:S(2)}, u32[]{:S(2)}) async-start(bf16[4,264,128]{2,1,0:T(8,128)(2,1)} %get-tuple-element.61), calls=%async_computation.1 | async-start | bytes 540672 | tf_op jit(solution)/shard_map/all_to_all | solution.py:587
  47.7 9.9 %copy-start.18 = (bf16[176,1024]{1,0:T(8,128)(2,1)}, bf16[176,1024]{1,0:T(8,128)(2,1)S(1)}, u32[]{:S(2)}) copy-start(bf16[176,1024]{1,0:T(8,128)(2,1)S(1)} %collective-permute-done.2) | copy-start | bytes 1081348
  47.7 27.4 %collective-permute-start.5 = (bf16[480,1024]{1,0:T(8,128)(2,1)}, bf16[480,1024]{1,0:T(8,128)(2,1)}, u32[]{:S(2)}, u32[]{:S(2)}) collective-permute-start(bf16[480,1024]{1,0:T(8,128)(2,1)} %pad_maximum_fusion.1), channel_id=1, source_target_pairs={{0,2},{1,3},{2,0},{3,1},{4,6},{5,7},{6,4},{7,5},{8,10},{9,11},{10,... | collective-permute-start | bytes 2949128 | tf_op jit(solution)/shard_map/ppermute | solution.py:551
  57.6 8.6 %copy-start.12 = (bf16[4,264,128]{2,1,0:T(8,128)(2,1)}, bf16[4,264,128]{2,1,0:T(8,128)(2,1)S(1)}, u32[]{:S(2)}) copy-start(bf16[4,264,128]{2,1,0:T(8,128)(2,1)S(1)} %all-to-all-done.1.got) | copy-start | bytes 811012
  57.6 1.0 copy-start.7
  57.7 1.3 copy-start.8
  60.3 36.7 %copy-start = (bf16[3,176,1024]{2,1,0:T(8,128)(2,1)}, bf16[3,176,1024]{2,1,0:T(8,128)(2,1)S(1)}, u32[]{:S(2)}) copy-start(bf16[3,176,1024]{2,1,0:T(8,128)(2,1)S(1)} %pad_maximum_fusion.rest_4_) | copy-start | bytes 3244036
  60.3 28.5 %collective-permute-start.11 = (bf16[3,176,1024]{2,1,0:T(8,128)(2,1)S(1)}, bf16[3,176,1024]{2,1,0:T(8,128)(2,1)S(1)}, u32[]{:S(2)}, u32[]{:S(2)}) collective-permute-start(bf16[3,176,1024]{2,1,0:T(8,128)(2,1)S(1)} %pad_maximum_fusion.rest_4_), channel_id=1, source_target_pairs={{0,64},{4,20},{8,72},{12,28},{16,80},{20,4},{24,88},{28,12},{32,96... | collective-permute-start | bytes 3244040 | tf_op jit(solution)/shard_map/ppermute | solution.py:564
  63.5 25.3 %collective-permute-start.10 = (bf16[3,176,1024]{2,1,0:T(8,128)(2,1)S(1)}, bf16[3,176,1024]{2,1,0:T(8,128)(2,1)S(1)}, u32[]{:S(2)}, u32[]{:S(2)}) collective-permute-start(bf16[3,176,1024]{2,1,0:T(8,128)(2,1)S(1)} %pad_maximum_fusion.rest_4_), channel_id=1, source_target_pairs={{0,96},{4,28},{8,104},{12,4},{16,112},{20,12},{24,120},{28,20},{32... | collective-permute-start | bytes 3244040 | tf_op jit(solution)/shard_map/ppermute | solution.py:564
  64.6 24.3 %collective-permute-start.9 = (bf16[3,176,1024]{2,1,0:T(8,128)(2,1)S(1)}, bf16[3,176,1024]{2,1,0:T(8,128)(2,1)}, u32[]{:S(2)}, u32[]{:S(2)}) collective-permute-start(bf16[3,176,1024]{2,1,0:T(8,128)(2,1)S(1)} %pad_maximum_fusion.rest_4_), channel_id=1, source_target_pairs={{0,32},{4,12},{8,40},{12,20},{16,48},{20,28},{24,56},{28,4},{32,64... | collective-permute-start | bytes 3244040 | tf_op jit(solution)/shard_map/ppermute | solution.py:564
  74.6 7.1 %collective-permute-start.8 = (bf16[256,256]{1,0:T(8,128)(2,1)S(1)}, bf16[256,256]{1,0:T(8,128)(2,1)S(1)}, u32[]{:S(2)}, u32[]{:S(2)}) collective-permute-start(bf16[256,256]{1,0:T(8,128)(2,1)S(1)} %get-tuple-element.102), channel_id=1, source_target_pairs={{0,2},{1,3},{2,0},{3,1},{4,6},{5,7},{6,4},{7,5},{8,10},{9,11},{10,... | collective-permute-start | bytes 393224 | tf_op jit(solution)/shard_map/ppermute | solution.py:551
  75.2 13.6 %collective-permute-start.7 = (bf16[256,256]{1,0:T(8,128)(2,1)}, bf16[256,256]{1,0:T(8,128)(2,1)S(1)}, u32[]{:S(2)}, u32[]{:S(2)}) collective-permute-start(bf16[256,256]{1,0:T(8,128)(2,1)} %get-tuple-element.103), channel_id=1, source_target_pairs={{0,3},{1,0},{2,1},{3,2},{4,7},{5,4},{6,5},{7,6},{8,11},{9,8},{10,9... | collective-permute-start | bytes 393224 | tf_op jit(solution)/shard_map/ppermute | solution.py:551
  81.7 7.1 %copy-start.23 = (bf16[256,256]{1,0:T(8,128)(2,1)}, bf16[256,256]{1,0:T(8,128)(2,1)S(1)}, u32[]{:S(2)}) copy-start(bf16[256,256]{1,0:T(8,128)(2,1)S(1)} %collective-permute-done.8.h2) | copy-start | bytes 393220
  81.7 7.1 %collective-permute-start.6 = (bf16[256,256]{1,0:T(8,128)(2,1)}, bf16[256,256]{1,0:T(8,128)(2,1)}, u32[]{:S(2)}, u32[]{:S(2)}) collective-permute-start(bf16[256,256]{1,0:T(8,128)(2,1)} %get-tuple-element.104), channel_id=1, source_target_pairs={{0,1},{1,2},{2,3},{3,0},{4,5},{5,6},{6,7},{7,4},{8,9},{9,10},{10,1... | collective-permute-start | bytes 393224 | tf_op jit(solution)/shard_map/ppermute | solution.py:551
  88.8 13.3 %copy-start.1 = (bf16[3,176,1024]{2,1,0:T(8,128)(2,1)}, bf16[3,176,1024]{2,1,0:T(8,128)(2,1)S(1)}, u32[]{:S(2)}) copy-start(bf16[3,176,1024]{2,1,0:T(8,128)(2,1)S(1)} %collective-permute-done.11.rest_7_) | copy-start | bytes 3244036
  88.8 10.4 %copy-start.2 = (bf16[3,176,1024]{2,1,0:T(8,128)(2,1)}, bf16[3,176,1024]{2,1,0:T(8,128)(2,1)S(1)}, u32[]{:S(2)}) copy-start(bf16[3,176,1024]{2,1,0:T(8,128)(2,1)S(1)} %collective-permute-done.10.rest_6_) | copy-start | bytes 3244036
  88.9 22.9 %copy-start.31 = (bf16[1024]{0:T(1024)(128)(2,1)S(1)}, bf16[1024]{0:T(1024)(128)(2,1)}, u32[]{:S(2)}) copy-start(bf16[1024]{0:T(1024)(128)(2,1)} %param.27) | copy-start | bytes 6148
  89.4 65.9 %all-to-all-start.2 = ((bf16[32,136,512]{2,1,0:T(8,128)(2,1)}), bf16[32,136,512]{2,1,0:T(8,128)(2,1)}, u32[]{:S(2)}, u32[]{:S(2)}) async-start(bf16[32,136,512]{2,1,0:T(8,128)(2,1)} %get-tuple-element.90), calls=%async_computation.2 | async-start | bytes 8912896 | tf_op jit(solution)/shard_map/all_to_all | solution.py:610
  96.4 2.9 %collective-permute-start.16 = (bf16[480,1024]{1,0:T(8,128)(2,1)}, bf16[480,1024]{1,0:T(8,128)(2,1)S(1)}, u32[]{:S(2)}, u32[]{:S(2)}) collective-permute-start(bf16[480,1024]{1,0:T(8,128)(2,1)} %copy-done.8), channel_id=1, source_target_pairs={{0,4},{4,0},{8,12},{12,8},{16,20},{20,16},{24,28},{28,24},{32,36},... | collective-permute-start | bytes 2949128 | tf_op jit(solution)/shard_map/ppermute | solution.py:552
  96.7 5.4 %collective-permute-start.17 = (bf16[480,1024]{1,0:T(8,128)(2,1)}, bf16[480,1024]{1,0:T(8,128)(2,1)S(1)}, u32[]{:S(2)}, u32[]{:S(2)}) collective-permute-start(bf16[480,1024]{1,0:T(8,128)(2,1)} %copy-done.7), channel_id=1, source_target_pairs={{0,4},{4,0},{8,12},{12,8},{16,20},{20,16},{24,28},{28,24},{32,36},... | collective-permute-start | bytes 2949128 | tf_op jit(solution)/shard_map/ppermute | solution.py:552
  97.0 12.7 %collective-permute-start.12 = (bf16[3,176,1024]{2,1,0:T(8,128)(2,1)S(1)}, bf16[3,176,1024]{2,1,0:T(8,128)(2,1)S(1)}, u32[]{:S(2)}, u32[]{:S(2)}) collective-permute-start(bf16[3,176,1024]{2,1,0:T(8,128)(2,1)S(1)} %pad_maximum_fusion.rest_4_), channel_id=1, source_target_pairs={{0,4},{4,0},{8,12},{12,8},{16,20},{20,16},{24,28},{28,24},{32,36},... | collective-permute-start | bytes 3244040 | tf_op jit(solution)/shard_map/ppermute | solution.py:552
  97.2 14.6 %collective-permute-start.13 = (bf16[3,176,1024]{2,1,0:T(8,128)(2,1)}, bf16[3,176,1024]{2,1,0:T(8,128)(2,1)S(1)}, u32[]{:S(2)}, u32[]{:S(2)}) collective-permute-start(bf16[3,176,1024]{2,1,0:T(8,128)(2,1)} %collective-permute-done.9.rest_5_), channel_id=1, source_target_pairs={{0,4},{4,0},{8,12},{12,8},{16,20},{20,16},{24,28},{28,24},{32,36},... | collective-permute-start | bytes 3244040 | tf_op jit(solution)/shard_map/ppermute | solution.py:552
  97.5 10.5 %collective-permute-start.18 = (bf16[480,1024]{1,0:T(8,128)(2,1)}, bf16[480,1024]{1,0:T(8,128)(2,1)S(1)}, u32[]{:S(2)}, u32[]{:S(2)}) collective-permute-start(bf16[480,1024]{1,0:T(8,128)(2,1)} %collective-permute-done.5.rest_14_), channel_id=1, source_target_pairs={{0,4},{4,0},{8,12},{12,8},{16,20},{20,16},{24,28},{28,24},{32,36},... | collective-permute-start | bytes 2949128 | tf_op jit(solution)/shard_map/ppermute | solution.py:552
  99.3 1.0 copy-start.9
  99.3 13.1 %collective-permute-start.14 = (bf16[3,176,1024]{2,1,0:T(8,128)(2,1)S(1)}, bf16[3,176,1024]{2,1,0:T(8,128)(2,1)S(1)}, u32[]{:S(2)}, u32[]{:S(2)}) collective-permute-start(bf16[3,176,1024]{2,1,0:T(8,128)(2,1)S(1)} %collective-permute-done.10.rest_6_), channel_id=1, source_target_pairs={{0,4},{4,0},{8,12},{12,8},{16,20},{20,16},{24,28},{28,24},{32,36},... | collective-permute-start | bytes 3244040 | tf_op jit(solution)/shard_map/ppermute | solution.py:552
  102.1 1.0 copy-start.10
  103.0 9.4 %collective-permute-start.15 = (bf16[3,176,1024]{2,1,0:T(8,128)(2,1)S(1)}, bf16[3,176,1024]{2,1,0:T(8,128)(2,1)S(1)}, u32[]{:S(2)}, u32[]{:S(2)}) collective-permute-start(bf16[3,176,1024]{2,1,0:T(8,128)(2,1)S(1)} %collective-permute-done.11.rest_7_), channel_id=1, source_target_pairs={{0,4},{4,0},{8,12},{12,8},{16,20},{20,16},{24,28},{28,24},{32,36},... | collective-permute-start | bytes 3244040 | tf_op jit(solution)/shard_map/ppermute | solution.py:552
  108.0 4.4 %copy-start.11 = (bf16[480,1024]{1,0:T(8,128)(2,1)}, bf16[480,1024]{1,0:T(8,128)(2,1)S(1)}, u32[]{:S(2)}) copy-start(bf16[480,1024]{1,0:T(8,128)(2,1)S(1)} %collective-permute-done.18.rest_17_) | copy-start | bytes 2949124
  108.0 18.6 %collective-permute-start.21 = (bf16[256,256]{1,0:T(8,128)(2,1)}, bf16[256,256]{1,0:T(8,128)(2,1)S(1)}, u32[]{:S(2)}, u32[]{:S(2)}) collective-permute-start(bf16[256,256]{1,0:T(8,128)(2,1)} %get-tuple-element.98), channel_id=1, source_target_pairs={{0,2},{1,3},{2,0},{3,1},{4,6},{5,7},{6,4},{7,5},{8,10},{9,11},{10,... | collective-permute-start | bytes 393224 | tf_op jit(solution)/shard_map/ppermute | solution.py:551
  109.7 2.7 %copy-start.3 = (bf16[3,176,1024]{2,1,0:T(8,128)(2,1)}, bf16[3,176,1024]{2,1,0:T(8,128)(2,1)S(1)}, u32[]{:S(2)}) copy-start(bf16[3,176,1024]{2,1,0:T(8,128)(2,1)S(1)} %collective-permute-done.12.rest_8_) | copy-start | bytes 3244036
  109.7 17.0 %collective-permute-start.20 = (bf16[256,256]{1,0:T(8,128)(2,1)}, bf16[256,256]{1,0:T(8,128)(2,1)S(1)}, u32[]{:S(2)}, u32[]{:S(2)}) collective-permute-start(bf16[256,256]{1,0:T(8,128)(2,1)} %get-tuple-element.99), channel_id=1, source_target_pairs={{0,3},{1,0},{2,1},{3,2},{4,7},{5,4},{6,5},{7,6},{8,11},{9,8},{10,9... | collective-permute-start | bytes 393224 | tf_op jit(solution)/shard_map/ppermute | solution.py:551
  111.7 1.0 copy-start.4
  111.7 14.9 %collective-permute-start.19 = (bf16[256,256]{1,0:T(8,128)(2,1)S(1)}, bf16[256,256]{1,0:T(8,128)(2,1)S(1)}, u32[]{:S(2)}, u32[]{:S(2)}) collective-permute-start(bf16[256,256]{1,0:T(8,128)(2,1)S(1)} %get-tuple-element.100), channel_id=1, source_target_pairs={{0,1},{1,2},{2,3},{3,0},{4,5},{5,6},{6,7},{7,4},{8,9},{9,10},{10,1... | collective-permute-start | bytes 393224 | tf_op jit(solution)/shard_map/ppermute | solution.py:551
  112.4 1.0 copy-start.5
  112.4 1.3 copy-start.6
  126.6 3.3 %copy-start.25 = (bf16[256,256]{1,0:T(8,128)(2,1)}, bf16[256,256]{1,0:T(8,128)(2,1)S(1)}, u32[]{:S(2)}) copy-start(bf16[256,256]{1,0:T(8,128)(2,1)S(1)} %collective-permute-done.21.h2) | copy-start | bytes 393220
  126.7 3.3 %copy-start.26 = (bf16[256,256]{1,0:T(8,128)(2,1)}, bf16[256,256]{1,0:T(8,128)(2,1)S(1)}, u32[]{:S(2)}) copy-start(bf16[256,256]{1,0:T(8,128)(2,1)S(1)} %collective-permute-done.20.h3) | copy-start | bytes 393220
  126.7 3.3 %copy-start.27 = (bf16[256,256]{1,0:T(8,128)(2,1)}, bf16[256,256]{1,0:T(8,128)(2,1)S(1)}, u32[]{:S(2)}) copy-start(bf16[256,256]{1,0:T(8,128)(2,1)S(1)} %collective-permute-done.19.h1) | copy-start | bytes 393220
  126.7 19.5 %collective-permute-start.25 = (bf16[256,1024]{1,0:T(8,128)(2,1)}, bf16[256,1024]{1,0:T(8,128)(2,1)S(1)}, u32[]{:S(2)}, u32[]{:S(2)}) collective-permute-start(bf16[256,1024]{1,0:T(8,128)(2,1)} %ffn.2.refs_0_), channel_id=1, source_target_pairs={{0,3},{1,0},{2,1},{3,2},{4,7},{5,4},{6,5},{7,6},{8,11},{9,8},{10,9... | collective-permute-start | bytes 1572872 | tf_op jit(solution)/shard_map/ppermute | solution.py:551
  129.9 19.5 %collective-permute-start.24 = (bf16[256,1024]{1,0:T(8,128)(2,1)}, bf16[256,1024]{1,0:T(8,128)(2,1)S(1)}, u32[]{:S(2)}, u32[]{:S(2)}) collective-permute-start(bf16[256,1024]{1,0:T(8,128)(2,1)} %ffn.2.refs_0_), channel_id=1, source_target_pairs={{0,1},{1,2},{2,3},{3,0},{4,5},{5,6},{6,7},{7,4},{8,9},{9,10},{10,1... | collective-permute-start | bytes 1572872 | tf_op jit(solution)/shard_map/ppermute | solution.py:551
  142.8 17.7 %collective-permute-start.23 = (bf16[256,1024]{1,0:T(8,128)(2,1)}, bf16[256,1024]{1,0:T(8,128)(2,1)S(1)}, u32[]{:S(2)}, u32[]{:S(2)}) collective-permute-start(bf16[256,1024]{1,0:T(8,128)(2,1)} %ffn.3.refs_3_), channel_id=1, source_target_pairs={{0,3},{1,0},{2,1},{3,2},{4,7},{5,4},{6,5},{7,6},{8,11},{9,8},{10,9... | collective-permute-start | bytes 1572872 | tf_op jit(solution)/shard_map/ppermute | solution.py:551
  146.1 16.3 %collective-permute-start.22 = (bf16[256,1024]{1,0:T(8,128)(2,1)}, bf16[256,1024]{1,0:T(8,128)(2,1)S(1)}, u32[]{:S(2)}, u32[]{:S(2)}) collective-permute-start(bf16[256,1024]{1,0:T(8,128)(2,1)} %ffn.3.refs_3_), channel_id=1, source_target_pairs={{0,1},{1,2},{2,3},{3,0},{4,5},{5,6},{6,7},{7,4},{8,9},{9,10},{10,1... | collective-permute-start | bytes 1572872 | tf_op jit(solution)/shard_map/ppermute | solution.py:551
  146.1 3.4 %copy-start.16 = (bf16[256,1024]{1,0:T(8,128)(2,1)}, bf16[256,1024]{1,0:T(8,128)(2,1)S(1)}, u32[]{:S(2)}) copy-start(bf16[256,1024]{1,0:T(8,128)(2,1)S(1)} %collective-permute-done.25.refs_2_) | copy-start | bytes 1572868
  146.2 19.6 %collective-permute-start.29 = (bf16[128,1024]{1,0:T(8,128)(2,1)S(1)}, bf16[128,1024]{1,0:T(8,128)(2,1)S(1)}, u32[]{:S(2)}, u32[]{:S(2)}) collective-permute-start(bf16[128,1024]{1,0:T(8,128)(2,1)S(1)} %slice.62), channel_id=1, source_target_pairs={{0,3},{1,0},{2,1},{3,2},{4,7},{5,4},{6,5},{7,6},{8,11},{9,8},{10,9... | collective-permute-start | bytes 786440 | tf_op jit(solution)/shard_map/ppermute | solution.py:551
  149.5 0.8 copy-start.17
  149.5 17.2 %collective-permute-start.28 = (bf16[128,1024]{1,0:T(8,128)(2,1)S(1)}, bf16[128,1024]{1,0:T(8,128)(2,1)S(1)}, u32[]{:S(2)}, u32[]{:S(2)}) collective-permute-start(bf16[128,1024]{1,0:T(8,128)(2,1)S(1)} %slice.61), channel_id=1, source_target_pairs={{0,1},{1,2},{2,3},{3,0},{4,5},{5,6},{6,7},{7,4},{8,9},{9,10},{10,1... | collective-permute-start | bytes 786440 | tf_op jit(solution)/shard_map/ppermute | solution.py:551
  160.5 6.2 %copy-start.14 = (bf16[256,1024]{1,0:T(8,128)(2,1)}, bf16[256,1024]{1,0:T(8,128)(2,1)S(1)}, u32[]{:S(2)}) copy-start(bf16[256,1024]{1,0:T(8,128)(2,1)S(1)} %collective-permute-done.23.refs_1_) | copy-start | bytes 1572868
  162.4 4.3 %copy-start.15 = (bf16[256,1024]{1,0:T(8,128)(2,1)}, bf16[256,1024]{1,0:T(8,128)(2,1)S(1)}, u32[]{:S(2)}) copy-start(bf16[256,1024]{1,0:T(8,128)(2,1)S(1)} %collective-permute-done.22.refs_0_) | copy-start | bytes 1572868
  162.5 8.6 %collective-permute-start.26 = (bf16[128,1024]{1,0:T(8,128)(2,1)S(1)}, bf16[128,1024]{1,0:T(8,128)(2,1)S(1)}, u32[]{:S(2)}, u32[]{:S(2)}) collective-permute-start(bf16[128,1024]{1,0:T(8,128)(2,1)S(1)} %slice.52), channel_id=1, source_target_pairs={{0,1},{1,2},{2,3},{3,0},{4,5},{5,6},{6,7},{7,4},{8,9},{9,10},{10,1... | collective-permute-start | bytes 786440 | tf_op jit(solution)/shard_map/ppermute | solution.py:551
  162.6 8.5 %collective-permute-start.27 = (bf16[128,1024]{1,0:T(8,128)(2,1)S(1)}, bf16[128,1024]{1,0:T(8,128)(2,1)S(1)}, u32[]{:S(2)}, u32[]{:S(2)}) collective-permute-start(bf16[128,1024]{1,0:T(8,128)(2,1)S(1)} %slice.53), channel_id=1, source_target_pairs={{0,3},{1,0},{2,1},{3,2},{4,7},{5,4},{6,5},{7,6},{8,11},{9,8},{10,9... | collective-permute-start | bytes 786440 | tf_op jit(solution)/shard_map/ppermute | solution.py:551
  165.8 1.0 copy-start.19
  166.8 0.7 copy-start.20
  (3 other events, 2.1 us)
where the time goes:
time: 177 us; the launch traced here: 175 us
  Pallas kernels  78.1 us (44%)
  starting transfers between devices  54 us (31%)
  local copies, waits for them, and re-layouts  17.5 us (10%)
  waiting for transfers between devices  17.4 us (10%)
  other arithmetic  6.85 us (4%)
    ppermute x20, starting transfers between devices, on_device(): lax.ppermute(a, 'tp', [(i, (i + d) % 4) for i in range(4)])  30.5 us
    pallas_call x2, Pallas kernels, ffn(): pl.pallas_call(ffn_kernel, grid_spec=gs, out_shape=jax.ShapeDtypeStruct((...  25.7 us
    pallas_call x2, Pallas kernels, recall(): pl.pallas_call(functools.partial(recall_kernel, half), grid_spec=gs, out_...  13.1 us
    pallas_call x1, Pallas kernels, project(): pl.pallas_call(project_kernel, grid_spec=gs, out_shape=[jax.ShapeDtypeStr...  12.9 us
    pallas_call x2, Pallas kernels, attend(): pl.pallas_call(attend_kernel, grid=(heads,), in_specs=[pl.BlockSpec((SEG,...  12.6 us
    all_to_all x2, starting transfers between devices, on_device(): lax.all_to_all(a, 'req', 0, 0, tiled=True, axis_index_groups=g)  9.77 us
    ppermute x20, waiting for transfers between devices, on_device(): lax.ppermute(a, 'tp', [(i, (i + d) % 4) for i in range(4)])  8.99 us
    unnamed x68, local copies, waits for them, and re-layouts  8.68 us
  transfers between devices with their start and end apart: 33, of which 10 were waited for; matrix products, arithmetic and copies ran while one was open for 7% of the time, Pallas kernels for 43%

commit v1 on v0

--- a/solution.py
+++ b/solution.py
@@ -60,7 +60,7 @@
         out[r, :] = (rms(tok[r, :].astype(F32), 1e-5) * g).astype(BF)
 
 
-def project_kernel(owner, tok0, tok1, tok2, gain, wq, wk, wv, row, codes, q_out, kv_out, ku_out, min_out, pay_out, cr_out, cc_out, sent, st, misc, buf, n0, n1, sem):
+def project_kernel(owner, slot, tok0, tok1, tok2, gain, wq, wk, wv, row, q_out, kv_out, ku_out, min_out, pay_out, cr_out, cc_out, sent, st, misc, buf, n0, n1, codes, sem):
     i = pl.program_id(0)
     here = CH // PAGE
     last_sem = 2 * here
@@ -70,6 +70,9 @@
         st[...] = jnp.zeros_like(st)
         misc[...] = jnp.full_like(misc, -1.0)
         misc[0:2, :] = jnp.zeros((2, 128), F32)
+        codes[...] = jnp.zeros_like(codes)
+        for p in range(owner.shape[0]):
+            codes[owner[p]] = jnp.broadcast_to((slot[p] + 1).astype(F32), codes.shape[1:]).astype(BF)
         pltpu.make_async_copy(codes, sent.at[:, pl.ds(PAGE, 8), :], sem.at[last_sem]).start()
         normed(tok0, gain, n0)
 
@@ -142,29 +145,29 @@
     return l0, l1, s[6:7] * 256.0 + s[7:8]
 
 
-def project(owner, tokens, gain, wq, wk, wv, row, codes):
+def project(owner, slot, tokens, gain, wq, wk, wv, row, reqs):
     t, d = tokens.shape
     tile = 512
     n = t // tile
     c = tile // CH
-    full = lambda a: pl.BlockSpec(a.shape, lambda i, o: (0,) * a.ndim)
-    rows = lambda w: pl.BlockSpec((tile, w), lambda i, o: (i, 0))
-    lanes = pl.BlockSpec((8, tile), lambda i, o: (0, i))
+    full = lambda a: pl.BlockSpec(a.shape, lambda i, o, l: (0,) * a.ndim)
+    rows = lambda w: pl.BlockSpec((tile, w), lambda i, o, l: (i, 0))
+    lanes = pl.BlockSpec((8, tile), lambda i, o, l: (0, i))
     gs = pltpu.PrefetchScalarGridSpec(
-        num_scalar_prefetch=1,
+        num_scalar_prefetch=2,
         grid=(n,),
         in_specs=[
-            pl.BlockSpec((CH, d), lambda i, o: (0, 0)),
-            pl.BlockSpec((CH, d), lambda i, o: (2 * i + 1, 0)),
-            pl.BlockSpec((CH, d), lambda i, o: (jnp.minimum(2 * i + 2, 2 * n - 1), 0)),
-            full(gain), full(wq), full(wk), full(wv), lanes, full(codes),
+            pl.BlockSpec((CH, d), lambda i, o, l: (0, 0)),
+            pl.BlockSpec((CH, d), lambda i, o, l: (2 * i + 1, 0)),
+            pl.BlockSpec((CH, d), lambda i, o, l: (jnp.minimum(2 * i + 2, 2 * n - 1), 0)),
+            full(gain), full(wq), full(wk), full(wv), lanes,
         ],
         out_specs=[
             rows(256),
             rows(512),
             rows(256),
-            pl.BlockSpec((c, 2, HD, HD), lambda i, o: (i, 0, 0, 0)),
-            pl.BlockSpec((8, 264, 128), lambda i, o: (0, 0, 0)),
+            pl.BlockSpec((c, 2, HD, HD), lambda i, o, l: (i, 0, 0, 0)),
+            pl.BlockSpec((8, 264, 128), lambda i, o, l: (0, 0, 0)),
             lanes,
             rows(8),
             pl.BlockSpec(memory_space=ANY),
@@ -175,6 +178,7 @@
             pltpu.VMEM((tile // PAGE, PAGE, 512), BF),
             pltpu.VMEM((CH, d), BF),
             pltpu.VMEM((CH, d), BF),
+            pltpu.VMEM((reqs, 8, 512), BF),
             pltpu.SemaphoreType.DMA((tile // PAGE + 1,)),
         ],
     )
@@ -189,10 +193,10 @@
             jax.ShapeDtypeStruct((8, 264, 128), BF),
             jax.ShapeDtypeStruct((8, t), F32),
             jax.ShapeDtypeStruct((t, 8), F32),
-            jax.ShapeDtypeStruct((codes.shape[0], PAGE + 8, 512), BF),
+            jax.ShapeDtypeStruct((reqs, PAGE + 8, 512), BF),
         ],
         name="project",
-    )(owner, tokens, tokens, tokens, gain, wq, wk, wv, row, codes)
+    )(owner, slot, tokens, tokens, tokens, gain, wq, wk, wv, row)
 
 
 def combine_kernel(place, got, e_out, info_out, pay_out, st):
@@ -358,7 +362,7 @@
             pl.BlockSpec((CH, 256), lambda b, p, d: (jnp.maximum(2 * b + half - per, 0), 0)),
             full(gain),
         ],
-        out_specs=pl.BlockSpec((1, CH, 256), lambda b, p, d: (lax.rem(b - p[2] + 4, 4), 0, 0)),
+        out_specs=pl.BlockSpec((1, CH, 256), lambda b, p, d: (b if half == 0 else lax.rem(b - p[2] + 4, 4), 0, 0)),
         scratch_shapes=[pltpu.VMEM((2, HD, HD), F32), pltpu.VMEM((8, 128), F32)],
     )
     return pl.pallas_call(
@@ -370,11 +374,17 @@
     )(place, bound, q, ku, kv, mi, e1, info, got, col, row, row, at0, at1, gain)
 
 
-def ffn_kernel(place, tok, gain, h0, h1, h2, h3, *rest):
+def ffn_kernel(half, place, gain, tokens, *rest):
+    y = place[2]
+    if half == 0:
+        heads = [rest[0].at[lax.rem(y - d + 4, 4)] for d in (0, 1, 3, 2)]
+    else:
+        heads = rest[0:4]
+    rest = rest[1:] if half == 0 else rest[4:]
     own = rest[0:4]
     gu = (rest[4:8], rest[8:12])
     do = (rest[12:15], rest[15:18])
-    out, wgu, wd, wo, norm, acc, sem = rest[18:]
+    out, tok, hv, wgu, wd, wo, norm, acc, sem = rest[18:]
     core = place[3]
     count = [0]
     waits = {}
@@ -416,15 +426,19 @@
         for c in waits[(kind, group)]:
             c.wait()
 
+    copy(("in", 0), tokens.at[pl.ds((2 * y + half) * ROWS, ROWS), :], tok)
+    for i in range(4):
+        copy(("in", 0), heads[i], hv.at[i])
     for group in range(3):
         fetch("out", group)
     fetch("up", 0)
     fetch("down", 0)
+    ready("in", 0)
     total = tok[...].astype(F32)
-    for i, (h, group) in enumerate(((h0, 0), (h1, 1), (h3, None), (h2, 2))):
+    for i, group in enumerate((0, 1, None, 2)):
         if group is not None:
             ready("out", group)
-        total = total + dot(h[...], wo[i])
+        total = total + dot(hv[i], wo[i])
     for group in (1, 2):
         fetch("up", group)
         fetch("down", group)
@@ -458,25 +472,25 @@
     gs = pltpu.PrefetchScalarGridSpec(
         num_scalar_prefetch=1,
         grid=(1,),
-        in_specs=[pl.BlockSpec((ROWS, d), lambda i, p: (2 * p[2] + half, 0)), full(gain)]
-        + [full(h) for h in heads]
-        + [anys] * len(ws),
+        in_specs=[full(gain)] + [anys] * (1 + len(heads) + len(ws)),
         out_specs=pl.BlockSpec((ROWS, d), lambda i, p: (0, 0)),
         scratch_shapes=[
+            pltpu.VMEM((ROWS, d), BF),
+            pltpu.VMEM((4, ROWS, 256), BF),
             pltpu.VMEM((2, 4, 704, 1024), BF),
             pltpu.VMEM((4, 704, 1024), BF),
             pltpu.VMEM((4, 256, 1024), BF),
             pltpu.VMEM((ROWS, d), BF),
             pltpu.VMEM((ROWS, d), F32),
-            pltpu.SemaphoreType.DMA((32,)),
+            pltpu.SemaphoreType.DMA((37,)),
         ],
     )
     return pl.pallas_call(
-        ffn_kernel,
+        functools.partial(ffn_kernel, half),
         grid_spec=gs,
         out_shape=jax.ShapeDtypeStruct((ROWS, d), BF),
         name="ffn",
-    )(place, tokens, gain, *heads, *ws)
+    )(place, gain, tokens, *heads, *ws)
 
 
 def staged(ins, bufs, outs, sem):
@@ -539,6 +553,46 @@
     )(place, *pieces, *rest)
 
 
+def cut_kernel(place, gate, up, down, last, piece, both, sem):
+    core = place[3]
+    at = jnp.where(core == 0, place[1], place[4])
+    rows = pl.ds(at * 176, 176)
+    from_gate = pltpu.make_async_copy(gate.at[rows, :], piece, sem.at[0])
+    from_up = pltpu.make_async_copy(up.at[rows, :], piece, sem.at[0])
+    rest = [
+        pltpu.make_async_copy(down.at[pl.ds(core * 352, 352), :], both.at[pl.ds(0, 352), :], sem.at[1]),
+        pltpu.make_async_copy(last.at[pl.ds(core * 128, 128), :], both.at[pl.ds(352, 128), :], sem.at[2]),
+    ]
+
+    @pl.when(core == 0)
+    def _():
+        from_gate.start()
+
+    @pl.when(core != 0)
+    def _():
+        from_up.start()
+
+    for c in rest:
+        c.start()
+    from_gate.wait()
+    for c in rest:
+        c.wait()
+
+
+def cut_weights(place, gate, up, down, last):
+    anys = pl.BlockSpec(memory_space=ANY)
+    vm = pl.BlockSpec(memory_space=pltpu.VMEM)
+    width = gate.shape[1]
+    return pl.pallas_call(
+        cut_kernel,
+        in_specs=[pl.BlockSpec(memory_space=pltpu.SMEM)] + [anys] * 4,
+        out_specs=[vm, vm],
+        out_shape=[jax.ShapeDtypeStruct((176, width), BF), jax.ShapeDtypeStruct((480, width), BF)],
+        scratch_shapes=[pltpu.SemaphoreType.DMA((3,))],
+        name="cut_weights",
+    )(place, gate, up, down, last)
+
+
 def on_device(
     tokens, attn_gain, w_query, w_key, w_value, persist_key, persist_value, log_forget, mem_gain,
     w_out, ffn_gain, w_gate, w_up, w_down, doc_ids, page_owner, page_slot,
@@ -564,22 +618,16 @@
         return lax.ppermute(a, "req", [(i, to(i)) for i in range(reqs)])
 
     gate, up = w_gate.T, w_up.T
-    at = jnp.where(core == 0, x, z)
-    cut = lambda w, i, n: lax.dynamic_slice_in_dim(w, i * n, n, 0)
-    piece = jnp.where(core == 0, cut(gate, at, 176), cut(up, at, 176))
+    piece, half_do = cut_weights(place, gate, up, w_down, w_out)
     s1, s3, s2 = [shift(piece, d) for d in (1, 3, 2)]
-    half_do = jnp.concatenate([cut(w_down, core, 352), cut(w_out, core, 128)])
     do1, do3, do2 = [shift(half_do, d) for d in (1, 3, 2)]
 
     doc = doc_ids.astype(F32)
     row = jnp.concatenate([doc[None], log_forget.T, jnp.zeros((5, count), F32)])
     bound = jnp.concatenate([jnp.full((1,), -1.0, F32), doc[CH - 1 : -1 : CH]])
 
-    hit = page_owner[None, :] == jnp.arange(reqs)[:, None]
-    code = jnp.sum(jnp.where(hit, page_slot[None, :] + 1, 0), axis=1).astype(BF)
-    codes = jnp.broadcast_to(code[:, None, None], (reqs, 8, 512))
     q, kv, ku, mi, pay, row, col, outgoing = project(
-        page_owner, tokens, attn_gain[None], w_query, w_key, w_value, row, codes
+        page_owner, page_slot, tokens, attn_gain[None], w_query, w_key, w_value, row, reqs
     )
 
     group8 = [[i * 8 + k for k in range(8)] for i in range(reqs // 8)]
@@ -587,11 +635,12 @@
     spread = lambda a, g: lax.all_to_all(a, "req", 0, 0, tiled=True, axis_index_groups=g)
     got8 = spread(pay, group8)
 
+    q, s1, s2, s3 = tie(q, s1, s2, s3)
     at0 = attend(q, kv, persist_key, persist_value, col, row, 0)
     at0, got8 = tie(at0, got8)
     e1, info, pay4 = combine(place, got8)
     got4 = spread(pay4, group4)
-    q1, at0, s1, s2, s3, _ = tie(q, at0, s1, s2, s3, pay4)
+    q1, at0, _ = tie(q, at0, pay4)
     at1 = attend(q1, kv, persist_key, persist_value, col, row, 1)
     at1, got4, s1, s2, s3, do1, do3 = tie(at1, got4, s1, s2, s3, do1, do3)
     near = jnp.stack([s1, s3, s2])
@@ -600,23 +649,28 @@
     gain = mem_gain[None]
     own_w = (gate, up, w_down, w_out)
     mem = lambda half: recall(half, place, bound, q, ku, kv, mi, e1, info, got4, col, row, at0, at1, gain)
-    send = lambda out: [out[0]] + [shift(out[d], d) for d in (1, 3, 2)]
+    do1x = swap(do1)
     out0 = mem(0)
-    heads0 = send(out0)
+    out0, do1x, do2 = tie(out0, do1x, do2)
+    heads0 = [lax.all_to_all(out0, "tp", 0, 0, tiled=True)]
+    do3x = swap(do3)
     out1 = mem(1)
-    out1, do2, *heads0 = tie(out1, do2, *heads0)
-    heads1 = send(out1)
-    outgoing, near, out1, *far = tie(outgoing, near, out1, *far)
+    out1, do3x, heads0[0] = tie(out1, do3x, heads0[0])
+    heads1 = [out1[0]] + [shift(out1[d], d) for d in (1, 3, 2)]
+    near, outgoing, _, *far = tie(near, outgoing, out1, *far)
+    nearx, do2x, *farx = [swap(a) for a in (near, do2, *far)]
+    outgoing, farx[0] = tie(outgoing, farx[0])
     arrived = lax.all_to_all(outgoing, "req", 0, 0, tiled=True)
     gu, do = [near, *far], [do1, do3, do2]
-    gux, dox = [swap(a) for a in gu], [swap(a) for a in do]
+    gux, dox = [nearx, *farx], [do1x, do3x, do2x]
+
     slots = arrived[:, PAGE, 0].astype(F32)
     wanted = slots[None, :] == (jnp.arange(count // PAGE) + 1).astype(F32)[:, None]
     source = jnp.sum(jnp.where(wanted, jnp.arange(reqs)[None, :], 0), axis=1).astype(jnp.int32)
     kv_cache = place_pages(jnp.clip(source, 0, reqs - 1), arrived, count // PAGE)
 
     feed = lambda half, heads: ffn(
-        half, place, tokens, ffn_gain[None], (heads[0], heads[1], heads[3], heads[2]), own_w, gu, gux, do, dox
+        half, place, tokens, ffn_gain[None], heads, own_w, gu, gux, do, dox
     )
     R, H = ROWS, ROWS // 2
     own0 = feed(0, heads0)

time: 177 us -> 179 us (1.011)
  waiting for transfers between devices: 17.4 us -> 28.2 us
  local copies, waits for them, and re-layouts: 17.5 us -> 9.89 us
  other arithmetic: 6.85 us -> 3.36 us
  Pallas kernels: 78.1 us -> 80.9 us
    all_to_all x1, waiting for transfers between devices: 1.97 us -> 8.36 us  [on_device(): arrived = lax.all_to_all(outgoing, 'req', 0, 0, tiled=True)]
    ppermute x20 -> x17, starting transfers between devices: 30.5 us -> 25.6 us  [on_device(): lax.ppermute(a, 'tp', [(i, (i + d) % 4) for i in range(4)])]
    all_to_all x0 -> x1, starting transfers between devices: none -> 4.32 us  [on_device(): heads0 = [lax.all_to_all(out0, 'tp', 0, 0, tiled=True)]]
    all_to_all x0 -> x1, waiting for transfers between devices: none -> 3.73 us  [on_device(): heads0 = [lax.all_to_all(out0, 'tp', 0, 0, tiled=True)]]
    all_to_all x2, waiting for transfers between devices: 0.01 us -> 3.07 us  [on_device(): lax.all_to_all(a, 'req', 0, 0, tiled=True, axis_index_groups=g)]
    unnamed x68 -> x46, local copies, waits for them, and re-layouts: 8.68 us -> 5.86 us
    pallas_call x2 -> x3, Pallas kernels: 25.7 us -> 28.5 us  [the longest x2 25.3 us: ffn(): pl.pallas_call(functools.partial(ffn_kernel, half), grid_spec=gs, out_sha...]
    ppermute x20 -> x17, waiting for transfers between devices: 8.99 us -> 6.65 us  [on_device(): lax.ppermute(a, 'tp', [(i, (i + d) % 4) for i in range(4)])]
  transfers between devices with their start and end apart: 33 -> 31, of which waited for: 10 -> 8; matrix products, arithmetic and copies ran while one was open for 7% -> 4% of each run, Pallas kernels for 43% -> 42%
where the time goes in v1:
time: 179 us; the launch traced here: 178 us
  Pallas kernels  80.9 us (45%)
  starting transfers between devices  54.2 us (30%)
  waiting for transfers between devices  28.2 us (16%)
  local copies, waits for them, and re-layouts  9.89 us (6%)
  other arithmetic  3.36 us (2%)
    ppermute x17, starting transfers between devices, on_device(): lax.ppermute(a, 'tp', [(i, (i + d) % 4) for i in range(4)])  25.6 us
    pallas_call x2, Pallas kernels, ffn(): pl.pallas_call(functools.partial(ffn_kernel, half), grid_spec=gs, out_sha...  25.3 us
    pallas_call x2, Pallas kernels, recall(): pl.pallas_call(functools.partial(recall_kernel, half), grid_spec=gs, out_...  13.1 us
    pallas_call x1, Pallas kernels, project(): pl.pallas_call(project_kernel, grid_spec=gs, out_shape=[jax.ShapeDtypeStr...  12.9 us
    pallas_call x2, Pallas kernels, attend(): pl.pallas_call(attend_kernel, grid=(heads,), in_specs=[pl.BlockSpec((SEG,...  12.7 us
    all_to_all x2, starting transfers between devices, on_device(): lax.all_to_all(a, 'req', 0, 0, tiled=True, axis_index_groups=g)  9.77 us
    pallas_call x3, Pallas kernels, join(): pl.pallas_call(functools.partial(join_kernel, spots), in_specs=[pl.BlockS...  8.42 us
    all_to_all x1, waiting for transfers between devices, on_device(): arrived = lax.all_to_all(outgoing, 'req', 0, 0, tiled=True)  8.36 us
  transfers between devices with their start and end apart: 31, of which 8 were waited for; matrix products, arithmetic and copies ran while one was open for 4% of the time, Pallas kernels for 42%

profile of v1, /device:TPU:32, one launch (start us, length us, event | category | flops | bytes accessed | tf_op | source)
XLA Modules:
  0.0 177.8 jit_solution(7470713442880255937)
XLA Ops:
  0.7 0.7 stack.35.place
  1.4 3.2 %cut_weights.1 = (bf16[176,1024]{1,0:T(8,128)(2,1)}, bf16[480,1024]{1,0:T(8,128)(2,1)}) custom-call(s32[5]{0:T(128)} %stack.35.place, bf16[704,1024]{1,0:T(8,128)(2,1)} %bitcast.21, bf16[704,1024]{1,0:T(8,128)(2,1)} %bitcast.24, bf16[704,1024]{1,0:T(8,128)(2,1)} %rest_6_.1, bf16[256,1024]{1,0:T(8,128)(2,1)} %rest_7_.1), custom_call_target="tpu_custom_call" | custom-call | tf_op jit(solution)/shard_map/cut_weights/pallas_call | solution.py:586
  4.6 1.6 collective-permute-start
  6.2 2.9 %collective-permute-start.1 = (bf16[176,1024]{1,0:T(8,128)(2,1)}, bf16[176,1024]{1,0:T(8,128)(2,1)S(1)}, u32[]{:S(2)}, u32[]{:S(2)}) collective-permute-start(bf16[176,1024]{1,0:T(8,128)(2,1)} %get-tuple-element.56), channel_id=1, source_target_pairs={{0,2},{1,3},{2,0},{3,1},{4,6},{5,7},{6,4},{7,5},{8,10},{9,11},{10,... | collective-permute-start | bytes 1081352 | tf_op jit(solution)/shard_map/ppermute | solution.py:605
  9.2 1.3 collective-permute-start.2
  10.5 0.7 collective-permute-start.3
  11.2 2.6 %collective-permute-start.4 = (bf16[480,1024]{1,0:T(8,128)(2,1)}, bf16[480,1024]{1,0:T(8,128)(2,1)}, u32[]{:S(2)}, u32[]{:S(2)}) collective-permute-start(bf16[480,1024]{1,0:T(8,128)(2,1)} %get-tuple-element.73), channel_id=1, source_target_pairs={{0,3},{1,0},{2,1},{3,2},{4,7},{5,4},{6,5},{7,6},{8,11},{9,8},{10,9... | collective-permute-start | bytes 2949128 | tf_op jit(solution)/shard_map/ppermute | solution.py:605
  13.8 0.7 maximum_maximum_fusion.row
  14.5 0.6 broadcast_in_dim.32.gain
  15.1 12.9 %project.1 = (bf16[2048,256]{1,0:T(8,128)(2,1)}, bf16[2048,512]{1,0:T(8,128)(2,1)}, bf16[2048,256]{1,0:T(8,128)(2,1)}, f32[8,2,128,128]{3,2,1,0:T(8,128)}, bf16[...) custom-call(s32[16]{0:T(128)} %owner.1, s32[16]{0:T(128)} %slot.1, ...), custom_call_target="tpu_custom_call" | custom-call | tf_op jit(solution)/shard_map/project/pallas_call | solution.py:185
  28.0 5.4 %all-to-all-start = ((bf16[8,264,128]{2,1,0:T(8,128)(2,1)}), bf16[8,264,128]{2,1,0:T(8,128)(2,1)S(1)}, u32[]{:S(2)}, u32[]{:S(2)}) async-start(bf16[8,264,128]{2,1,0:T(8,128)(2,1)} %get-tuple-element.63), calls=%async_computation | async-start | bytes 1081344 | tf_op jit(solution)/shard_map/all_to_all | solution.py:635
  33.5 6.3 %attend.2.at0 = f32[1024,256]{1,0:T(8,128)} custom-call(bf16[2048,256]{1,0:T(8,128)(2,1)} %get-tuple-element.69.q, bf16[2048,512]{1,0:T(8,128)(2,1)} %get-tuple-element.59.k.v.kv, bf16[2048,512]{1,0:T(8,128)(2,1)} %get-tuple-element.59.k.v.kv, bf16[16,256]{1,0:T(8,128)(2,1)} %pk.3, bf16[16,256]{1,0:T(8,128)(2,1)} %pv.3, f32[2048,8]{1,0:T(8,128)} %get-tuple-element.61.col, ...), custom_call_target="tpu_custom_call" | custom-call | flops 1400000000 | bytes 4000000 | tf_op jit(solution)/shard_map/attend/pallas_call | solution.py:270
  39.8 2.7 %all-to-all-done.got = bf16[8,264,128]{2,1,0:T(8,128)(2,1)S(1)} async-done(((bf16[8,264,128]{2,1,0:T(8,128)(2,1)}), bf16[8,264,128]{2,1,0:T(8,128)(2,1)S(1)}, u32[]{:S(2)}, u32[]{:S(2)}) %all-to-all-start) | async-done | bytes 540704 | tf_op jit(solution)/shard_map/all_to_all | solution.py:635
  42.5 0.8 copy-done.7
  43.3 2.0 %combine.1 = (f32[2,128,128]{2,1,0:T(8,128)}, f32[8,128]{1,0:T(8,128)}, bf16[4,264,128]{2,1,0:T(8,128)(2,1)}) custom-call(s32[5]{0:T(128)} %stack.35.place, bf16[8,264,128]{2,1,0:T(8,128)(2,1)} %copy-done.7), custom_call_target="tpu_custom_call" | custom-call | tf_op jit(solution)/shard_map/combine/pallas_call | solution.py:227
  45.3 4.4 %all-to-all-start.1 = ((bf16[4,264,128]{2,1,0:T(8,128)(2,1)}), bf16[4,264,128]{2,1,0:T(8,128)(2,1)S(1)}, u32[]{:S(2)}, u32[]{:S(2)}) async-start(bf16[4,264,128]{2,1,0:T(8,128)(2,1)} %get-tuple-element.68), calls=%async_computation.1 | async-start | bytes 540672 | tf_op jit(solution)/shard_map/all_to_all | solution.py:635
  49.7 6.4 %attend.3.at1 = f32[1024,256]{1,0:T(8,128)} custom-call(bf16[2048,256]{1,0:T(8,128)(2,1)} %get-tuple-element.69.q, bf16[2048,512]{1,0:T(8,128)(2,1)} %get-tuple-element.59.k.v.kv, bf16[2048,512]{1,0:T(8,128)(2,1)} %get-tuple-element.59.k.v.kv, bf16[16,256]{1,0:T(8,128)(2,1)} %pk.3, bf16[16,256]{1,0:T(8,128)(2,1)} %pv.3, f32[2048,8]{1,0:T(8,128)} %get-tuple-element.61.col, ...), custom_call_target="tpu_custom_call" | custom-call | flops 1400000000 | bytes 4000000 | tf_op jit(solution)/shard_map/attend/pallas_call | solution.py:270
  56.0 0.4 all-to-all-done.1.got
  56.5 0.1 pad_maximum_fusion.rest_5_.rest_8_
  56.6 0.5 copy-done.6
  57.1 1.7 collective-permute-start.8
  58.8 1.6 collective-permute-start.9
  60.3 1.9 %collective-permute-start.10 = (bf16[3,176,1024]{2,1,0:T(8,128)(2,1)S(1)}, bf16[3,176,1024]{2,1,0:T(8,128)(2,1)}, u32[]{:S(2)}, u32[]{:S(2)}) collective-permute-start(bf16[3,176,1024]{2,1,0:T(8,128)(2,1)S(1)} %pad_maximum_fusion.rest_5_.rest_8_), channel_id=1, source_target_pairs={{0,64},{4,20},{8,72},{12,28},{16,80},{20,4},{24,88},{28,12},{32,96... | collective-permute-start | bytes 3244040 | tf_op jit(solution)/shard_map/ppermute | solution.py:618
  62.3 5.2 %collective-permute-done.7.rest_15_.rest_18_ = bf16[480,1024]{1,0:T(8,128)(2,1)} collective-permute-done((bf16[480,1024]{1,0:T(8,128)(2,1)}, bf16[480,1024]{1,0:T(8,128)(2,1)}, u32[]{:S(2)}, u32[]{:S(2)}) %collective-permute-start.7) | collective-permute-done | bytes 983072 | tf_op jit(solution)/shard_map/ppermute | solution.py:605
  67.5 0.1 slice.30
  67.6 0.6 pad_maximum_fusion.1.bound
  68.2 6.6 %recall.3 = bf16[4,256,256]{2,1,0:T(8,128)(2,1)} custom-call(s32[5]{0:T(128)} %stack.35.place, f32[8]{0:T(128)} %pad_maximum_fusion.1.bound, bf16[2048,256]{1,0:T(8,128)(2,1)} %get-tuple-element.69.q, bf16[2048,256]{1,0:T(8,128)(2,1)} %get-tuple-element.58.ku, bf16[2048,512]{1,0:T(8,128)(2,1)} %get-tuple-element.59.k.v.kv, ...), custom_call_target="tpu_custom_call" | custom-call | flops 400000000 | bytes 4000000 | tf_op jit(solution)/shard_map/recall/pallas_call | solution.py:368
  74.8 4.3 %all-to-all-start.2 = ((bf16[4,256,256]{2,1,0:T(8,128)(2,1)}), bf16[4,256,256]{2,1,0:T(8,128)(2,1)}, u32[]{:S(2)}, u32[]{:S(2)}) async-start(bf16[4,256,256]{2,1,0:T(8,128)(2,1)} %recall.3), calls=%async_computation.2 | async-start | bytes 1048576 | tf_op jit(solution)/shard_map/all_to_all | solution.py:655
  79.1 6.6 %recall.2 = bf16[4,256,256]{2,1,0:T(8,128)(2,1)} custom-call(s32[5]{0:T(128)} %stack.35.place, f32[8]{0:T(128)} %pad_maximum_fusion.1.bound, bf16[2048,256]{1,0:T(8,128)(2,1)} %get-tuple-element.69.q, bf16[2048,256]{1,0:T(8,128)(2,1)} %get-tuple-element.58.ku, bf16[2048,512]{1,0:T(8,128)(2,1)} %get-tuple-element.59.k.v.kv, ...), custom_call_target="tpu_custom_call" | custom-call | flops 400000000 | bytes 4000000 | tf_op jit(solution)/shard_map/recall/pallas_call | solution.py:368
  85.7 3.7 %all-to-all-done.2.rest_0_ = bf16[4,256,256]{2,1,0:T(8,128)(2,1)} async-done(((bf16[4,256,256]{2,1,0:T(8,128)(2,1)}), bf16[4,256,256]{2,1,0:T(8,128)(2,1)}, u32[]{:S(2)}, u32[]{:S(2)}) %all-to-all-start.2) | async-done | bytes 524320 | tf_op jit(solution)/shard_map/all_to_all | solution.py:655
  89.5 2.8 %collective-permute-done.12.rest_10_.rest_13_ = bf16[3,176,1024]{2,1,0:T(8,128)(2,1)} collective-permute-done((bf16[3,176,1024]{2,1,0:T(8,128)(2,1)S(1)}, bf16[3,176,1024]{2,1,0:T(8,128)(2,1)}, u32[]{:S(2)}, u32[]{:S(2)}) %collective-permute-start.12) | collective-permute-done | bytes 1081376 | tf_op jit(solution)/shard_map/ppermute | solution.py:606
  92.4 8.1 %all-to-all-start.3 = ((bf16[32,136,512]{2,1,0:T(8,128)(2,1)}), bf16[32,136,512]{2,1,0:T(8,128)(2,1)}, u32[]{:S(2)}, u32[]{:S(2)}) async-start(bf16[32,136,512]{2,1,0:T(8,128)(2,1)} %get-tuple-element.100), calls=%async_computation.3 | async-start | bytes 8912896 | tf_op jit(solution)/shard_map/all_to_all | solution.py:663
  100.5 0.2 collective-permute-start.11
  100.7 0.4 collective-permute-start.15
  101.1 0.1 collective-permute-start.13
  101.2 0.4 collective-permute-start.14
  101.6 1.9 %slice_bitcast_fusion = (bf16[256,256]{1,0:T(8,128)(2,1)}, bf16[256,256]{1,0:T(8,128)(2,1)}, bf16[256,256]{1,0:T(8,128)(2,1)}, bf16[256,256]{1,0:T(8,128)(2,1)}) fusion(bf16[4,256,256]{2,1,0:T(8,128)(2,1)} %recall.2), kind=kLoop, calls=%fused_computation.1 | loop fusion | bytes 1048576 | tf_op jit(solution)/shard_map/squeeze | solution.py:659
  103.5 0.6 collective-permute-start.16
  104.1 3.5 %collective-permute-done.15.rest_18_.rest_21_ = bf16[480,1024]{1,0:T(8,128)(2,1)S(1)} collective-permute-done((bf16[480,1024]{1,0:T(8,128)(2,1)}, bf16[480,1024]{1,0:T(8,128)(2,1)S(1)}, u32[]{:S(2)}, u32[]{:S(2)}) %collective-permute-start.15) | collective-permute-done | bytes 983072 | tf_op jit(solution)/shard_map/ppermute | solution.py:606
  107.6 1.6 collective-permute-start.17
  109.1 1.1 collective-permute-start.18
  110.2 0.6 broadcast_in_dim.31.gain
  110.8 1.0 copy-done.4
  111.8 12.6 %ffn.2.refs_0_ = bf16[256,1024]{1,0:T(8,128)(2,1)} custom-call(s32[5]{0:T(128)} %stack.35.place, bf16[1,1024]{1,0:T(2,128)(2,1)} %broadcast_in_dim.31.gain, bf16[2048,1024]{1,0:T(8,128)(2,1)} %tokens.3, bf16[4,256,256]{2,1,0:T(8,128)(2,1)} %all-to-all-done.2.rest_0_, bf16[704,1024]{1,0:T(8,128)(2,1)} %bitcast.22, bf16[704,1024]{1,0:T(8,128)(2,1)} %bitcast.25, ...), custom_call_target="tpu_custom_call" | custom-call | tf_op jit(solution)/shard_map/ffn/pallas_call | solution.py:488
  124.5 0.7 copy-done.18
  125.2 3.2 %collective-permute-start.22 = (bf16[256,1024]{1,0:T(8,128)(2,1)}, bf16[256,1024]{1,0:T(8,128)(2,1)S(1)}, u32[]{:S(2)}, u32[]{:S(2)}) collective-permute-start(bf16[256,1024]{1,0:T(8,128)(2,1)} %ffn.2.refs_0_), channel_id=1, source_target_pairs={{0,3},{1,0},{2,1},{3,2},{4,7},{5,4},{6,5},{7,6},{8,11},{9,8},{10,9... | collective-permute-start | bytes 1572872 | tf_op jit(solution)/shard_map/ppermute | solution.py:605
  128.5 12.7 %ffn.3.refs_3_ = bf16[256,1024]{1,0:T(8,128)(2,1)} custom-call(s32[5]{0:T(128)} %stack.35.place, bf16[1,1024]{1,0:T(2,128)(2,1)} %broadcast_in_dim.31.gain, bf16[2048,1024]{1,0:T(8,128)(2,1)} %tokens.3, bf16[256,256]{1,0:T(8,128)(2,1)} %get-tuple-element.95.rest_0_, bf16[256,256]{1,0:T(8,128)(2,1)} %copy-done.16, bf16[256,256]{1,0:T(8,128)(2,1)} %copy-done.17, ...), custom_call_target="tpu_custom_call" | custom-call | tf_op jit(solution)/shard_map/ffn/pallas_call | solution.py:488
  141.3 3.2 %collective-permute-start.20 = (bf16[256,1024]{1,0:T(8,128)(2,1)}, bf16[256,1024]{1,0:T(8,128)(2,1)S(1)}, u32[]{:S(2)}, u32[]{:S(2)}) collective-permute-start(bf16[256,1024]{1,0:T(8,128)(2,1)} %ffn.3.refs_3_), channel_id=1, source_target_pairs={{0,3},{1,0},{2,1},{3,2},{4,7},{5,4},{6,5},{7,6},{8,11},{9,8},{10,9... | collective-permute-start | bytes 1572872 | tf_op jit(solution)/shard_map/ppermute | solution.py:605
  144.6 3.3 %collective-permute-start.26 = (bf16[128,1024]{1,0:T(8,128)(2,1)S(1)}, bf16[128,1024]{1,0:T(8,128)(2,1)S(1)}, u32[]{:S(2)}, u32[]{:S(2)}) collective-permute-start(bf16[128,1024]{1,0:T(8,128)(2,1)S(1)} %slice.42), channel_id=1, source_target_pairs={{0,3},{1,0},{2,1},{3,2},{4,7},{5,4},{6,5},{7,6},{8,11},{9,8},{10,9... | collective-permute-start | bytes 786440 | tf_op jit(solution)/shard_map/ppermute | solution.py:605
  147.9 3.1 %join.3.refs_4_ = bf16[2048,1024]{1,0:T(8,128)(2,1)} custom-call(s32[5]{0:T(128)} %stack.35.place, bf16[256,1024]{1,0:T(8,128)(2,1)} %ffn.2.refs_0_, bf16[256,1024]{1,0:T(8,128)(2,1)} %copy-done.10, bf16[256,1024]{1,0:T(8,128)(2,1)} %copy-done.11, bf16[256,1024]{1,0:T(8,128)(2,1)} %ffn.3.refs_3_), custom_call_target="tpu_custom_call" | custom-call | tf_op jit(solution)/shard_map/join/pallas_call | solution.py:545
  151.0 8.4 %all-to-all-done.3.got = bf16[32,136,512]{2,1,0:T(8,128)(2,1)} async-done(((bf16[32,136,512]{2,1,0:T(8,128)(2,1)}), bf16[32,136,512]{2,1,0:T(8,128)(2,1)}, u32[]{:S(2)}, u32[]{:S(2)}) %all-to-all-start.3) | async-done | bytes 4456480 | tf_op jit(solution)/shard_map/all_to_all | solution.py:663
  159.4 1.2 fusion
  160.5 0.2 select_reduce_fusion
  160.7 0.6 broadcast_clamp_fusion.source
  161.3 3.2 %place.1 = bf16[16,128,512]{2,1,0:T(8,128)(2,1)} custom-call(s32[16]{0:T(128)} %broadcast_clamp_fusion.source, bf16[32,136,512]{2,1,0:T(8,128)(2,1)} %all-to-all-done.3.got), custom_call_target="tpu_custom_call" | custom-call | tf_op jit(solution)/shard_map/place/pallas_call | solution.py:522
  164.6 0.6 collective-permute-start.23
  165.3 2.7 %collective-permute-start.24 = (bf16[128,1024]{1,0:T(8,128)(2,1)S(1)}, bf16[128,1024]{1,0:T(8,128)(2,1)S(1)}, u32[]{:S(2)}, u32[]{:S(2)}) collective-permute-start(bf16[128,1024]{1,0:T(8,128)(2,1)S(1)} %slice.37), channel_id=1, source_target_pairs={{0,3},{1,0},{2,1},{3,2},{4,7},{5,4},{6,5},{7,6},{8,11},{9,8},{10,9... | collective-permute-start | bytes 786440 | tf_op jit(solution)/shard_map/ppermute | solution.py:605
  168.1 0.7 copy-done.12
  168.7 0.7 copy-done.13
  169.4 2.9 %join.4.refs_2_ = bf16[2048,1024]{1,0:T(8,128)(2,1)} custom-call(s32[5]{0:T(128)} %stack.35.place, bf16[256,1024]{1,0:T(8,128)(2,1)} %copy-done.8, bf16[256,1024]{1,0:T(8,128)(2,1)} %copy-done.9, bf16[128,1024]{1,0:T(8,128)(2,1)} %copy-done.12, bf16[128,1024]{1,0:T(8,128)(2,1)} %copy-done.13, ...), custom_call_target="tpu_custom_call", output_to_operand_aliasing={{}: (5, {})} | custom-call | tf_op jit(solution)/shard_map/join/pallas_call | solution.py:545
  172.4 1.4 collective-permute-done.23.refs_0_
  173.8 0.7 copy-done.14
  174.5 0.7 copy-done.15
  175.2 2.4 %join.5 = bf16[2048,1024]{1,0:T(8,128)(2,1)} custom-call(s32[5]{0:T(128)} %stack.35.place, bf16[128,1024]{1,0:T(8,128)(2,1)} %copy-done.14, bf16[128,1024]{1,0:T(8,128)(2,1)} %copy-done.15, bf16[2048,1024]{1,0:T(8,128)(2,1)} %join.4.refs_2_), custom_call_target="tpu_custom_call", output_to_operand_aliasing={{}: (3, {})} | custom-call | tf_op jit(solution)/shard_map/join/pallas_call | solution.py:545
  (76 shorter events, 0.6 us)
Async XLA Ops:
  1.4 12.4 %copy-start.20 = (s32[2048]{0:T(1024)S(1)}, s32[2048]{0:T(1024)}, u32[]{:S(2)}) copy-start(s32[2048]{0:T(1024)} %param.31) | copy-start | bytes 24580
  1.4 12.5 %copy-start.19 = (f32[2048,2]{0,1:T(2,128)S(1)}, f32[2048,2]{0,1:T(2,128)}, u32[]{:S(2)}) copy-start(f32[2048,2]{0,1:T(2,128)} %param.24) | copy-start | bytes 49156
  1.4 13.2 %copy-start.21 = (bf16[1024]{0:T(1024)(128)(2,1)S(1)}, bf16[1024]{0:T(1024)(128)(2,1)}, u32[]{:S(2)}) copy-start(bf16[1024]{0:T(1024)(128)(2,1)} %param.18) | copy-start | bytes 6148
  4.6 28.8 %collective-permute-start = (bf16[176,1024]{1,0:T(8,128)(2,1)}, bf16[176,1024]{1,0:T(8,128)(2,1)S(1)}, u32[]{:S(2)}, u32[]{:S(2)}) collective-permute-start(bf16[176,1024]{1,0:T(8,128)(2,1)} %get-tuple-element.56), channel_id=1, source_target_pairs={{0,1},{1,2},{2,3},{3,0},{4,5},{5,6},{6,7},{7,4},{8,9},{9,10},{10,1... | collective-permute-start | bytes 1081352 | tf_op jit(solution)/shard_map/ppermute | solution.py:605
  6.2 27.2 %collective-permute-start.1 = (bf16[176,1024]{1,0:T(8,128)(2,1)}, bf16[176,1024]{1,0:T(8,128)(2,1)S(1)}, u32[]{:S(2)}, u32[]{:S(2)}) collective-permute-start(bf16[176,1024]{1,0:T(8,128)(2,1)} %get-tuple-element.56), channel_id=1, source_target_pairs={{0,2},{1,3},{2,0},{3,1},{4,6},{5,7},{6,4},{7,5},{8,10},{9,11},{10,... | collective-permute-start | bytes 1081352 | tf_op jit(solution)/shard_map/ppermute | solution.py:605
  9.2 24.3 %collective-permute-start.2 = (bf16[176,1024]{1,0:T(8,128)(2,1)}, bf16[176,1024]{1,0:T(8,128)(2,1)S(1)}, u32[]{:S(2)}, u32[]{:S(2)}) collective-permute-start(bf16[176,1024]{1,0:T(8,128)(2,1)} %get-tuple-element.56), channel_id=1, source_target_pairs={{0,3},{1,0},{2,1},{3,2},{4,7},{5,4},{6,5},{7,6},{8,11},{9,8},{10,9... | collective-permute-start | bytes 1081352 | tf_op jit(solution)/shard_map/ppermute | solution.py:605
  10.5 45.9 %collective-permute-start.3 = (bf16[480,1024]{1,0:T(8,128)(2,1)}, bf16[480,1024]{1,0:T(8,128)(2,1)}, u32[]{:S(2)}, u32[]{:S(2)}) collective-permute-start(bf16[480,1024]{1,0:T(8,128)(2,1)} %get-tuple-element.73), channel_id=1, source_target_pairs={{0,1},{1,2},{2,3},{3,0},{4,5},{5,6},{6,7},{7,4},{8,9},{9,10},{10,1... | collective-permute-start | bytes 2949128 | tf_op jit(solution)/shard_map/ppermute | solution.py:605
  11.2 45.2 %collective-permute-start.4 = (bf16[480,1024]{1,0:T(8,128)(2,1)}, bf16[480,1024]{1,0:T(8,128)(2,1)}, u32[]{:S(2)}, u32[]{:S(2)}) collective-permute-start(bf16[480,1024]{1,0:T(8,128)(2,1)} %get-tuple-element.73), channel_id=1, source_target_pairs={{0,3},{1,0},{2,1},{3,2},{4,7},{5,4},{6,5},{7,6},{8,11},{9,8},{10,9... | collective-permute-start | bytes 2949128 | tf_op jit(solution)/shard_map/ppermute | solution.py:605
  28.0 14.5 %all-to-all-start = ((bf16[8,264,128]{2,1,0:T(8,128)(2,1)}), bf16[8,264,128]{2,1,0:T(8,128)(2,1)S(1)}, u32[]{:S(2)}, u32[]{:S(2)}) async-start(bf16[8,264,128]{2,1,0:T(8,128)(2,1)} %get-tuple-element.63), calls=%async_computation | async-start | bytes 1081344 | tf_op jit(solution)/shard_map/all_to_all | solution.py:635
  33.4 34.1 %collective-permute-start.7 = (bf16[480,1024]{1,0:T(8,128)(2,1)}, bf16[480,1024]{1,0:T(8,128)(2,1)}, u32[]{:S(2)}, u32[]{:S(2)}) collective-permute-start(bf16[480,1024]{1,0:T(8,128)(2,1)} %get-tuple-element.73), channel_id=1, source_target_pairs={{0,2},{1,3},{2,0},{3,1},{4,6},{5,7},{6,4},{7,5},{8,10},{9,11},{10,... | collective-permute-start | bytes 2949128 | tf_op jit(solution)/shard_map/ppermute | solution.py:605
  42.5 0.8 copy-start.7
  45.3 11.1 %all-to-all-start.1 = ((bf16[4,264,128]{2,1,0:T(8,128)(2,1)}), bf16[4,264,128]{2,1,0:T(8,128)(2,1)S(1)}, u32[]{:S(2)}, u32[]{:S(2)}) async-start(bf16[4,264,128]{2,1,0:T(8,128)(2,1)} %get-tuple-element.68), calls=%async_computation.1 | async-start | bytes 540672 | tf_op jit(solution)/shard_map/all_to_all | solution.py:635
  56.4 0.7 copy-start.6
  56.4 18.3 %collective-permute-start.6 = (bf16[480,1024]{1,0:T(8,128)(2,1)}, bf16[480,1024]{1,0:T(8,128)(2,1)}, u32[]{:S(2)}, u32[]{:S(2)}) collective-permute-start(bf16[480,1024]{1,0:T(8,128)(2,1)} %collective-permute-done.3.rest_13_.rest_16_), channel_id=1, source_target_pairs={{0,4},{4,0},{8,12},{12,8},{16,20},{20,16},{24,28},{28,24},{32,36},... | collective-permute-start | bytes 2949128 | tf_op jit(solution)/shard_map/ppermute | solution.py:606
  57.1 43.4 %copy-start = (bf16[3,176,1024]{2,1,0:T(8,128)(2,1)}, bf16[3,176,1024]{2,1,0:T(8,128)(2,1)S(1)}, u32[]{:S(2)}) copy-start(bf16[3,176,1024]{2,1,0:T(8,128)(2,1)S(1)} %pad_maximum_fusion.rest_5_.rest_8_) | copy-start | bytes 3244036
  57.1 32.3 %collective-permute-start.8 = (bf16[3,176,1024]{2,1,0:T(8,128)(2,1)S(1)}, bf16[3,176,1024]{2,1,0:T(8,128)(2,1)S(1)}, u32[]{:S(2)}, u32[]{:S(2)}) collective-permute-start(bf16[3,176,1024]{2,1,0:T(8,128)(2,1)S(1)} %pad_maximum_fusion.rest_5_.rest_8_), channel_id=1, source_target_pairs={{0,32},{4,12},{8,40},{12,20},{16,48},{20,28},{24,56},{28,4},{32,64... | collective-permute-start | bytes 3244040 | tf_op jit(solution)/shard_map/ppermute | solution.py:618
  58.8 30.6 %collective-permute-start.9 = (bf16[3,176,1024]{2,1,0:T(8,128)(2,1)S(1)}, bf16[3,176,1024]{2,1,0:T(8,128)(2,1)S(1)}, u32[]{:S(2)}, u32[]{:S(2)}) collective-permute-start(bf16[3,176,1024]{2,1,0:T(8,128)(2,1)S(1)} %pad_maximum_fusion.rest_5_.rest_8_), channel_id=1, source_target_pairs={{0,96},{4,28},{8,104},{12,4},{16,112},{20,12},{24,120},{28,20},{32... | collective-permute-start | bytes 3244040 | tf_op jit(solution)/shard_map/ppermute | solution.py:618
  60.3 29.1 %collective-permute-start.10 = (bf16[3,176,1024]{2,1,0:T(8,128)(2,1)S(1)}, bf16[3,176,1024]{2,1,0:T(8,128)(2,1)}, u32[]{:S(2)}, u32[]{:S(2)}) collective-permute-start(bf16[3,176,1024]{2,1,0:T(8,128)(2,1)S(1)} %pad_maximum_fusion.rest_5_.rest_8_), channel_id=1, source_target_pairs={{0,64},{4,20},{8,72},{12,28},{16,80},{20,4},{24,88},{28,12},{32,96... | collective-permute-start | bytes 3244040 | tf_op jit(solution)/shard_map/ppermute | solution.py:618
  67.5 18.2 %collective-permute-start.5 = (bf16[480,1024]{1,0:T(8,128)(2,1)}, bf16[480,1024]{1,0:T(8,128)(2,1)}, u32[]{:S(2)}, u32[]{:S(2)}) collective-permute-start(bf16[480,1024]{1,0:T(8,128)(2,1)} %collective-permute-done.4.rest_14_.rest_17_), channel_id=1, source_target_pairs={{0,4},{4,0},{8,12},{12,8},{16,20},{20,16},{24,28},{28,24},{32,36},... | collective-permute-start | bytes 2949128 | tf_op jit(solution)/shard_map/ppermute | solution.py:606
  74.8 14.6 %all-to-all-start.2 = ((bf16[4,256,256]{2,1,0:T(8,128)(2,1)}), bf16[4,256,256]{2,1,0:T(8,128)(2,1)}, u32[]{:S(2)}, u32[]{:S(2)}) async-start(bf16[4,256,256]{2,1,0:T(8,128)(2,1)} %recall.3), calls=%async_computation.2 | async-start | bytes 1048576 | tf_op jit(solution)/shard_map/all_to_all | solution.py:655
  89.4 3.0 %copy-start.1 = (bf16[3,176,1024]{2,1,0:T(8,128)(2,1)}, bf16[3,176,1024]{2,1,0:T(8,128)(2,1)S(1)}, u32[]{:S(2)}) copy-start(bf16[3,176,1024]{2,1,0:T(8,128)(2,1)S(1)} %collective-permute-done.8.rest_6_.rest_9_) | copy-start | bytes 3244036
  89.4 11.7 %copy-start.2 = (bf16[3,176,1024]{2,1,0:T(8,128)(2,1)}, bf16[3,176,1024]{2,1,0:T(8,128)(2,1)S(1)}, u32[]{:S(2)}) copy-start(bf16[3,176,1024]{2,1,0:T(8,128)(2,1)S(1)} %collective-permute-done.9.rest_7_.rest_10_) | copy-start | bytes 3244036
  89.4 20.8 %copy-start.22 = (bf16[1024]{0:T(1024)(128)(2,1)S(1)}, bf16[1024]{0:T(1024)(128)(2,1)}, u32[]{:S(2)}) copy-start(bf16[1024]{0:T(1024)(128)(2,1)} %param.27) | copy-start | bytes 6148
  89.4 2.9 %collective-permute-start.12 = (bf16[3,176,1024]{2,1,0:T(8,128)(2,1)S(1)}, bf16[3,176,1024]{2,1,0:T(8,128)(2,1)}, u32[]{:S(2)}, u32[]{:S(2)}) collective-permute-start(bf16[3,176,1024]{2,1,0:T(8,128)(2,1)S(1)} %collective-permute-done.8.rest_6_.rest_9_), channel_id=1, source_target_pairs={{0,4},{4,0},{8,12},{12,8},{16,20},{20,16},{24,28},{28,24},{32,36},... | collective-permute-start | bytes 3244040 | tf_op jit(solution)/shard_map/ppermute | solution.py:606
  92.4 67.0 %all-to-all-start.3 = ((bf16[32,136,512]{2,1,0:T(8,128)(2,1)}), bf16[32,136,512]{2,1,0:T(8,128)(2,1)}, u32[]{:S(2)}, u32[]{:S(2)}) async-start(bf16[32,136,512]{2,1,0:T(8,128)(2,1)} %get-tuple-element.100), calls=%async_computation.3 | async-start | bytes 8912896 | tf_op jit(solution)/shard_map/all_to_all | solution.py:663
  100.5 8.7 %collective-permute-start.11 = (bf16[3,176,1024]{2,1,0:T(8,128)(2,1)S(1)}, bf16[3,176,1024]{2,1,0:T(8,128)(2,1)S(1)}, u32[]{:S(2)}, u32[]{:S(2)}) collective-permute-start(bf16[3,176,1024]{2,1,0:T(8,128)(2,1)S(1)} %pad_maximum_fusion.rest_5_.rest_8_), channel_id=1, source_target_pairs={{0,4},{4,0},{8,12},{12,8},{16,20},{20,16},{24,28},{28,24},{32,36},... | collective-permute-start | bytes 3244040 | tf_op jit(solution)/shard_map/ppermute | solution.py:606
  100.7 6.9 %collective-permute-start.15 = (bf16[480,1024]{1,0:T(8,128)(2,1)}, bf16[480,1024]{1,0:T(8,128)(2,1)S(1)}, u32[]{:S(2)}, u32[]{:S(2)}) collective-permute-start(bf16[480,1024]{1,0:T(8,128)(2,1)} %collective-permute-done.7.rest_15_.rest_18_), channel_id=1, source_target_pairs={{0,4},{4,0},{8,12},{12,8},{16,20},{20,16},{24,28},{28,24},{32,36},... | collective-permute-start | bytes 2949128 | tf_op jit(solution)/shard_map/ppermute | solution.py:606
  101.1 9.8 %collective-permute-start.13 = (bf16[3,176,1024]{2,1,0:T(8,128)(2,1)S(1)}, bf16[3,176,1024]{2,1,0:T(8,128)(2,1)S(1)}, u32[]{:S(2)}, u32[]{:S(2)}) collective-permute-start(bf16[3,176,1024]{2,1,0:T(8,128)(2,1)S(1)} %collective-permute-done.9.rest_7_.rest_10_), channel_id=1, source_target_pairs={{0,4},{4,0},{8,12},{12,8},{16,20},{20,16},{24,28},{28,24},{32,36},... | collective-permute-start | bytes 3244040 | tf_op jit(solution)/shard_map/ppermute | solution.py:606
  101.2 10.6 %collective-permute-start.14 = (bf16[3,176,1024]{2,1,0:T(8,128)(2,1)}, bf16[3,176,1024]{2,1,0:T(8,128)(2,1)}, u32[]{:S(2)}, u32[]{:S(2)}) collective-permute-start(bf16[3,176,1024]{2,1,0:T(8,128)(2,1)} %collective-permute-done.10.rest_8_.rest_11_), channel_id=1, source_target_pairs={{0,4},{4,0},{8,12},{12,8},{16,20},{20,16},{24,28},{28,24},{32,36},... | collective-permute-start | bytes 3244040 | tf_op jit(solution)/shard_map/ppermute | solution.py:606
  103.5 21.0 %collective-permute-start.16 = (bf16[256,256]{1,0:T(8,128)(2,1)}, bf16[256,256]{1,0:T(8,128)(2,1)S(1)}, u32[]{:S(2)}, u32[]{:S(2)}) collective-permute-start(bf16[256,256]{1,0:T(8,128)(2,1)} %get-tuple-element.110), channel_id=1, source_target_pairs={{0,1},{1,2},{2,3},{3,0},{4,5},{5,6},{6,7},{7,4},{8,9},{9,10},{10,1... | collective-permute-start | bytes 393224 | tf_op jit(solution)/shard_map/ppermute | solution.py:605
  107.6 3.2 %copy-start.5 = (bf16[480,1024]{1,0:T(8,128)(2,1)}, bf16[480,1024]{1,0:T(8,128)(2,1)S(1)}, u32[]{:S(2)}) copy-start(bf16[480,1024]{1,0:T(8,128)(2,1)S(1)} %collective-permute-done.15.rest_18_.rest_21_) | copy-start | bytes 2949124
  107.6 16.9 %collective-permute-start.17 = (bf16[256,256]{1,0:T(8,128)(2,1)}, bf16[256,256]{1,0:T(8,128)(2,1)S(1)}, u32[]{:S(2)}, u32[]{:S(2)}) collective-permute-start(bf16[256,256]{1,0:T(8,128)(2,1)} %get-tuple-element.109), channel_id=1, source_target_pairs={{0,3},{1,0},{2,1},{3,2},{4,7},{5,4},{6,5},{7,6},{8,11},{9,8},{10,9... | collective-permute-start | bytes 393224 | tf_op jit(solution)/shard_map/ppermute | solution.py:605
  109.1 2.7 %copy-start.3 = (bf16[3,176,1024]{2,1,0:T(8,128)(2,1)}, bf16[3,176,1024]{2,1,0:T(8,128)(2,1)S(1)}, u32[]{:S(2)}) copy-start(bf16[3,176,1024]{2,1,0:T(8,128)(2,1)S(1)} %collective-permute-done.11.rest_9_.rest_12_) | copy-start | bytes 3244036
  109.1 15.4 %collective-permute-start.18 = (bf16[256,256]{1,0:T(8,128)(2,1)}, bf16[256,256]{1,0:T(8,128)(2,1)S(1)}, u32[]{:S(2)}, u32[]{:S(2)}) collective-permute-start(bf16[256,256]{1,0:T(8,128)(2,1)} %get-tuple-element.108), channel_id=1, source_target_pairs={{0,2},{1,3},{2,0},{3,1},{4,6},{5,7},{6,4},{7,5},{8,10},{9,11},{10,... | collective-permute-start | bytes 393224 | tf_op jit(solution)/shard_map/ppermute | solution.py:605
  110.8 1.0 copy-start.4
  124.5 4.0 %copy-start.16 = (bf16[256,256]{1,0:T(8,128)(2,1)}, bf16[256,256]{1,0:T(8,128)(2,1)S(1)}, u32[]{:S(2)}) copy-start(bf16[256,256]{1,0:T(8,128)(2,1)S(1)} %collective-permute-done.16.rest_1_) | copy-start | bytes 393220
  124.5 4.0 %copy-start.17 = (bf16[256,256]{1,0:T(8,128)(2,1)}, bf16[256,256]{1,0:T(8,128)(2,1)S(1)}, u32[]{:S(2)}) copy-start(bf16[256,256]{1,0:T(8,128)(2,1)S(1)} %collective-permute-done.17.rest_2_) | copy-start | bytes 393220
  124.5 0.7 copy-start.18
  125.2 19.2 %collective-permute-start.21 = (bf16[256,1024]{1,0:T(8,128)(2,1)}, bf16[256,1024]{1,0:T(8,128)(2,1)S(1)}, u32[]{:S(2)}, u32[]{:S(2)}) collective-permute-start(bf16[256,1024]{1,0:T(8,128)(2,1)} %ffn.2.refs_0_), channel_id=1, source_target_pairs={{0,1},{1,2},{2,3},{3,0},{4,5},{5,6},{6,7},{7,4},{8,9},{9,10},{10,1... | collective-permute-start | bytes 1572872 | tf_op jit(solution)/shard_map/ppermute | solution.py:605
  125.2 19.4 %collective-permute-start.22 = (bf16[256,1024]{1,0:T(8,128)(2,1)}, bf16[256,1024]{1,0:T(8,128)(2,1)S(1)}, u32[]{:S(2)}, u32[]{:S(2)}) collective-permute-start(bf16[256,1024]{1,0:T(8,128)(2,1)} %ffn.2.refs_0_), channel_id=1, source_target_pairs={{0,3},{1,0},{2,1},{3,2},{4,7},{5,4},{6,5},{7,6},{8,11},{9,8},{10,9... | collective-permute-start | bytes 1572872 | tf_op jit(solution)/shard_map/ppermute | solution.py:605
  141.2 23.4 %collective-permute-start.19 = (bf16[256,1024]{1,0:T(8,128)(2,1)}, bf16[256,1024]{1,0:T(8,128)(2,1)S(1)}, u32[]{:S(2)}, u32[]{:S(2)}) collective-permute-start(bf16[256,1024]{1,0:T(8,128)(2,1)} %ffn.3.refs_3_), channel_id=1, source_target_pairs={{0,1},{1,2},{2,3},{3,0},{4,5},{5,6},{6,7},{7,4},{8,9},{9,10},{10,1... | collective-permute-start | bytes 1572872 | tf_op jit(solution)/shard_map/ppermute | solution.py:605
  141.3 23.3 %collective-permute-start.20 = (bf16[256,1024]{1,0:T(8,128)(2,1)}, bf16[256,1024]{1,0:T(8,128)(2,1)S(1)}, u32[]{:S(2)}, u32[]{:S(2)}) collective-permute-start(bf16[256,1024]{1,0:T(8,128)(2,1)} %ffn.3.refs_3_), channel_id=1, source_target_pairs={{0,3},{1,0},{2,1},{3,2},{4,7},{5,4},{6,5},{7,6},{8,11},{9,8},{10,9... | collective-permute-start | bytes 1572872 | tf_op jit(solution)/shard_map/ppermute | solution.py:605
  144.5 3.4 %copy-start.10 = (bf16[256,1024]{1,0:T(8,128)(2,1)}, bf16[256,1024]{1,0:T(8,128)(2,1)S(1)}, u32[]{:S(2)}) copy-start(bf16[256,1024]{1,0:T(8,128)(2,1)S(1)} %collective-permute-done.21.refs_1_) | copy-start | bytes 1572868
  144.5 23.5 %collective-permute-start.25 = (bf16[128,1024]{1,0:T(8,128)(2,1)S(1)}, bf16[128,1024]{1,0:T(8,128)(2,1)S(1)}, u32[]{:S(2)}, u32[]{:S(2)}) collective-permute-start(bf16[128,1024]{1,0:T(8,128)(2,1)S(1)} %slice.41), channel_id=1, source_target_pairs={{0,1},{1,2},{2,3},{3,0},{4,5},{5,6},{6,7},{7,4},{8,9},{9,10},{10,1... | collective-permute-start | bytes 786440 | tf_op jit(solution)/shard_map/ppermute | solution.py:605
  144.6 3.3 %copy-start.11 = (bf16[256,1024]{1,0:T(8,128)(2,1)}, bf16[256,1024]{1,0:T(8,128)(2,1)S(1)}, u32[]{:S(2)}) copy-start(bf16[256,1024]{1,0:T(8,128)(2,1)S(1)} %collective-permute-done.22.refs_2_) | copy-start | bytes 1572868
  144.6 23.4 %collective-permute-start.26 = (bf16[128,1024]{1,0:T(8,128)(2,1)S(1)}, bf16[128,1024]{1,0:T(8,128)(2,1)S(1)}, u32[]{:S(2)}, u32[]{:S(2)}) collective-permute-start(bf16[128,1024]{1,0:T(8,128)(2,1)S(1)} %slice.42), channel_id=1, source_target_pairs={{0,3},{1,0},{2,1},{3,2},{4,7},{5,4},{6,5},{7,6},{8,11},{9,8},{10,9... | collective-permute-start | bytes 786440 | tf_op jit(solution)/shard_map/ppermute | solution.py:605
  164.6 3.5 %copy-start.8 = (bf16[256,1024]{1,0:T(8,128)(2,1)}, bf16[256,1024]{1,0:T(8,128)(2,1)S(1)}, u32[]{:S(2)}) copy-start(bf16[256,1024]{1,0:T(8,128)(2,1)S(1)} %collective-permute-done.19.refs_0_) | copy-start | bytes 1572868
  164.6 3.5 %copy-start.9 = (bf16[256,1024]{1,0:T(8,128)(2,1)}, bf16[256,1024]{1,0:T(8,128)(2,1)S(1)}, u32[]{:S(2)}) copy-start(bf16[256,1024]{1,0:T(8,128)(2,1)S(1)} %collective-permute-done.20.refs_1_) | copy-start | bytes 1572868
  164.6 9.1 %collective-permute-start.23 = (bf16[128,1024]{1,0:T(8,128)(2,1)S(1)}, bf16[128,1024]{1,0:T(8,128)(2,1)S(1)}, u32[]{:S(2)}, u32[]{:S(2)}) collective-permute-start(bf16[128,1024]{1,0:T(8,128)(2,1)S(1)} %slice.36), channel_id=1, source_target_pairs={{0,1},{1,2},{2,3},{3,0},{4,5},{5,6},{6,7},{7,4},{8,9},{9,10},{10,1... | collective-permute-start | bytes 786440 | tf_op jit(solution)/shard_map/ppermute | solution.py:605
  165.3 8.5 %collective-permute-start.24 = (bf16[128,1024]{1,0:T(8,128)(2,1)S(1)}, bf16[128,1024]{1,0:T(8,128)(2,1)S(1)}, u32[]{:S(2)}, u32[]{:S(2)}) collective-permute-start(bf16[128,1024]{1,0:T(8,128)(2,1)S(1)} %slice.37), channel_id=1, source_target_pairs={{0,3},{1,0},{2,1},{3,2},{4,7},{5,4},{6,5},{7,6},{8,11},{9,8},{10,9... | collective-permute-start | bytes 786440 | tf_op jit(solution)/shard_map/ppermute | solution.py:605
  168.0 0.7 copy-start.12
  168.7 0.7 copy-start.13
  173.8 0.7 copy-start.14
  174.5 0.7 copy-start.15

commit v2 on v1

--- a/solution.py
+++ b/solution.py
@@ -286,7 +286,7 @@
     )(q, kv, kv, pk, pv, col, row)
 
 
-def recall_kernel(half, place, bound, q, ku, kv, mi, e1, info, got, col, row, rows, at0, at1, gain, out, pst, pdoc):
+def recall_kernel(half, place, bound, q, ku, kv, mi, e1, info, got, col, row, rows, at0, at1, gain, o0, o1, o2, o3, pst, pdoc):
     b = pl.program_id(0)
     chunk = 2 * b + half
 
@@ -337,7 +337,11 @@
         qw = qh.astype(F32)
         rec = rec * (lax.rsqrt(jnp.mean(qw * qw, axis=-1, keepdims=True) + 1e-6) * (1.0 / math.sqrt(HD)))
         at = jnp.where(chunk < SEG // CH, at0[:, s], at1[:, s])
-        out[0, :, s] = (at + rms(rec, 1e-5) * gain[:, s]).astype(BF)
+        val = (at + rms(rec, 1e-5) * gain[:, s]).astype(BF)
+        for d, out in enumerate((o0, o1, o2, o3)):
+            @pl.when(lax.rem(b - place[2] + 4, 4) == d)
+            def _():
+                out[:, s] = val
 
 
 def recall(half, place, bound, q, ku, kv, mi, e1, info, got, col, row, at0, at1, gain):
@@ -362,13 +366,13 @@
             pl.BlockSpec((CH, 256), lambda b, p, d: (jnp.maximum(2 * b + half - per, 0), 0)),
             full(gain),
         ],
-        out_specs=pl.BlockSpec((1, CH, 256), lambda b, p, d: (b if half == 0 else lax.rem(b - p[2] + 4, 4), 0, 0)),
+        out_specs=[pl.BlockSpec((CH, 256), lambda b, p, d: (0, 0))] * 4,
         scratch_shapes=[pltpu.VMEM((2, HD, HD), F32), pltpu.VMEM((8, 128), F32)],
     )
     return pl.pallas_call(
         functools.partial(recall_kernel, half),
         grid_spec=gs,
-        out_shape=jax.ShapeDtypeStruct((4, CH, 256), BF),
+        out_shape=[jax.ShapeDtypeStruct((CH, 256), BF)] * 4,
         name="recall",
         cost_estimate=pl.CostEstimate(flops=400_000_000, transcendentals=0, bytes_accessed=4_000_000),
     )(place, bound, q, ku, kv, mi, e1, info, got, col, row, row, at0, at1, gain)
@@ -376,15 +380,9 @@
 
 def ffn_kernel(half, place, gain, tokens, *rest):
     y = place[2]
-    if half == 0:
-        heads = [rest[0].at[lax.rem(y - d + 4, 4)] for d in (0, 1, 3, 2)]
-    else:
-        heads = rest[0:4]
-    rest = rest[1:] if half == 0 else rest[4:]
-    own = rest[0:4]
-    gu = (rest[4:8], rest[8:12])
-    do = (rest[12:15], rest[15:18])
-    out, tok, hv, wgu, wd, wo, norm, acc, sem = rest[18:]
+    heads, own = rest[0:4], rest[4:8]
+    sets = (rest[8:14], rest[14:20])
+    out, tok, hv, wgu, wd, wo, norm, acc, sem = rest[20:]
     core = place[3]
     count = [0]
     waits = {}
@@ -395,9 +393,9 @@
         waits.setdefault(key, []).append(c)
         c.start()
 
-    def fetch(kind, group):
-        key = (kind, group)
-        if group == 0:
+    def fetch(kind, i):
+        key = (kind, i)
+        if i == 0:
             if kind == "out":
                 copy(key, own[3], wo.at[0])
             elif kind == "up":
@@ -406,21 +404,17 @@
             else:
                 copy(key, own[2], wd.at[0])
             return
-        spots = (1, 2) if group == 1 else (3,)
         for which in range(2):
             at = core if which == 0 else 1 - core
+            p, q = sets[which][2 * i - 2], sets[which][2 * i - 1]
             if kind == "up":
-                pos = jnp.where(at == 0, place[1], place[4])
-                span = pl.ds(spots[0], len(spots))
-                for i, hop in enumerate((0, 3, 1, 2)):
-                    p = lax.rem(pos + hop, 4)
-                    copy(key, gu[which][i].at[pl.ds(spots[0] - 1, len(spots))], wgu.at[at, span, pl.ds(p * 176, 176), :])
-                continue
-            for i in spots:
-                if kind == "down":
-                    copy(key, do[which][i - 1].at[pl.ds(0, 352), :], wd.at[i, pl.ds(at * 352, 352), :])
-                else:
-                    copy(key, do[which][i - 1].at[pl.ds(352, 128), :], wo.at[i, pl.ds(at * 128, 128), :])
+                copy(key, p.at[pl.ds(0, 352), :], wgu.at[0, i, pl.ds(at * 352, 352), :])
+                copy(key, p.at[pl.ds(352, 240), :], wgu.at[1, i, pl.ds(at * 352, 240), :])
+                copy(key, q.at[pl.ds(0, 112), :], wgu.at[1, i, pl.ds(at * 352 + 240, 112), :])
+            elif kind == "down":
+                copy(key, q.at[pl.ds(112, 352), :], wd.at[i, pl.ds(at * 352, 352), :])
+            else:
+                copy(key, q.at[pl.ds(464, 128), :], wo.at[i, pl.ds(at * 128, 128), :])
 
     def ready(kind, group):
         for c in waits[(kind, group)]:
@@ -429,29 +423,28 @@
     copy(("in", 0), tokens.at[pl.ds((2 * y + half) * ROWS, ROWS), :], tok)
     for i in range(4):
         copy(("in", 0), heads[i], hv.at[i])
-    for group in range(3):
-        fetch("out", group)
+    for i in range(4):
+        fetch("out", i)
     fetch("up", 0)
     fetch("down", 0)
     ready("in", 0)
     total = tok[...].astype(F32)
-    for i, group in enumerate((0, 1, None, 2)):
-        if group is not None:
-            ready("out", group)
+    for i in range(4):
+        ready("out", i)
         total = total + dot(hv[i], wo[i])
-    for group in (1, 2):
-        fetch("up", group)
-        fetch("down", group)
+    for i in (1, 2, 3):
+        fetch("up", i)
+        fetch("down", i)
     resid = total.astype(BF).astype(F32)
     acc[...] = resid
     norm[...] = (rms(resid, 1e-5) * gain[...].astype(F32)).astype(BF)
 
     def step(i, carry):
-        for index, group in ((0, 0), (1, 1), (3, 2)):
+        for index in range(4):
             @pl.when(i == index)
             def _():
-                ready("up", group)
-                ready("down", group)
+                ready("up", index)
+                ready("down", index)
 
         n = norm[...]
         g = dot_t(n, wgu[0, i])
@@ -464,11 +457,11 @@
     out[...] = acc[...].astype(BF)
 
 
-def ffn(half, place, tokens, gain, heads, own, gu, gux, do, dox):
+def ffn(half, place, tokens, gain, heads, own, mine, other):
     d = tokens.shape[1]
     full = lambda a: pl.BlockSpec(a.shape, lambda i, p: (0,) * a.ndim)
     anys = pl.BlockSpec(memory_space=ANY)
-    ws = [*own, *gu, *gux, *do, *dox]
+    ws = [*own, *mine, *other]
     gs = pltpu.PrefetchScalarGridSpec(
         num_scalar_prefetch=1,
         grid=(1,),
@@ -482,7 +475,7 @@
             pltpu.VMEM((4, 256, 1024), BF),
             pltpu.VMEM((ROWS, d), BF),
             pltpu.VMEM((ROWS, d), F32),
-            pltpu.SemaphoreType.DMA((37,)),
+            pltpu.SemaphoreType.DMA((39,)),
         ],
     )
     return pl.pallas_call(
@@ -553,42 +546,31 @@
     )(place, *pieces, *rest)
 
 
-def cut_kernel(place, gate, up, down, last, piece, both, sem):
+def cut_kernel(place, gate, up, down, last, p, q, sem):
     core = place[3]
-    at = jnp.where(core == 0, place[1], place[4])
-    rows = pl.ds(at * 176, 176)
-    from_gate = pltpu.make_async_copy(gate.at[rows, :], piece, sem.at[0])
-    from_up = pltpu.make_async_copy(up.at[rows, :], piece, sem.at[0])
-    rest = [
-        pltpu.make_async_copy(down.at[pl.ds(core * 352, 352), :], both.at[pl.ds(0, 352), :], sem.at[1]),
-        pltpu.make_async_copy(last.at[pl.ds(core * 128, 128), :], both.at[pl.ds(352, 128), :], sem.at[2]),
+    copies = [
+        pltpu.make_async_copy(gate.at[pl.ds(core * 352, 352), :], p.at[pl.ds(0, 352), :], sem.at[0]),
+        pltpu.make_async_copy(up.at[pl.ds(core * 352, 240), :], p.at[pl.ds(352, 240), :], sem.at[1]),
+        pltpu.make_async_copy(up.at[pl.ds(core * 352 + 240, 112), :], q.at[pl.ds(0, 112), :], sem.at[2]),
+        pltpu.make_async_copy(down.at[pl.ds(core * 352, 352), :], q.at[pl.ds(112, 352), :], sem.at[3]),
+        pltpu.make_async_copy(last.at[pl.ds(core * 128, 128), :], q.at[pl.ds(464, 128), :], sem.at[4]),
     ]
-
-    @pl.when(core == 0)
-    def _():
-        from_gate.start()
-
-    @pl.when(core != 0)
-    def _():
-        from_up.start()
-
-    for c in rest:
+    for c in copies:
         c.start()
-    from_gate.wait()
-    for c in rest:
+    for c in copies:
         c.wait()
 
 
 def cut_weights(place, gate, up, down, last):
     anys = pl.BlockSpec(memory_space=ANY)
     vm = pl.BlockSpec(memory_space=pltpu.VMEM)
-    width = gate.shape[1]
+    shape = jax.ShapeDtypeStruct((592, gate.shape[1]), BF)
     return pl.pallas_call(
         cut_kernel,
         in_specs=[pl.BlockSpec(memory_space=pltpu.SMEM)] + [anys] * 4,
         out_specs=[vm, vm],
-        out_shape=[jax.ShapeDtypeStruct((176, width), BF), jax.ShapeDtypeStruct((480, width), BF)],
-        scratch_shapes=[pltpu.SemaphoreType.DMA((3,))],
+        out_shape=[shape, shape],
+        scratch_shapes=[pltpu.SemaphoreType.DMA((5,))],
         name="cut_weights",
     )(place, gate, up, down, last)
 
@@ -606,21 +588,9 @@
     swap = lambda a: lax.ppermute(a, "req", [(i, i ^ 1) for i in range(reqs)])
     tie = lambda *a: lax.optimization_barrier(a)
 
-    def around(a, d):
-        def to(i):
-            xx, zz, c = i // 8, (i // 2) % 4, i % 2
-            if c == 0:
-                xx = (xx + d) % 4
-            else:
-                zz = (zz + d) % 4
-            return xx * 8 + zz * 2 + c
-
-        return lax.ppermute(a, "req", [(i, to(i)) for i in range(reqs)])
-
     gate, up = w_gate.T, w_up.T
-    piece, half_do = cut_weights(place, gate, up, w_down, w_out)
-    s1, s3, s2 = [shift(piece, d) for d in (1, 3, 2)]
-    do1, do3, do2 = [shift(half_do, d) for d in (1, 3, 2)]
+    p, qq = cut_weights(place, gate, up, w_down, w_out)
+    p1, q3, q1w, p3 = shift(p, 1), shift(qq, -1), shift(qq, 1), shift(p, -1)
 
     doc = doc_ids.astype(F32)
     row = jnp.concatenate([doc[None], log_forget.T, jnp.zeros((5, count), F32)])
@@ -635,34 +605,33 @@
     spread = lambda a, g: lax.all_to_all(a, "req", 0, 0, tiled=True, axis_index_groups=g)
     got8 = spread(pay, group8)
 
-    q, s1, s2, s3 = tie(q, s1, s2, s3)
     at0 = attend(q, kv, persist_key, persist_value, col, row, 0)
     at0, got8 = tie(at0, got8)
     e1, info, pay4 = combine(place, got8)
     got4 = spread(pay4, group4)
     q1, at0, _ = tie(q, at0, pay4)
     at1 = attend(q1, kv, persist_key, persist_value, col, row, 1)
-    at1, got4, s1, s2, s3, do1, do3 = tie(at1, got4, s1, s2, s3, do1, do3)
-    near = jnp.stack([s1, s3, s2])
-    far = [around(near, d) for d in (1, 3, 2)]
+    at1, got4, outgoing = tie(at1, got4, outgoing)
+    arrived = lax.all_to_all(outgoing, "req", 0, 0, tiled=True)
+    at1, p1, q3, q1w, p3 = tie(at1, p1, q3, q1w, p3)
+    p2, q2 = shift(p1, 1), shift(q3, -1)
 
     gain = mem_gain[None]
     own_w = (gate, up, w_down, w_out)
     mem = lambda half: recall(half, place, bound, q, ku, kv, mi, e1, info, got4, col, row, at0, at1, gain)
-    do1x = swap(do1)
+    send = lambda out: [out[0]] + [shift(out[d], d) for d in (1, 3, 2)]
+    p1x, q3x, q1x, p3x = swap(p1), swap(q3), swap(q1w), swap(p3)
     out0 = mem(0)
-    out0, do1x, do2 = tie(out0, do1x, do2)
-    heads0 = [lax.all_to_all(out0, "tp", 0, 0, tiled=True)]
-    do3x = swap(do3)
+    tied = tie(*out0, p1x, q3x, q1x, p3x)
+    out0, (p1x, q3x, q1x, p3x) = tied[:4], tied[4:]
+    heads0 = send(out0)
     out1 = mem(1)
-    out1, do3x, heads0[0] = tie(out1, do3x, heads0[0])
-    heads1 = [out1[0]] + [shift(out1[d], d) for d in (1, 3, 2)]
-    near, outgoing, _, *far = tie(near, outgoing, out1, *far)
-    nearx, do2x, *farx = [swap(a) for a in (near, do2, *far)]
-    outgoing, farx[0] = tie(outgoing, farx[0])
-    arrived = lax.all_to_all(outgoing, "req", 0, 0, tiled=True)
-    gu, do = [near, *far], [do1, do3, do2]
-    gux, dox = [nearx, *farx], [do1x, do3x, do2x]
+    tied = tie(*out1, *heads0)
+    out1, heads0 = tied[:4], tied[4:]
+    heads1 = send(out1)
+    p2, q2, _ = tie(p2, q2, out1[0])
+    p2x, q2x = swap(p2), swap(q2)
+    mine, other = [p1, q1w, p3, q3, p2, q2], [p1x, q1x, p3x, q3x, p2x, q2x]
 
     slots = arrived[:, PAGE, 0].astype(F32)
     wanted = slots[None, :] == (jnp.arange(count // PAGE) + 1).astype(F32)[:, None]
@@ -670,7 +639,7 @@
     kv_cache = place_pages(jnp.clip(source, 0, reqs - 1), arrived, count // PAGE)
 
     feed = lambda half, heads: ffn(
-        half, place, tokens, ffn_gain[None], heads, own_w, gu, gux, do, dox
+        half, place, tokens, ffn_gain[None], heads, own_w, mine, other
     )
     R, H = ROWS, ROWS // 2
     own0 = feed(0, heads0)

time: 179 us -> 167 us (0.933)
  starting transfers between devices: 54.2 us -> 48 us
  waiting for transfers between devices: 28.2 us -> 24.6 us
    ppermute x17 -> x20, waiting for transfers between devices: 6.65 us -> 18.4 us  [on_device(): lax.ppermute(a, 'tp', [(i, (i + d) % 4) for i in range(4)])]
    all_to_all x1, waiting for transfers between devices: 8.36 us -> 0.01 us  [on_device(): arrived = lax.all_to_all(outgoing, 'req', 0, 0, tiled=True)]
    ppermute x3 -> x0, starting transfers between devices: 5.18 us -> none  [around(): return lax.ppermute(a, 'req', [(i, to(i)) for i in range(reqs)])]
    ppermute x17 -> x20, starting transfers between devices: 25.6 us -> 30 us  [on_device(): lax.ppermute(a, 'tp', [(i, (i + d) % 4) for i in range(4)])]
    all_to_all x1 -> x0, starting transfers between devices: 4.32 us -> none  [on_device(): heads0 = [lax.all_to_all(out0, 'tp', 0, 0, tiled=True)]]
    all_to_all x1 -> x0, waiting for transfers between devices: 3.73 us -> none  [on_device(): heads0 = [lax.all_to_all(out0, 'tp', 0, 0, tiled=True)]]
    ppermute x7 -> x6, waiting for transfers between devices: 6.36 us -> 3.02 us  [on_device(): swap = lambda a: lax.ppermute(a, 'req', [(i, i ^ 1) for i in range(reqs)])]
    pallas_call x2, Pallas kernels: 25.3 us -> 23 us  [ffn(): pl.pallas_call(functools.partial(ffn_kernel, half), grid_spec=gs, out_sha...]
  transfers between devices with their start and end apart: 31 -> 29, of which waited for: 8 -> 7; matrix products, arithmetic and copies ran while one was open for 4% -> 3% of each run, Pallas kernels for 42% -> 45%
where the time goes in v2:
time: 167 us; the launch traced here: 166 us
  Pallas kernels  80.9 us (48%)
  starting transfers between devices  48 us (29%)
  waiting for transfers between devices  24.6 us (15%)
  local copies, waits for them, and re-layouts  8.4 us (5%)
  other arithmetic  3.27 us (2%)
    ppermute x20, starting transfers between devices, on_device(): lax.ppermute(a, 'tp', [(i, (i + d) % 4) for i in range(4)])  30 us
    pallas_call x2, Pallas kernels, ffn(): pl.pallas_call(functools.partial(ffn_kernel, half), grid_spec=gs, out_sha...  23 us
    ppermute x20, waiting for transfers between devices, on_device(): lax.ppermute(a, 'tp', [(i, (i + d) % 4) for i in range(4)])  18.4 us
    pallas_call x2, Pallas kernels, recall(): pl.pallas_call(functools.partial(recall_kernel, half), grid_spec=gs, out_...  14.9 us
    pallas_call x1, Pallas kernels, project(): pl.pallas_call(project_kernel, grid_spec=gs, out_shape=[jax.ShapeDtypeStr...  12.9 us
    pallas_call x2, Pallas kernels, attend(): pl.pallas_call(attend_kernel, grid=(heads,), in_specs=[pl.BlockSpec((SEG,...  12.6 us
    all_to_all x2, starting transfers between devices, on_device(): lax.all_to_all(a, 'req', 0, 0, tiled=True, axis_index_groups=g)  9.71 us
    pallas_call x3, Pallas kernels, join(): pl.pallas_call(functools.partial(join_kernel, spots), in_specs=[pl.BlockS...  8.42 us
  transfers between devices with their start and end apart: 29, of which 7 were waited for; matrix products, arithmetic and copies ran while one was open for 3% of the time, Pallas kernels for 45%

profile of v2, /device:TPU:32, one launch (start us, length us, event | category | flops | bytes accessed | tf_op | source)
XLA Modules:
  0.0 166.4 jit_solution(9060124477681677223)
XLA Ops:
  0.7 0.7 stack.23.place
  1.3 3.9 %cut_weights.1 = (bf16[592,1024]{1,0:T(8,128)(2,1)}, bf16[592,1024]{1,0:T(8,128)(2,1)}) custom-call(s32[5]{0:T(128)} %stack.23.place, bf16[704,1024]{1,0:T(8,128)(2,1)} %bitcast.10, bf16[704,1024]{1,0:T(8,128)(2,1)} %bitcast.13, bf16[704,1024]{1,0:T(8,128)(2,1)} %rest_6_.3, bf16[256,1024]{1,0:T(8,128)(2,1)} %rest_7_.3), custom_call_target="tpu_custom_call" | custom-call | tf_op jit(solution)/shard_map/cut_weights/pallas_call | solution.py:568
  5.2 3.1 %collective-permute-start.1 = (bf16[592,1024]{1,0:T(8,128)(2,1)}, bf16[592,1024]{1,0:T(8,128)(2,1)S(1)}, u32[]{:S(2)}, u32[]{:S(2)}) collective-permute-start(bf16[592,1024]{1,0:T(8,128)(2,1)} %get-tuple-element.83), channel_id=1, source_target_pairs={{0,3},{1,0},{2,1},{3,2},{4,7},{5,4},{6,5},{7,6},{8,11},{9,8},{10,9... | collective-permute-start | bytes 3637256 | tf_op jit(solution)/shard_map/ppermute | solution.py:587
  8.3 0.6 collective-permute-start
  8.9 2.7 %collective-permute-start.3 = (bf16[592,1024]{1,0:T(8,128)(2,1)}, bf16[592,1024]{1,0:T(8,128)(2,1)}, u32[]{:S(2)}, u32[]{:S(2)}) collective-permute-start(bf16[592,1024]{1,0:T(8,128)(2,1)} %get-tuple-element.82), channel_id=1, source_target_pairs={{0,3},{1,0},{2,1},{3,2},{4,7},{5,4},{6,5},{7,6},{8,11},{9,8},{10,9... | collective-permute-start | bytes 3637256 | tf_op jit(solution)/shard_map/ppermute | solution.py:587
  11.6 0.6 broadcast_in_dim.32.gain
  12.2 0.1 pad.2.clone
  12.3 0.7 maximum_maximum_fusion.row
  13.0 12.9 %project.1 = (bf16[2048,256]{1,0:T(8,128)(2,1)}, bf16[2048,512]{1,0:T(8,128)(2,1)}, bf16[2048,256]{1,0:T(8,128)(2,1)}, f32[8,2,128,128]{3,2,1,0:T(8,128)}, bf16[...) custom-call(s32[16]{0:T(128)} %owner.1, s32[16]{0:T(128)} %slot.1, ...), custom_call_target="tpu_custom_call" | custom-call | tf_op jit(solution)/shard_map/project/pallas_call | solution.py:185
  25.9 5.4 %all-to-all-start = ((bf16[8,264,128]{2,1,0:T(8,128)(2,1)}), bf16[8,264,128]{2,1,0:T(8,128)(2,1)S(1)}, u32[]{:S(2)}, u32[]{:S(2)}) async-start(bf16[8,264,128]{2,1,0:T(8,128)(2,1)} %get-tuple-element.71), calls=%async_computation | async-start | bytes 1081344 | tf_op jit(solution)/shard_map/all_to_all | solution.py:605
  31.3 6.3 %attend.2.at0 = f32[1024,256]{1,0:T(8,128)} custom-call(bf16[2048,256]{1,0:T(8,128)(2,1)} %get-tuple-element.77.q, bf16[2048,512]{1,0:T(8,128)(2,1)} %get-tuple-element.67.k.v.kv, bf16[2048,512]{1,0:T(8,128)(2,1)} %get-tuple-element.67.k.v.kv, bf16[16,256]{1,0:T(8,128)(2,1)} %pk.3, bf16[16,256]{1,0:T(8,128)(2,1)} %pv.3, f32[2048,8]{1,0:T(8,128)} %get-tuple-element.69.col, ...), custom_call_target="tpu_custom_call" | custom-call | flops 1400000000 | bytes 4000000 | tf_op jit(solution)/shard_map/attend/pallas_call | solution.py:270
  37.6 2.8 %all-to-all-done.got = bf16[8,264,128]{2,1,0:T(8,128)(2,1)S(1)} async-done(((bf16[8,264,128]{2,1,0:T(8,128)(2,1)}), bf16[8,264,128]{2,1,0:T(8,128)(2,1)S(1)}, u32[]{:S(2)}, u32[]{:S(2)}) %all-to-all-start) | async-done | bytes 540704 | tf_op jit(solution)/shard_map/all_to_all | solution.py:605
  40.4 0.8 copy-done.5
  41.2 2.0 %combine.1 = (f32[2,128,128]{2,1,0:T(8,128)}, f32[8,128]{1,0:T(8,128)}, bf16[4,264,128]{2,1,0:T(8,128)(2,1)}) custom-call(s32[5]{0:T(128)} %stack.23.place, bf16[8,264,128]{2,1,0:T(8,128)(2,1)} %copy-done.5), custom_call_target="tpu_custom_call" | custom-call | tf_op jit(solution)/shard_map/combine/pallas_call | solution.py:227
  43.2 4.3 %all-to-all-start.1 = ((bf16[4,264,128]{2,1,0:T(8,128)(2,1)}), bf16[4,264,128]{2,1,0:T(8,128)(2,1)S(1)}, u32[]{:S(2)}, u32[]{:S(2)}) async-start(bf16[4,264,128]{2,1,0:T(8,128)(2,1)} %get-tuple-element.76), calls=%async_computation.1 | async-start | bytes 540672 | tf_op jit(solution)/shard_map/all_to_all | solution.py:605
  47.5 6.3 %attend.3.at1 = f32[1024,256]{1,0:T(8,128)} custom-call(bf16[2048,256]{1,0:T(8,128)(2,1)} %get-tuple-element.77.q, bf16[2048,512]{1,0:T(8,128)(2,1)} %get-tuple-element.67.k.v.kv, bf16[2048,512]{1,0:T(8,128)(2,1)} %get-tuple-element.67.k.v.kv, bf16[16,256]{1,0:T(8,128)(2,1)} %pk.3, bf16[16,256]{1,0:T(8,128)(2,1)} %pv.3, f32[2048,8]{1,0:T(8,128)} %get-tuple-element.69.col, ...), custom_call_target="tpu_custom_call" | custom-call | flops 1400000000 | bytes 4000000 | tf_op jit(solution)/shard_map/attend/pallas_call | solution.py:270
  53.8 0.4 all-to-all-done.1.got
  54.2 0.7 copy-done.4
  54.9 6.7 %all-to-all-start.2 = ((bf16[32,136,512]{2,1,0:T(8,128)(2,1)}), bf16[32,136,512]{2,1,0:T(8,128)(2,1)}, u32[]{:S(2)}, u32[]{:S(2)}) async-start(bf16[32,136,512]{2,1,0:T(8,128)(2,1)} %get-tuple-element.120), calls=%async_computation.2 | async-start | bytes 8912896 | tf_op jit(solution)/shard_map/all_to_all | solution.py:615
  61.5 2.4 %collective-permute-done.rest_8_ = bf16[592,1024]{1,0:T(8,128)(2,1)} collective-permute-done((bf16[592,1024]{1,0:T(8,128)(2,1)}, bf16[592,1024]{1,0:T(8,128)(2,1)}, u32[]{:S(2)}, u32[]{:S(2)}) %collective-permute-start) | collective-permute-done | bytes 1212448 | tf_op jit(solution)/shard_map/ppermute | solution.py:587
  64.0 0.1 collective-permute-start.4
  64.1 0.5 collective-permute-start.5
  64.6 0.1 collective-permute-start.6
  64.7 0.4 collective-permute-start.7
  65.1 3.0 %collective-permute-done.4.rest_14_ = bf16[592,1024]{1,0:T(8,128)(2,1)} collective-permute-done((bf16[592,1024]{1,0:T(8,128)(2,1)}, bf16[592,1024]{1,0:T(8,128)(2,1)}, u32[]{:S(2)}, u32[]{:S(2)}) %collective-permute-start.4) | collective-permute-done | bytes 1212448 | tf_op jit(solution)/shard_map/ppermute | solution.py:588
  68.1 1.1 collective-permute-start.12
  69.1 0.1 slice.18
  69.2 0.7 pad_maximum_fusion.bound
  69.9 7.4 %recall.3 = (bf16[256,256]{1,0:T(8,128)(2,1)}, bf16[256,256]{1,0:T(8,128)(2,1)}, bf16[256,256]{1,0:T(8,128)(2,1)}, bf16[256,256]{1,0:T(8,128)(2,1)}) custom-call(s32[5]{0:T(128)} %stack.23.place, f32[8]{0:T(128)} %pad_maximum_fusion.bound, bf16[2048,256]{1,0:T(8,128)(2,1)} %get-tuple-element.77.q, bf16[2048,256]{1,0:T(8,128)(2,1)} %get-tuple-element.66.ku, ...), custom_call_target="tpu_custom_call" | custom-call | flops 400000000 | bytes 4000000 | tf_op jit(solution)/shard_map/recall/pallas_call | solution.py:372
  77.4 1.2 collective-permute-start.8
  78.6 2.3 %collective-permute-start.9 = (bf16[256,256]{1,0:T(8,128)(2,1)}, bf16[256,256]{1,0:T(8,128)(2,1)S(1)}, u32[]{:S(2)}, u32[]{:S(2)}) collective-permute-start(bf16[256,256]{1,0:T(8,128)(2,1)} %get-tuple-element.99), channel_id=1, source_target_pairs={{0,3},{1,0},{2,1},{3,2},{4,7},{5,4},{6,5},{7,6},{8,11},{9,8},{10,9... | collective-permute-start | bytes 393224 | tf_op jit(solution)/shard_map/ppermute | solution.py:587
  80.9 7.4 %recall.2 = (bf16[256,256]{1,0:T(8,128)(2,1)}, bf16[256,256]{1,0:T(8,128)(2,1)}, bf16[256,256]{1,0:T(8,128)(2,1)}, bf16[256,256]{1,0:T(8,128)(2,1)}) custom-call(s32[5]{0:T(128)} %stack.23.place, f32[8]{0:T(128)} %pad_maximum_fusion.bound, bf16[2048,256]{1,0:T(8,128)(2,1)} %get-tuple-element.77.q, bf16[2048,256]{1,0:T(8,128)(2,1)} %get-tuple-element.66.ku, ...), custom_call_target="tpu_custom_call" | custom-call | flops 400000000 | bytes 4000000 | tf_op jit(solution)/shard_map/recall/pallas_call | solution.py:372
  88.3 12.4 %collective-permute-done.8.rest_1_ = bf16[256,256]{1,0:T(8,128)(2,1)S(1)} collective-permute-done((bf16[256,256]{1,0:T(8,128)(2,1)}, bf16[256,256]{1,0:T(8,128)(2,1)S(1)}, u32[]{:S(2)}, u32[]{:S(2)}) %collective-permute-start.8) | collective-permute-done | bytes 131104 | tf_op jit(solution)/shard_map/ppermute | solution.py:587
  100.8 0.1 collective-permute-start.13
  100.9 0.5 collective-permute-start.14
  101.4 1.8 %collective-permute-start.15 = (bf16[256,256]{1,0:T(8,128)(2,1)}, bf16[256,256]{1,0:T(8,128)(2,1)S(1)}, u32[]{:S(2)}, u32[]{:S(2)}) collective-permute-start(bf16[256,256]{1,0:T(8,128)(2,1)} %get-tuple-element.112), channel_id=1, source_target_pairs={{0,1},{1,2},{2,3},{3,0},{4,5},{5,6},{6,7},{7,4},{8,9},{9,10},{10,1... | collective-permute-start | bytes 393224 | tf_op jit(solution)/shard_map/ppermute | solution.py:587
  103.2 2.5 %collective-permute-start.16 = (bf16[256,256]{1,0:T(8,128)(2,1)}, bf16[256,256]{1,0:T(8,128)(2,1)S(1)}, u32[]{:S(2)}, u32[]{:S(2)}) collective-permute-start(bf16[256,256]{1,0:T(8,128)(2,1)} %get-tuple-element.113), channel_id=1, source_target_pairs={{0,3},{1,0},{2,1},{3,2},{4,7},{5,4},{6,5},{7,6},{8,11},{9,8},{10,9... | collective-permute-start | bytes 393224 | tf_op jit(solution)/shard_map/ppermute | solution.py:587
  105.7 1.5 collective-permute-start.17
  107.2 0.6 broadcast_in_dim.31.gain
  107.8 1.0 copy-done.2
  108.8 1.0 copy-done.3
  109.8 11.5 %ffn.2.refs_0_ = bf16[256,1024]{1,0:T(8,128)(2,1)} custom-call(s32[5]{0:T(128)} %stack.23.place, bf16[1,1024]{1,0:T(2,128)(2,1)} %broadcast_in_dim.31.gain, bf16[2048,1024]{1,0:T(8,128)(2,1)} %tokens.3, bf16[256,256]{1,0:T(8,128)(2,1)} %get-tuple-element.101.rest_0_, bf16[256,256]{1,0:T(8,128)(2,1)} %copy-done.14, bf16[256,256]{1,0:T(8,128)(2,1)} %copy-done.15, ...), custom_call_target="tpu_custom_call" | custom-call | tf_op jit(solution)/shard_map/ffn/pallas_call | solution.py:481
  121.3 1.5 collective-permute-start.20
  122.8 1.8 %collective-permute-start.21 = (bf16[256,1024]{1,0:T(8,128)(2,1)}, bf16[256,1024]{1,0:T(8,128)(2,1)S(1)}, u32[]{:S(2)}, u32[]{:S(2)}) collective-permute-start(bf16[256,1024]{1,0:T(8,128)(2,1)} %ffn.2.refs_0_), channel_id=1, source_target_pairs={{0,3},{1,0},{2,1},{3,2},{4,7},{5,4},{6,5},{7,6},{8,11},{9,8},{10,9... | collective-permute-start | bytes 1572872 | tf_op jit(solution)/shard_map/ppermute | solution.py:587
  124.7 11.5 %ffn.3.refs_3_ = bf16[256,1024]{1,0:T(8,128)(2,1)} custom-call(s32[5]{0:T(128)} %stack.23.place, bf16[1,1024]{1,0:T(2,128)(2,1)} %broadcast_in_dim.31.gain, bf16[2048,1024]{1,0:T(8,128)(2,1)} %tokens.3, bf16[256,256]{1,0:T(8,128)(2,1)} %get-tuple-element.115.rest_0_, bf16[256,256]{1,0:T(8,128)(2,1)} %copy-done.17, bf16[256,256]{1,0:T(8,128)(2,1)} %copy-done.18, ...), custom_call_target="tpu_custom_call" | custom-call | tf_op jit(solution)/shard_map/ffn/pallas_call | solution.py:481
  136.2 0.3 collective-permute-start.18
  136.4 3.0 %collective-permute-start.19 = (bf16[256,1024]{1,0:T(8,128)(2,1)}, bf16[256,1024]{1,0:T(8,128)(2,1)S(1)}, u32[]{:S(2)}, u32[]{:S(2)}) collective-permute-start(bf16[256,1024]{1,0:T(8,128)(2,1)} %ffn.3.refs_3_), channel_id=1, source_target_pairs={{0,3},{1,0},{2,1},{3,2},{4,7},{5,4},{6,5},{7,6},{8,11},{9,8},{10,9... | collective-permute-start | bytes 1572872 | tf_op jit(solution)/shard_map/ppermute | solution.py:587
  139.5 0.1 collective-permute-start.24
  139.6 3.3 %collective-permute-start.25 = (bf16[128,1024]{1,0:T(8,128)(2,1)S(1)}, bf16[128,1024]{1,0:T(8,128)(2,1)S(1)}, u32[]{:S(2)}, u32[]{:S(2)}) collective-permute-start(bf16[128,1024]{1,0:T(8,128)(2,1)S(1)} %slice.26), channel_id=1, source_target_pairs={{0,3},{1,0},{2,1},{3,2},{4,7},{5,4},{6,5},{7,6},{8,11},{9,8},{10,9... | collective-permute-start | bytes 786440 | tf_op jit(solution)/shard_map/ppermute | solution.py:587
  142.9 3.1 %join.3.refs_4_ = bf16[2048,1024]{1,0:T(8,128)(2,1)} custom-call(s32[5]{0:T(128)} %stack.23.place, bf16[256,1024]{1,0:T(8,128)(2,1)} %ffn.2.refs_0_, bf16[256,1024]{1,0:T(8,128)(2,1)} %copy-done.8, bf16[256,1024]{1,0:T(8,128)(2,1)} %copy-done.9, bf16[256,1024]{1,0:T(8,128)(2,1)} %ffn.3.refs_3_), custom_call_target="tpu_custom_call" | custom-call | tf_op jit(solution)/shard_map/join/pallas_call | solution.py:538
  146.0 1.2 fusion
  147.2 0.2 select_reduce_fusion
  147.4 0.5 broadcast_clamp_fusion.source
  147.9 3.2 %place.1 = bf16[16,128,512]{2,1,0:T(8,128)(2,1)} custom-call(s32[16]{0:T(128)} %broadcast_clamp_fusion.source, bf16[32,136,512]{2,1,0:T(8,128)(2,1)} %all-to-all-done.2.got), custom_call_target="tpu_custom_call" | custom-call | tf_op jit(solution)/shard_map/place/pallas_call | solution.py:515
  151.2 1.4 collective-permute-done.18.refs_0_
  152.5 0.1 collective-permute-start.22
  152.7 3.3 %collective-permute-start.23 = (bf16[128,1024]{1,0:T(8,128)(2,1)S(1)}, bf16[128,1024]{1,0:T(8,128)(2,1)S(1)}, u32[]{:S(2)}, u32[]{:S(2)}) collective-permute-start(bf16[128,1024]{1,0:T(8,128)(2,1)S(1)} %slice.21), channel_id=1, source_target_pairs={{0,3},{1,0},{2,1},{3,2},{4,7},{5,4},{6,5},{7,6},{8,11},{9,8},{10,9... | collective-permute-start | bytes 786440 | tf_op jit(solution)/shard_map/ppermute | solution.py:587
  155.9 2.2 %collective-permute-done.24.refs_2_ = bf16[128,1024]{1,0:T(8,128)(2,1)S(1)} collective-permute-done((bf16[128,1024]{1,0:T(8,128)(2,1)S(1)}, bf16[128,1024]{1,0:T(8,128)(2,1)S(1)}, u32[]{:S(2)}, u32[]{:S(2)}) %collective-permute-start.24) | collective-permute-done | bytes 262176 | tf_op jit(solution)/shard_map/ppermute | solution.py:587
  158.2 0.7 copy-done.10
  158.8 0.7 copy-done.11
  159.5 2.9 %join.4.refs_2_ = bf16[2048,1024]{1,0:T(8,128)(2,1)} custom-call(s32[5]{0:T(128)} %stack.23.place, bf16[256,1024]{1,0:T(8,128)(2,1)} %copy-done.6, bf16[256,1024]{1,0:T(8,128)(2,1)} %copy-done.7, bf16[128,1024]{1,0:T(8,128)(2,1)} %copy-done.10, bf16[128,1024]{1,0:T(8,128)(2,1)} %copy-done.11, ...), custom_call_target="tpu_custom_call", output_to_operand_aliasing={{}: (5, {})} | custom-call | tf_op jit(solution)/shard_map/join/pallas_call | solution.py:538
  162.5 0.7 copy-done.12
  163.1 0.7 copy-done.13
  163.8 2.4 %join.5 = bf16[2048,1024]{1,0:T(8,128)(2,1)} custom-call(s32[5]{0:T(128)} %stack.23.place, bf16[128,1024]{1,0:T(8,128)(2,1)} %copy-done.12, bf16[128,1024]{1,0:T(8,128)(2,1)} %copy-done.13, bf16[2048,1024]{1,0:T(8,128)(2,1)} %join.4.refs_2_), custom_call_target="tpu_custom_call", output_to_operand_aliasing={{}: (3, {})} | custom-call | tf_op jit(solution)/shard_map/join/pallas_call | solution.py:538
  (72 shorter events, 0.2 us)
Async XLA Ops:
  1.3 10.2 %copy-start.21 = (s32[2048]{0:T(1024)S(1)}, s32[2048]{0:T(1024)}, u32[]{:S(2)}) copy-start(s32[2048]{0:T(1024)} %param.31) | copy-start | bytes 24580
  1.3 10.2 %copy-start.22 = (bf16[1024]{0:T(1024)(128)(2,1)S(1)}, bf16[1024]{0:T(1024)(128)(2,1)}, u32[]{:S(2)}) copy-start(bf16[1024]{0:T(1024)(128)(2,1)} %param.18) | copy-start | bytes 6148
  1.3 10.9 %copy-start.20 = (f32[2048,2]{0,1:T(2,128)S(1)}, f32[2048,2]{0,1:T(2,128)}, u32[]{:S(2)}) copy-start(f32[2048,2]{0,1:T(2,128)} %param.24) | copy-start | bytes 49156
  5.2 58.7 %collective-permute-start.1 = (bf16[592,1024]{1,0:T(8,128)(2,1)}, bf16[592,1024]{1,0:T(8,128)(2,1)S(1)}, u32[]{:S(2)}, u32[]{:S(2)}) collective-permute-start(bf16[592,1024]{1,0:T(8,128)(2,1)} %get-tuple-element.83), channel_id=1, source_target_pairs={{0,3},{1,0},{2,1},{3,2},{4,7},{5,4},{6,5},{7,6},{8,11},{9,8},{10,9... | collective-permute-start | bytes 3637256 | tf_op jit(solution)/shard_map/ppermute | solution.py:587
  8.3 55.6 %collective-permute-start.2 = (bf16[592,1024]{1,0:T(8,128)(2,1)}, bf16[592,1024]{1,0:T(8,128)(2,1)S(1)}, u32[]{:S(2)}, u32[]{:S(2)}) collective-permute-start(bf16[592,1024]{1,0:T(8,128)(2,1)} %get-tuple-element.83), channel_id=1, source_target_pairs={{0,1},{1,2},{2,3},{3,0},{4,5},{5,6},{6,7},{7,4},{8,9},{9,10},{10,1... | collective-permute-start | bytes 3637256 | tf_op jit(solution)/shard_map/ppermute | solution.py:587
  8.3 55.6 %collective-permute-start = (bf16[592,1024]{1,0:T(8,128)(2,1)}, bf16[592,1024]{1,0:T(8,128)(2,1)}, u32[]{:S(2)}, u32[]{:S(2)}) collective-permute-start(bf16[592,1024]{1,0:T(8,128)(2,1)} %get-tuple-element.82), channel_id=1, source_target_pairs={{0,1},{1,2},{2,3},{3,0},{4,5},{5,6},{6,7},{7,4},{8,9},{9,10},{10,1... | collective-permute-start | bytes 3637256 | tf_op jit(solution)/shard_map/ppermute | solution.py:587
  8.9 55.1 %collective-permute-start.3 = (bf16[592,1024]{1,0:T(8,128)(2,1)}, bf16[592,1024]{1,0:T(8,128)(2,1)}, u32[]{:S(2)}, u32[]{:S(2)}) collective-permute-start(bf16[592,1024]{1,0:T(8,128)(2,1)} %get-tuple-element.82), channel_id=1, source_target_pairs={{0,3},{1,0},{2,1},{3,2},{4,7},{5,4},{6,5},{7,6},{8,11},{9,8},{10,9... | collective-permute-start | bytes 3637256 | tf_op jit(solution)/shard_map/ppermute | solution.py:587
  25.9 14.5 %all-to-all-start = ((bf16[8,264,128]{2,1,0:T(8,128)(2,1)}), bf16[8,264,128]{2,1,0:T(8,128)(2,1)S(1)}, u32[]{:S(2)}, u32[]{:S(2)}) async-start(bf16[8,264,128]{2,1,0:T(8,128)(2,1)} %get-tuple-element.71), calls=%async_computation | async-start | bytes 1081344 | tf_op jit(solution)/shard_map/all_to_all | solution.py:605
  40.4 0.8 copy-start.5
  43.2 11.0 %all-to-all-start.1 = ((bf16[4,264,128]{2,1,0:T(8,128)(2,1)}), bf16[4,264,128]{2,1,0:T(8,128)(2,1)S(1)}, u32[]{:S(2)}, u32[]{:S(2)}) async-start(bf16[4,264,128]{2,1,0:T(8,128)(2,1)} %get-tuple-element.76), calls=%async_computation.1 | async-start | bytes 540672 | tf_op jit(solution)/shard_map/all_to_all | solution.py:605
  54.2 0.7 copy-start.4
  54.9 91.1 %all-to-all-start.2 = ((bf16[32,136,512]{2,1,0:T(8,128)(2,1)}), bf16[32,136,512]{2,1,0:T(8,128)(2,1)}, u32[]{:S(2)}, u32[]{:S(2)}) async-start(bf16[32,136,512]{2,1,0:T(8,128)(2,1)} %get-tuple-element.120), calls=%async_computation.2 | async-start | bytes 8912896 | tf_op jit(solution)/shard_map/all_to_all | solution.py:615
  63.9 13.4 %copy-start = (bf16[592,1024]{1,0:T(8,128)(2,1)}, bf16[592,1024]{1,0:T(8,128)(2,1)S(1)}, u32[]{:S(2)}) copy-start(bf16[592,1024]{1,0:T(8,128)(2,1)S(1)} %collective-permute-done.1.rest_11_) | copy-start | bytes 3637252
  64.0 13.4 %copy-start.1 = (bf16[592,1024]{1,0:T(8,128)(2,1)}, bf16[592,1024]{1,0:T(8,128)(2,1)S(1)}, u32[]{:S(2)}) copy-start(bf16[592,1024]{1,0:T(8,128)(2,1)S(1)} %collective-permute-done.2.rest_9_) | copy-start | bytes 3637252
  64.0 4.1 %collective-permute-start.4 = (bf16[592,1024]{1,0:T(8,128)(2,1)}, bf16[592,1024]{1,0:T(8,128)(2,1)}, u32[]{:S(2)}, u32[]{:S(2)}) collective-permute-start(bf16[592,1024]{1,0:T(8,128)(2,1)} %collective-permute-done.rest_8_), channel_id=1, source_target_pairs={{0,4},{4,0},{8,12},{12,8},{16,20},{20,16},{24,28},{28,24},{32,36},... | collective-permute-start | bytes 3637256 | tf_op jit(solution)/shard_map/ppermute | solution.py:588
  64.1 13.3 %collective-permute-start.5 = (bf16[592,1024]{1,0:T(8,128)(2,1)S(1)}, bf16[592,1024]{1,0:T(8,128)(2,1)}, u32[]{:S(2)}, u32[]{:S(2)}) collective-permute-start(bf16[592,1024]{1,0:T(8,128)(2,1)S(1)} %collective-permute-done.1.rest_11_), channel_id=1, source_target_pairs={{0,4},{4,0},{8,12},{12,8},{16,20},{20,16},{24,28},{28,24},{32,36},... | collective-permute-start | bytes 3637256 | tf_op jit(solution)/shard_map/ppermute | solution.py:588
  64.6 12.8 %collective-permute-start.6 = (bf16[592,1024]{1,0:T(8,128)(2,1)S(1)}, bf16[592,1024]{1,0:T(8,128)(2,1)}, u32[]{:S(2)}, u32[]{:S(2)}) collective-permute-start(bf16[592,1024]{1,0:T(8,128)(2,1)S(1)} %collective-permute-done.2.rest_9_), channel_id=1, source_target_pairs={{0,4},{4,0},{8,12},{12,8},{16,20},{20,16},{24,28},{28,24},{32,36},... | collective-permute-start | bytes 3637256 | tf_op jit(solution)/shard_map/ppermute | solution.py:588
  64.7 12.7 %collective-permute-start.7 = (bf16[592,1024]{1,0:T(8,128)(2,1)}, bf16[592,1024]{1,0:T(8,128)(2,1)}, u32[]{:S(2)}, u32[]{:S(2)}) collective-permute-start(bf16[592,1024]{1,0:T(8,128)(2,1)} %collective-permute-done.3.rest_10_), channel_id=1, source_target_pairs={{0,4},{4,0},{8,12},{12,8},{16,20},{20,16},{24,28},{28,24},{32,36},... | collective-permute-start | bytes 3637256 | tf_op jit(solution)/shard_map/ppermute | solution.py:588
  65.1 35.7 %collective-permute-start.11 = (bf16[592,1024]{1,0:T(8,128)(2,1)}, bf16[592,1024]{1,0:T(8,128)(2,1)}, u32[]{:S(2)}, u32[]{:S(2)}) collective-permute-start(bf16[592,1024]{1,0:T(8,128)(2,1)} %collective-permute-done.rest_8_), channel_id=1, source_target_pairs={{0,1},{1,2},{2,3},{3,0},{4,5},{5,6},{6,7},{7,4},{8,9},{9,10},{10,1... | collective-permute-start | bytes 3637256 | tf_op jit(solution)/shard_map/ppermute | solution.py:587
  68.1 32.7 %collective-permute-start.12 = (bf16[592,1024]{1,0:T(8,128)(2,1)S(1)}, bf16[592,1024]{1,0:T(8,128)(2,1)}, u32[]{:S(2)}, u32[]{:S(2)}) collective-permute-start(bf16[592,1024]{1,0:T(8,128)(2,1)S(1)} %collective-permute-done.1.rest_11_), channel_id=1, source_target_pairs={{0,3},{1,0},{2,1},{3,2},{4,7},{5,4},{6,5},{7,6},{8,11},{9,8},{10,9... | collective-permute-start | bytes 3637256 | tf_op jit(solution)/shard_map/ppermute | solution.py:587
  77.4 29.8 %copy-start.23 = (bf16[1024]{0:T(1024)(128)(2,1)S(1)}, bf16[1024]{0:T(1024)(128)(2,1)}, u32[]{:S(2)}) copy-start(bf16[1024]{0:T(1024)(128)(2,1)} %param.27) | copy-start | bytes 6148
  77.4 23.4 %collective-permute-start.8 = (bf16[256,256]{1,0:T(8,128)(2,1)}, bf16[256,256]{1,0:T(8,128)(2,1)S(1)}, u32[]{:S(2)}, u32[]{:S(2)}) collective-permute-start(bf16[256,256]{1,0:T(8,128)(2,1)} %get-tuple-element.98), channel_id=1, source_target_pairs={{0,1},{1,2},{2,3},{3,0},{4,5},{5,6},{6,7},{7,4},{8,9},{9,10},{10,1... | collective-permute-start | bytes 393224 | tf_op jit(solution)/shard_map/ppermute | solution.py:587
  78.6 22.2 %collective-permute-start.9 = (bf16[256,256]{1,0:T(8,128)(2,1)}, bf16[256,256]{1,0:T(8,128)(2,1)S(1)}, u32[]{:S(2)}, u32[]{:S(2)}) collective-permute-start(bf16[256,256]{1,0:T(8,128)(2,1)} %get-tuple-element.99), channel_id=1, source_target_pairs={{0,3},{1,0},{2,1},{3,2},{4,7},{5,4},{6,5},{7,6},{8,11},{9,8},{10,9... | collective-permute-start | bytes 393224 | tf_op jit(solution)/shard_map/ppermute | solution.py:587
  80.9 19.9 %collective-permute-start.10 = (bf16[256,256]{1,0:T(8,128)(2,1)}, bf16[256,256]{1,0:T(8,128)(2,1)S(1)}, u32[]{:S(2)}, u32[]{:S(2)}) collective-permute-start(bf16[256,256]{1,0:T(8,128)(2,1)} %get-tuple-element.100), channel_id=1, source_target_pairs={{0,2},{1,3},{2,0},{3,1},{4,6},{5,7},{6,4},{7,5},{8,10},{9,11},{10,... | collective-permute-start | bytes 393224 | tf_op jit(solution)/shard_map/ppermute | solution.py:587
  100.8 7.0 %copy-start.14 = (bf16[256,256]{1,0:T(8,128)(2,1)}, bf16[256,256]{1,0:T(8,128)(2,1)S(1)}, u32[]{:S(2)}) copy-start(bf16[256,256]{1,0:T(8,128)(2,1)S(1)} %collective-permute-done.8.rest_1_) | copy-start | bytes 393220
  100.8 7.0 %copy-start.15 = (bf16[256,256]{1,0:T(8,128)(2,1)}, bf16[256,256]{1,0:T(8,128)(2,1)S(1)}, u32[]{:S(2)}) copy-start(bf16[256,256]{1,0:T(8,128)(2,1)S(1)} %collective-permute-done.9.rest_2_) | copy-start | bytes 393220
  100.8 7.0 %copy-start.16 = (bf16[256,256]{1,0:T(8,128)(2,1)}, bf16[256,256]{1,0:T(8,128)(2,1)S(1)}, u32[]{:S(2)}) copy-start(bf16[256,256]{1,0:T(8,128)(2,1)S(1)} %collective-permute-done.10.rest_3_) | copy-start | bytes 393220
  100.8 6.9 %collective-permute-start.13 = (bf16[592,1024]{1,0:T(8,128)(2,1)}, bf16[592,1024]{1,0:T(8,128)(2,1)S(1)}, u32[]{:S(2)}, u32[]{:S(2)}) collective-permute-start(bf16[592,1024]{1,0:T(8,128)(2,1)} %collective-permute-done.11.rest_12_), channel_id=1, source_target_pairs={{0,4},{4,0},{8,12},{12,8},{16,20},{20,16},{24,28},{28,24},{32,36},... | collective-permute-start | bytes 3637256 | tf_op jit(solution)/shard_map/ppermute | solution.py:588
  100.9 6.8 %collective-permute-start.14 = (bf16[592,1024]{1,0:T(8,128)(2,1)}, bf16[592,1024]{1,0:T(8,128)(2,1)S(1)}, u32[]{:S(2)}, u32[]{:S(2)}) collective-permute-start(bf16[592,1024]{1,0:T(8,128)(2,1)} %collective-permute-done.12.rest_13_), channel_id=1, source_target_pairs={{0,4},{4,0},{8,12},{12,8},{16,20},{20,16},{24,28},{28,24},{32,36},... | collective-permute-start | bytes 3637256 | tf_op jit(solution)/shard_map/ppermute | solution.py:588
  101.4 19.9 %collective-permute-start.15 = (bf16[256,256]{1,0:T(8,128)(2,1)}, bf16[256,256]{1,0:T(8,128)(2,1)S(1)}, u32[]{:S(2)}, u32[]{:S(2)}) collective-permute-start(bf16[256,256]{1,0:T(8,128)(2,1)} %get-tuple-element.112), channel_id=1, source_target_pairs={{0,1},{1,2},{2,3},{3,0},{4,5},{5,6},{6,7},{7,4},{8,9},{9,10},{10,1... | collective-permute-start | bytes 393224 | tf_op jit(solution)/shard_map/ppermute | solution.py:587
  103.2 18.1 %collective-permute-start.16 = (bf16[256,256]{1,0:T(8,128)(2,1)}, bf16[256,256]{1,0:T(8,128)(2,1)S(1)}, u32[]{:S(2)}, u32[]{:S(2)}) collective-permute-start(bf16[256,256]{1,0:T(8,128)(2,1)} %get-tuple-element.113), channel_id=1, source_target_pairs={{0,3},{1,0},{2,1},{3,2},{4,7},{5,4},{6,5},{7,6},{8,11},{9,8},{10,9... | collective-permute-start | bytes 393224 | tf_op jit(solution)/shard_map/ppermute | solution.py:587
  105.7 15.6 %collective-permute-start.17 = (bf16[256,256]{1,0:T(8,128)(2,1)}, bf16[256,256]{1,0:T(8,128)(2,1)S(1)}, u32[]{:S(2)}, u32[]{:S(2)}) collective-permute-start(bf16[256,256]{1,0:T(8,128)(2,1)} %get-tuple-element.114), channel_id=1, source_target_pairs={{0,2},{1,3},{2,0},{3,1},{4,6},{5,7},{6,4},{7,5},{8,10},{9,11},{10,... | collective-permute-start | bytes 393224 | tf_op jit(solution)/shard_map/ppermute | solution.py:587
  107.8 1.0 copy-start.2
  108.8 1.0 copy-start.3
  121.3 3.4 %copy-start.17 = (bf16[256,256]{1,0:T(8,128)(2,1)}, bf16[256,256]{1,0:T(8,128)(2,1)S(1)}, u32[]{:S(2)}) copy-start(bf16[256,256]{1,0:T(8,128)(2,1)S(1)} %collective-permute-done.15.rest_1_) | copy-start | bytes 393220
  121.3 3.3 %copy-start.18 = (bf16[256,256]{1,0:T(8,128)(2,1)}, bf16[256,256]{1,0:T(8,128)(2,1)S(1)}, u32[]{:S(2)}) copy-start(bf16[256,256]{1,0:T(8,128)(2,1)S(1)} %collective-permute-done.16.rest_2_) | copy-start | bytes 393220
  121.3 3.3 %copy-start.19 = (bf16[256,256]{1,0:T(8,128)(2,1)}, bf16[256,256]{1,0:T(8,128)(2,1)S(1)}, u32[]{:S(2)}) copy-start(bf16[256,256]{1,0:T(8,128)(2,1)S(1)} %collective-permute-done.17.rest_3_) | copy-start | bytes 393220
  121.3 18.1 %collective-permute-start.20 = (bf16[256,1024]{1,0:T(8,128)(2,1)}, bf16[256,1024]{1,0:T(8,128)(2,1)S(1)}, u32[]{:S(2)}, u32[]{:S(2)}) collective-permute-start(bf16[256,1024]{1,0:T(8,128)(2,1)} %ffn.2.refs_0_), channel_id=1, source_target_pairs={{0,1},{1,2},{2,3},{3,0},{4,5},{5,6},{6,7},{7,4},{8,9},{9,10},{10,1... | collective-permute-start | bytes 1572872 | tf_op jit(solution)/shard_map/ppermute | solution.py:587
  122.8 16.8 %collective-permute-start.21 = (bf16[256,1024]{1,0:T(8,128)(2,1)}, bf16[256,1024]{1,0:T(8,128)(2,1)S(1)}, u32[]{:S(2)}, u32[]{:S(2)}) collective-permute-start(bf16[256,1024]{1,0:T(8,128)(2,1)} %ffn.2.refs_0_), channel_id=1, source_target_pairs={{0,3},{1,0},{2,1},{3,2},{4,7},{5,4},{6,5},{7,6},{8,11},{9,8},{10,9... | collective-permute-start | bytes 1572872 | tf_op jit(solution)/shard_map/ppermute | solution.py:587
  136.2 16.4 %collective-permute-start.18 = (bf16[256,1024]{1,0:T(8,128)(2,1)}, bf16[256,1024]{1,0:T(8,128)(2,1)S(1)}, u32[]{:S(2)}, u32[]{:S(2)}) collective-permute-start(bf16[256,1024]{1,0:T(8,128)(2,1)} %ffn.3.refs_3_), channel_id=1, source_target_pairs={{0,1},{1,2},{2,3},{3,0},{4,5},{5,6},{6,7},{7,4},{8,9},{9,10},{10,1... | collective-permute-start | bytes 1572872 | tf_op jit(solution)/shard_map/ppermute | solution.py:587
  136.4 16.1 %collective-permute-start.19 = (bf16[256,1024]{1,0:T(8,128)(2,1)}, bf16[256,1024]{1,0:T(8,128)(2,1)S(1)}, u32[]{:S(2)}, u32[]{:S(2)}) collective-permute-start(bf16[256,1024]{1,0:T(8,128)(2,1)} %ffn.3.refs_3_), channel_id=1, source_target_pairs={{0,3},{1,0},{2,1},{3,2},{4,7},{5,4},{6,5},{7,6},{8,11},{9,8},{10,9... | collective-permute-start | bytes 1572872 | tf_op jit(solution)/shard_map/ppermute | solution.py:587
  139.5 3.4 %copy-start.8 = (bf16[256,1024]{1,0:T(8,128)(2,1)}, bf16[256,1024]{1,0:T(8,128)(2,1)S(1)}, u32[]{:S(2)}) copy-start(bf16[256,1024]{1,0:T(8,128)(2,1)S(1)} %collective-permute-done.20.refs_1_) | copy-start | bytes 1572868
  139.5 18.6 %collective-permute-start.24 = (bf16[128,1024]{1,0:T(8,128)(2,1)S(1)}, bf16[128,1024]{1,0:T(8,128)(2,1)S(1)}, u32[]{:S(2)}, u32[]{:S(2)}) collective-permute-start(bf16[128,1024]{1,0:T(8,128)(2,1)S(1)} %slice.25), channel_id=1, source_target_pairs={{0,1},{1,2},{2,3},{3,0},{4,5},{5,6},{6,7},{7,4},{8,9},{9,10},{10,1... | collective-permute-start | bytes 786440 | tf_op jit(solution)/shard_map/ppermute | solution.py:587
  139.6 3.3 %copy-start.9 = (bf16[256,1024]{1,0:T(8,128)(2,1)}, bf16[256,1024]{1,0:T(8,128)(2,1)S(1)}, u32[]{:S(2)}) copy-start(bf16[256,1024]{1,0:T(8,128)(2,1)S(1)} %collective-permute-done.21.refs_2_) | copy-start | bytes 1572868
  139.6 18.5 %collective-permute-start.25 = (bf16[128,1024]{1,0:T(8,128)(2,1)S(1)}, bf16[128,1024]{1,0:T(8,128)(2,1)S(1)}, u32[]{:S(2)}, u32[]{:S(2)}) collective-permute-start(bf16[128,1024]{1,0:T(8,128)(2,1)S(1)} %slice.26), channel_id=1, source_target_pairs={{0,3},{1,0},{2,1},{3,2},{4,7},{5,4},{6,5},{7,6},{8,11},{9,8},{10,9... | collective-permute-start | bytes 786440 | tf_op jit(solution)/shard_map/ppermute | solution.py:587
  152.5 5.6 %copy-start.6 = (bf16[256,1024]{1,0:T(8,128)(2,1)}, bf16[256,1024]{1,0:T(8,128)(2,1)S(1)}, u32[]{:S(2)}) copy-start(bf16[256,1024]{1,0:T(8,128)(2,1)S(1)} %collective-permute-done.18.refs_0_) | copy-start | bytes 1572868
  152.5 5.6 %copy-start.7 = (bf16[256,1024]{1,0:T(8,128)(2,1)}, bf16[256,1024]{1,0:T(8,128)(2,1)S(1)}, u32[]{:S(2)}) copy-start(bf16[256,1024]{1,0:T(8,128)(2,1)S(1)} %collective-permute-done.19.refs_1_) | copy-start | bytes 1572868
  152.5 9.9 %collective-permute-start.22 = (bf16[128,1024]{1,0:T(8,128)(2,1)S(1)}, bf16[128,1024]{1,0:T(8,128)(2,1)S(1)}, u32[]{:S(2)}, u32[]{:S(2)}) collective-permute-start(bf16[128,1024]{1,0:T(8,128)(2,1)S(1)} %slice.20), channel_id=1, source_target_pairs={{0,1},{1,2},{2,3},{3,0},{4,5},{5,6},{6,7},{7,4},{8,9},{9,10},{10,1... | collective-permute-start | bytes 786440 | tf_op jit(solution)/shard_map/ppermute | solution.py:587
  152.7 9.8 %collective-permute-start.23 = (bf16[128,1024]{1,0:T(8,128)(2,1)S(1)}, bf16[128,1024]{1,0:T(8,128)(2,1)S(1)}, u32[]{:S(2)}, u32[]{:S(2)}) collective-permute-start(bf16[128,1024]{1,0:T(8,128)(2,1)S(1)} %slice.21), channel_id=1, source_target_pairs={{0,3},{1,0},{2,1},{3,2},{4,7},{5,4},{6,5},{7,6},{8,11},{9,8},{10,9... | collective-permute-start | bytes 786440 | tf_op jit(solution)/shard_map/ppermute | solution.py:587
  158.1 0.7 copy-start.10
  158.8 0.7 copy-start.11
  162.4 0.7 copy-start.12
  163.1 0.7 copy-start.13

commit v3 on v2

--- a/solution.py
+++ b/solution.py
@@ -606,7 +606,7 @@
     got8 = spread(pay, group8)
 
     at0 = attend(q, kv, persist_key, persist_value, col, row, 0)
-    at0, got8 = tie(at0, got8)
+    at0, got8, bound, ffn_gain = tie(at0, got8, bound, ffn_gain[None])
     e1, info, pay4 = combine(place, got8)
     got4 = spread(pay4, group4)
     q1, at0, _ = tie(q, at0, pay4)
@@ -627,9 +627,9 @@
     heads0 = send(out0)
     out1 = mem(1)
     tied = tie(*out1, *heads0)
+    p2, q2, _ = tie(p2, q2, tied[0])
     out1, heads0 = tied[:4], tied[4:]
     heads1 = send(out1)
-    p2, q2, _ = tie(p2, q2, out1[0])
     p2x, q2x = swap(p2), swap(q2)
     mine, other = [p1, q1w, p3, q3, p2, q2], [p1x, q1x, p3x, q3x, p2x, q2x]
 
@@ -639,7 +639,7 @@
     kv_cache = place_pages(jnp.clip(source, 0, reqs - 1), arrived, count // PAGE)
 
     feed = lambda half, heads: ffn(
-        half, place, tokens, ffn_gain[None], heads, own_w, mine, other
+        half, place, tokens, ffn_gain, heads, own_w, mine, other
     )
     R, H = ROWS, ROWS // 2
     own0 = feed(0, heads0)
@@ -653,7 +653,9 @@
     lo1, hi1 = shift(a1[:H], 1), shift(b1[H:], -1)
     joined = join(place, [a1, b1, lo0, hi0], ((3, R, R), (1, R, R), (2, 0, H), (2, H, H)), joined)
     lo1, hi1, joined = tie(lo1, hi1, joined)
-    layer_out = join(place, [lo1, hi1], ((2, R, H), (2, R + H, H)), joined)
+    at = (y + 2) % 4 * (2 * R) + R
+    layer_out = lax.dynamic_update_slice(joined, lo1, (at, 0))
+    layer_out = lax.dynamic_update_slice(layer_out, hi1, (at + H, 0))
     return layer_out, kv_cache
 
 

time: 167 us -> 164 us (0.982)
  Pallas kernels: 80.9 us -> 78.6 us
    pallas_call x3 -> x2, Pallas kernels: 8.42 us -> 5.99 us  [join(): pl.pallas_call(functools.partial(join_kernel, spots), in_specs=[pl.BlockS...]
    unnamed x48 -> x44, local copies, waits for them, and re-layouts: 6.32 us -> 4.97 us
  transfers between devices with their start and end apart: 29 -> 29, of which waited for: 7 -> 7; matrix products, arithmetic and copies ran while one was open for 3% -> 3% of each run, Pallas kernels for 45% -> 46%
where the time goes in v3:
time: 164 us; the launch traced here: 163 us
  Pallas kernels  78.6 us (48%)
  starting transfers between devices  48 us (29%)
  waiting for transfers between devices  23.9 us (15%)
  local copies, waits for them, and re-layouts  8.5 us (5%)
  other arithmetic  3.22 us (2%)
    ppermute x20, starting transfers between devices, on_device(): lax.ppermute(a, 'tp', [(i, (i + d) % 4) for i in range(4)])  30 us
    pallas_call x2, Pallas kernels, ffn(): pl.pallas_call(functools.partial(ffn_kernel, half), grid_spec=gs, out_sha...  23 us
    ppermute x20, waiting for transfers between devices, on_device(): lax.ppermute(a, 'tp', [(i, (i + d) % 4) for i in range(4)])  19.1 us
    pallas_call x2, Pallas kernels, recall(): pl.pallas_call(functools.partial(recall_kernel, half), grid_spec=gs, out_...  14.9 us
    pallas_call x1, Pallas kernels, project(): pl.pallas_call(project_kernel, grid_spec=gs, out_shape=[jax.ShapeDtypeStr...  13 us
    pallas_call x2, Pallas kernels, attend(): pl.pallas_call(attend_kernel, grid=(heads,), in_specs=[pl.BlockSpec((SEG,...  12.6 us
    all_to_all x2, starting transfers between devices, on_device(): lax.all_to_all(a, 'req', 0, 0, tiled=True, axis_index_groups=g)  9.76 us
    all_to_all x1, starting transfers between devices, on_device(): arrived = lax.all_to_all(outgoing, 'req', 0, 0, tiled=True)  6.63 us
  transfers between devices with their start and end apart: 29, of which 7 were waited for; matrix products, arithmetic and copies ran while one was open for 3% of the time, Pallas kernels for 46%

profile of v3, /device:TPU:32, one launch (start us, length us, event | category | flops | bytes accessed | tf_op | source)
XLA Modules:
  0.0 163.3 jit_solution(6714866985274920418)
XLA Ops:
  0.7 0.7 stack.23.place
  1.3 3.9 %cut_weights.1 = (bf16[592,1024]{1,0:T(8,128)(2,1)}, bf16[592,1024]{1,0:T(8,128)(2,1)}) custom-call(s32[5]{0:T(128)} %stack.23.place, bf16[704,1024]{1,0:T(8,128)(2,1)} %bitcast.10, bf16[704,1024]{1,0:T(8,128)(2,1)} %bitcast.13, bf16[704,1024]{1,0:T(8,128)(2,1)} %rest_6_.3, bf16[256,1024]{1,0:T(8,128)(2,1)} %rest_7_.3), custom_call_target="tpu_custom_call" | custom-call | tf_op jit(solution)/shard_map/cut_weights/pallas_call | solution.py:568
  5.2 3.1 %collective-permute-start.1 = (bf16[592,1024]{1,0:T(8,128)(2,1)}, bf16[592,1024]{1,0:T(8,128)(2,1)S(1)}, u32[]{:S(2)}, u32[]{:S(2)}) collective-permute-start(bf16[592,1024]{1,0:T(8,128)(2,1)} %get-tuple-element.87), channel_id=1, source_target_pairs={{0,3},{1,0},{2,1},{3,2},{4,7},{5,4},{6,5},{7,6},{8,11},{9,8},{10,9... | collective-permute-start | bytes 3637256 | tf_op jit(solution)/shard_map/ppermute | solution.py:587
  8.3 0.6 collective-permute-start
  8.9 2.7 %collective-permute-start.3 = (bf16[592,1024]{1,0:T(8,128)(2,1)}, bf16[592,1024]{1,0:T(8,128)(2,1)}, u32[]{:S(2)}, u32[]{:S(2)}) collective-permute-start(bf16[592,1024]{1,0:T(8,128)(2,1)} %get-tuple-element.86), channel_id=1, source_target_pairs={{0,3},{1,0},{2,1},{3,2},{4,7},{5,4},{6,5},{7,6},{8,11},{9,8},{10,9... | collective-permute-start | bytes 3637256 | tf_op jit(solution)/shard_map/ppermute | solution.py:587
  11.6 0.6 broadcast_in_dim.30.gain
  12.2 0.1 pad.4.clone
  12.2 0.7 maximum_maximum_fusion.row
  12.9 13.0 %project.1 = (bf16[2048,256]{1,0:T(8,128)(2,1)}, bf16[2048,512]{1,0:T(8,128)(2,1)}, bf16[2048,256]{1,0:T(8,128)(2,1)}, f32[8,2,128,128]{3,2,1,0:T(8,128)}, bf16[...) custom-call(s32[16]{0:T(128)} %owner.1, s32[16]{0:T(128)} %slot.1, ...), custom_call_target="tpu_custom_call" | custom-call | tf_op jit(solution)/shard_map/project/pallas_call | solution.py:185
  26.0 5.4 %all-to-all-start = ((bf16[8,264,128]{2,1,0:T(8,128)(2,1)}), bf16[8,264,128]{2,1,0:T(8,128)(2,1)S(1)}, u32[]{:S(2)}, u32[]{:S(2)}) async-start(bf16[8,264,128]{2,1,0:T(8,128)(2,1)} %get-tuple-element.71), calls=%async_computation | async-start | bytes 1081344 | tf_op jit(solution)/shard_map/all_to_all | solution.py:605
  31.4 0.1 slice.18
  31.5 0.6 broadcast_in_dim.33.gain
  32.1 0.7 pad_maximum_fusion.bound
  32.8 6.3 %attend.2.at0 = f32[1024,256]{1,0:T(8,128)} custom-call(bf16[2048,256]{1,0:T(8,128)(2,1)} %get-tuple-element.81.q, bf16[2048,512]{1,0:T(8,128)(2,1)} %get-tuple-element.68.k.v.kv, bf16[2048,512]{1,0:T(8,128)(2,1)} %get-tuple-element.68.k.v.kv, bf16[16,256]{1,0:T(8,128)(2,1)} %pk.3, bf16[16,256]{1,0:T(8,128)(2,1)} %pv.3, f32[2048,8]{1,0:T(8,128)} %get-tuple-element.69.col, ...), custom_call_target="tpu_custom_call" | custom-call | flops 1400000000 | bytes 4000000 | tf_op jit(solution)/shard_map/attend/pallas_call | solution.py:270
  39.1 1.4 all-to-all-done.got
  40.5 0.8 copy-done.5
  41.3 2.0 %combine.1 = (f32[2,128,128]{2,1,0:T(8,128)}, f32[8,128]{1,0:T(8,128)}, bf16[4,264,128]{2,1,0:T(8,128)(2,1)}) custom-call(s32[5]{0:T(128)} %stack.23.place, bf16[8,264,128]{2,1,0:T(8,128)(2,1)} %copy-done.5), custom_call_target="tpu_custom_call" | custom-call | tf_op jit(solution)/shard_map/combine/pallas_call | solution.py:227
  43.3 4.3 %all-to-all-start.1 = ((bf16[4,264,128]{2,1,0:T(8,128)(2,1)}), bf16[4,264,128]{2,1,0:T(8,128)(2,1)S(1)}, u32[]{:S(2)}, u32[]{:S(2)}) async-start(bf16[4,264,128]{2,1,0:T(8,128)(2,1)} %get-tuple-element.80), calls=%async_computation.1 | async-start | bytes 540672 | tf_op jit(solution)/shard_map/all_to_all | solution.py:605
  47.6 6.3 %attend.3.at1 = f32[1024,256]{1,0:T(8,128)} custom-call(bf16[2048,256]{1,0:T(8,128)(2,1)} %get-tuple-element.81.q, bf16[2048,512]{1,0:T(8,128)(2,1)} %get-tuple-element.68.k.v.kv, bf16[2048,512]{1,0:T(8,128)(2,1)} %get-tuple-element.68.k.v.kv, bf16[16,256]{1,0:T(8,128)(2,1)} %pk.3, bf16[16,256]{1,0:T(8,128)(2,1)} %pv.3, f32[2048,8]{1,0:T(8,128)} %get-tuple-element.69.col, ...), custom_call_target="tpu_custom_call" | custom-call | flops 1400000000 | bytes 4000000 | tf_op jit(solution)/shard_map/attend/pallas_call | solution.py:270
  53.9 0.4 all-to-all-done.1.got
  54.4 0.7 copy-done.4
  55.1 6.6 %all-to-all-start.2 = ((bf16[32,136,512]{2,1,0:T(8,128)(2,1)}), bf16[32,136,512]{2,1,0:T(8,128)(2,1)}, u32[]{:S(2)}, u32[]{:S(2)}) async-start(bf16[32,136,512]{2,1,0:T(8,128)(2,1)} %get-tuple-element.124), calls=%async_computation.2 | async-start | bytes 8912896 | tf_op jit(solution)/shard_map/all_to_all | solution.py:615
  61.7 2.2 %collective-permute-done.rest_8_ = bf16[592,1024]{1,0:T(8,128)(2,1)} collective-permute-done((bf16[592,1024]{1,0:T(8,128)(2,1)}, bf16[592,1024]{1,0:T(8,128)(2,1)}, u32[]{:S(2)}, u32[]{:S(2)}) %collective-permute-start) | collective-permute-done | bytes 1212448 | tf_op jit(solution)/shard_map/ppermute | solution.py:587
  63.9 0.0 collective-permute-done.1.rest_11_
  64.0 0.1 collective-permute-start.4
  64.1 0.5 collective-permute-start.5
  64.6 0.1 collective-permute-start.6
  64.6 0.4 collective-permute-start.7
  65.1 3.0 %collective-permute-done.4.rest_14_ = bf16[592,1024]{1,0:T(8,128)(2,1)} collective-permute-done((bf16[592,1024]{1,0:T(8,128)(2,1)}, bf16[592,1024]{1,0:T(8,128)(2,1)}, u32[]{:S(2)}, u32[]{:S(2)}) %collective-permute-start.4) | collective-permute-done | bytes 1212448 | tf_op jit(solution)/shard_map/ppermute | solution.py:588
  68.1 1.1 collective-permute-start.12
  69.1 7.4 %recall.3 = (bf16[256,256]{1,0:T(8,128)(2,1)}, bf16[256,256]{1,0:T(8,128)(2,1)}, bf16[256,256]{1,0:T(8,128)(2,1)}, bf16[256,256]{1,0:T(8,128)(2,1)}) custom-call(s32[5]{0:T(128)} %stack.23.place, f32[8]{0:T(128)} %pad_maximum_fusion.bound, bf16[2048,256]{1,0:T(8,128)(2,1)} %get-tuple-element.81.q, bf16[2048,256]{1,0:T(8,128)(2,1)} %get-tuple-element.74.ku, ...), custom_call_target="tpu_custom_call" | custom-call | flops 400000000 | bytes 4000000 | tf_op jit(solution)/shard_map/recall/pallas_call | solution.py:372
  76.6 1.2 collective-permute-start.8
  77.8 2.3 %collective-permute-start.9 = (bf16[256,256]{1,0:T(8,128)(2,1)}, bf16[256,256]{1,0:T(8,128)(2,1)S(1)}, u32[]{:S(2)}, u32[]{:S(2)}) collective-permute-start(bf16[256,256]{1,0:T(8,128)(2,1)} %get-tuple-element.103), channel_id=1, source_target_pairs={{0,3},{1,0},{2,1},{3,2},{4,7},{5,4},{6,5},{7,6},{8,11},{9,8},{10,9... | collective-permute-start | bytes 393224 | tf_op jit(solution)/shard_map/ppermute | solution.py:587
  80.1 7.4 %recall.2 = (bf16[256,256]{1,0:T(8,128)(2,1)}, bf16[256,256]{1,0:T(8,128)(2,1)}, bf16[256,256]{1,0:T(8,128)(2,1)}, bf16[256,256]{1,0:T(8,128)(2,1)}) custom-call(s32[5]{0:T(128)} %stack.23.place, f32[8]{0:T(128)} %pad_maximum_fusion.bound, bf16[2048,256]{1,0:T(8,128)(2,1)} %get-tuple-element.81.q, bf16[2048,256]{1,0:T(8,128)(2,1)} %get-tuple-element.74.ku, ...), custom_call_target="tpu_custom_call" | custom-call | flops 400000000 | bytes 4000000 | tf_op jit(solution)/shard_map/recall/pallas_call | solution.py:372
  87.6 13.2 %collective-permute-done.8.rest_1_ = bf16[256,256]{1,0:T(8,128)(2,1)S(1)} collective-permute-done((bf16[256,256]{1,0:T(8,128)(2,1)}, bf16[256,256]{1,0:T(8,128)(2,1)S(1)}, u32[]{:S(2)}, u32[]{:S(2)}) %collective-permute-start.8) | collective-permute-done | bytes 131104 | tf_op jit(solution)/shard_map/ppermute | solution.py:587
  100.8 0.1 collective-permute-start.13
  100.9 0.5 collective-permute-start.14
  101.4 1.8 %collective-permute-start.15 = (bf16[256,256]{1,0:T(8,128)(2,1)}, bf16[256,256]{1,0:T(8,128)(2,1)S(1)}, u32[]{:S(2)}, u32[]{:S(2)}) collective-permute-start(bf16[256,256]{1,0:T(8,128)(2,1)} %get-tuple-element.116), channel_id=1, source_target_pairs={{0,1},{1,2},{2,3},{3,0},{4,5},{5,6},{6,7},{7,4},{8,9},{9,10},{10,1... | collective-permute-start | bytes 393224 | tf_op jit(solution)/shard_map/ppermute | solution.py:587
  103.2 2.5 %collective-permute-start.16 = (bf16[256,256]{1,0:T(8,128)(2,1)}, bf16[256,256]{1,0:T(8,128)(2,1)S(1)}, u32[]{:S(2)}, u32[]{:S(2)}) collective-permute-start(bf16[256,256]{1,0:T(8,128)(2,1)} %get-tuple-element.117), channel_id=1, source_target_pairs={{0,3},{1,0},{2,1},{3,2},{4,7},{5,4},{6,5},{7,6},{8,11},{9,8},{10,9... | collective-permute-start | bytes 393224 | tf_op jit(solution)/shard_map/ppermute | solution.py:587
  105.7 1.5 collective-permute-start.17
  107.2 1.0 copy-done.2
  108.2 1.0 copy-done.3
  109.2 11.5 %ffn.2.refs_0_ = bf16[256,1024]{1,0:T(8,128)(2,1)} custom-call(s32[5]{0:T(128)} %stack.23.place, bf16[1,1024]{1,0:T(2,128)(2,1)} %broadcast_in_dim.33.gain, bf16[2048,1024]{1,0:T(8,128)(2,1)} %tokens.3, bf16[256,256]{1,0:T(8,128)(2,1)} %get-tuple-element.105.rest_0_, bf16[256,256]{1,0:T(8,128)(2,1)} %copy-done.12, bf16[256,256]{1,0:T(8,128)(2,1)} %copy-done.13, ...), custom_call_target="tpu_custom_call" | custom-call | tf_op jit(solution)/shard_map/ffn/pallas_call | solution.py:481
  120.8 1.5 collective-permute-start.20
  122.2 1.8 %collective-permute-start.21 = (bf16[256,1024]{1,0:T(8,128)(2,1)}, bf16[256,1024]{1,0:T(8,128)(2,1)S(1)}, u32[]{:S(2)}, u32[]{:S(2)}) collective-permute-start(bf16[256,1024]{1,0:T(8,128)(2,1)} %ffn.2.refs_0_), channel_id=1, source_target_pairs={{0,3},{1,0},{2,1},{3,2},{4,7},{5,4},{6,5},{7,6},{8,11},{9,8},{10,9... | collective-permute-start | bytes 1572872 | tf_op jit(solution)/shard_map/ppermute | solution.py:587
  124.1 11.5 %ffn.3.refs_3_ = bf16[256,1024]{1,0:T(8,128)(2,1)} custom-call(s32[5]{0:T(128)} %stack.23.place, bf16[1,1024]{1,0:T(2,128)(2,1)} %broadcast_in_dim.33.gain, bf16[2048,1024]{1,0:T(8,128)(2,1)} %tokens.3, bf16[256,256]{1,0:T(8,128)(2,1)} %get-tuple-element.119.rest_0_, bf16[256,256]{1,0:T(8,128)(2,1)} %copy-done.15, bf16[256,256]{1,0:T(8,128)(2,1)} %copy-done.16, ...), custom_call_target="tpu_custom_call" | custom-call | tf_op jit(solution)/shard_map/ffn/pallas_call | solution.py:481
  135.6 0.3 collective-permute-start.18
  135.8 3.0 %collective-permute-start.19 = (bf16[256,1024]{1,0:T(8,128)(2,1)}, bf16[256,1024]{1,0:T(8,128)(2,1)S(1)}, u32[]{:S(2)}, u32[]{:S(2)}) collective-permute-start(bf16[256,1024]{1,0:T(8,128)(2,1)} %ffn.3.refs_3_), channel_id=1, source_target_pairs={{0,3},{1,0},{2,1},{3,2},{4,7},{5,4},{6,5},{7,6},{8,11},{9,8},{10,9... | collective-permute-start | bytes 1572872 | tf_op jit(solution)/shard_map/ppermute | solution.py:587
  138.9 0.1 collective-permute-start.24
  139.0 3.3 %collective-permute-start.25 = (bf16[128,1024]{1,0:T(8,128)(2,1)S(1)}, bf16[128,1024]{1,0:T(8,128)(2,1)S(1)}, u32[]{:S(2)}, u32[]{:S(2)}) collective-permute-start(bf16[128,1024]{1,0:T(8,128)(2,1)S(1)} %slice.26), channel_id=1, source_target_pairs={{0,3},{1,0},{2,1},{3,2},{4,7},{5,4},{6,5},{7,6},{8,11},{9,8},{10,9... | collective-permute-start | bytes 786440 | tf_op jit(solution)/shard_map/ppermute | solution.py:587
  142.3 3.1 %join.2.refs_4_ = bf16[2048,1024]{1,0:T(8,128)(2,1)} custom-call(s32[5]{0:T(128)} %stack.23.place, bf16[256,1024]{1,0:T(8,128)(2,1)} %ffn.2.refs_0_, bf16[256,1024]{1,0:T(8,128)(2,1)} %copy-done.8, bf16[256,1024]{1,0:T(8,128)(2,1)} %copy-done.9, bf16[256,1024]{1,0:T(8,128)(2,1)} %ffn.3.refs_3_), custom_call_target="tpu_custom_call" | custom-call | tf_op jit(solution)/shard_map/join/pallas_call | solution.py:538
  145.4 1.2 fusion
  146.6 0.2 select_reduce_fusion
  146.8 0.5 broadcast_clamp_fusion.source
  147.3 3.2 %place.1 = bf16[16,128,512]{2,1,0:T(8,128)(2,1)} custom-call(s32[16]{0:T(128)} %broadcast_clamp_fusion.source, bf16[32,136,512]{2,1,0:T(8,128)(2,1)} %all-to-all-done.2.got), custom_call_target="tpu_custom_call" | custom-call | tf_op jit(solution)/shard_map/place/pallas_call | solution.py:515
  150.5 1.4 collective-permute-done.18.refs_0_
  152.0 0.1 collective-permute-start.22
  152.1 3.3 %collective-permute-start.23 = (bf16[128,1024]{1,0:T(8,128)(2,1)S(1)}, bf16[128,1024]{1,0:T(8,128)(2,1)S(1)}, u32[]{:S(2)}, u32[]{:S(2)}) collective-permute-start(bf16[128,1024]{1,0:T(8,128)(2,1)S(1)} %slice.21), channel_id=1, source_target_pairs={{0,3},{1,0},{2,1},{3,2},{4,7},{5,4},{6,5},{7,6},{8,11},{9,8},{10,9... | collective-permute-start | bytes 786440 | tf_op jit(solution)/shard_map/ppermute | solution.py:587
  155.4 2.2 %collective-permute-done.24.refs_2_ = bf16[128,1024]{1,0:T(8,128)(2,1)S(1)} collective-permute-done((bf16[128,1024]{1,0:T(8,128)(2,1)S(1)}, bf16[128,1024]{1,0:T(8,128)(2,1)S(1)}, u32[]{:S(2)}, u32[]{:S(2)}) %collective-permute-start.24) | collective-permute-done | bytes 262176 | tf_op jit(solution)/shard_map/ppermute | solution.py:587
  157.6 0.7 copy-done.10
  158.2 0.7 copy-done.11
  158.9 2.9 %join.3 = bf16[2048,1024]{1,0:T(8,128)(2,1)} custom-call(s32[5]{0:T(128)} %stack.23.place, bf16[256,1024]{1,0:T(8,128)(2,1)} %copy-done.6, bf16[256,1024]{1,0:T(8,128)(2,1)} %copy-done.7, bf16[128,1024]{1,0:T(8,128)(2,1)} %copy-done.10, bf16[128,1024]{1,0:T(8,128)(2,1)} %copy-done.11, bf16[2048,1024]{1,0:T(8,128)(2,1)} %join.2.refs_4_), custom_call_target="tpu_custom_call", output_to_operand_aliasing={{}: (5, {})} | custom-call | tf_op jit(solution)/shard_map/join/pallas_call | solution.py:538
  161.9 0.7 constant_dynamic-update-slice_fusion
  162.6 0.7 constant_dynamic-update-slice_fusion.1
  (69 shorter events, 0.2 us)
Async XLA Ops:
  1.3 10.2 %copy-start.20 = (bf16[1024]{0:T(1024)(128)(2,1)S(1)}, bf16[1024]{0:T(1024)(128)(2,1)}, u32[]{:S(2)}) copy-start(bf16[1024]{0:T(1024)(128)(2,1)} %param.18) | copy-start | bytes 6148
  1.3 10.8 %copy-start.19 = (s32[2048]{0:T(1024)S(1)}, s32[2048]{0:T(1024)}, u32[]{:S(2)}) copy-start(s32[2048]{0:T(1024)} %param.31) | copy-start | bytes 24580
  1.3 10.9 %copy-start.18 = (f32[2048,2]{0,1:T(2,128)S(1)}, f32[2048,2]{0,1:T(2,128)}, u32[]{:S(2)}) copy-start(f32[2048,2]{0,1:T(2,128)} %param.24) | copy-start | bytes 49156
  5.2 58.7 %collective-permute-start.1 = (bf16[592,1024]{1,0:T(8,128)(2,1)}, bf16[592,1024]{1,0:T(8,128)(2,1)S(1)}, u32[]{:S(2)}, u32[]{:S(2)}) collective-permute-start(bf16[592,1024]{1,0:T(8,128)(2,1)} %get-tuple-element.87), channel_id=1, source_target_pairs={{0,3},{1,0},{2,1},{3,2},{4,7},{5,4},{6,5},{7,6},{8,11},{9,8},{10,9... | collective-permute-start | bytes 3637256 | tf_op jit(solution)/shard_map/ppermute | solution.py:587
  8.3 55.6 %collective-permute-start.2 = (bf16[592,1024]{1,0:T(8,128)(2,1)}, bf16[592,1024]{1,0:T(8,128)(2,1)S(1)}, u32[]{:S(2)}, u32[]{:S(2)}) collective-permute-start(bf16[592,1024]{1,0:T(8,128)(2,1)} %get-tuple-element.87), channel_id=1, source_target_pairs={{0,1},{1,2},{2,3},{3,0},{4,5},{5,6},{6,7},{7,4},{8,9},{9,10},{10,1... | collective-permute-start | bytes 3637256 | tf_op jit(solution)/shard_map/ppermute | solution.py:587
  8.3 55.6 %collective-permute-start = (bf16[592,1024]{1,0:T(8,128)(2,1)}, bf16[592,1024]{1,0:T(8,128)(2,1)}, u32[]{:S(2)}, u32[]{:S(2)}) collective-permute-start(bf16[592,1024]{1,0:T(8,128)(2,1)} %get-tuple-element.86), channel_id=1, source_target_pairs={{0,1},{1,2},{2,3},{3,0},{4,5},{5,6},{6,7},{7,4},{8,9},{9,10},{10,1... | collective-permute-start | bytes 3637256 | tf_op jit(solution)/shard_map/ppermute | solution.py:587
  8.9 55.1 %collective-permute-start.3 = (bf16[592,1024]{1,0:T(8,128)(2,1)}, bf16[592,1024]{1,0:T(8,128)(2,1)}, u32[]{:S(2)}, u32[]{:S(2)}) collective-permute-start(bf16[592,1024]{1,0:T(8,128)(2,1)} %get-tuple-element.86), channel_id=1, source_target_pairs={{0,3},{1,0},{2,1},{3,2},{4,7},{5,4},{6,5},{7,6},{8,11},{9,8},{10,9... | collective-permute-start | bytes 3637256 | tf_op jit(solution)/shard_map/ppermute | solution.py:587
  12.9 18.5 %copy-start.21 = (bf16[1024]{0:T(1024)(128)(2,1)S(1)}, bf16[1024]{0:T(1024)(128)(2,1)}, u32[]{:S(2)}) copy-start(bf16[1024]{0:T(1024)(128)(2,1)} %param.27) | copy-start | bytes 6148
  26.0 14.5 %all-to-all-start = ((bf16[8,264,128]{2,1,0:T(8,128)(2,1)}), bf16[8,264,128]{2,1,0:T(8,128)(2,1)S(1)}, u32[]{:S(2)}, u32[]{:S(2)}) async-start(bf16[8,264,128]{2,1,0:T(8,128)(2,1)} %get-tuple-element.71), calls=%async_computation | async-start | bytes 1081344 | tf_op jit(solution)/shard_map/all_to_all | solution.py:605
  40.5 0.8 copy-start.5
  43.3 11.0 %all-to-all-start.1 = ((bf16[4,264,128]{2,1,0:T(8,128)(2,1)}), bf16[4,264,128]{2,1,0:T(8,128)(2,1)S(1)}, u32[]{:S(2)}, u32[]{:S(2)}) async-start(bf16[4,264,128]{2,1,0:T(8,128)(2,1)} %get-tuple-element.80), calls=%async_computation.1 | async-start | bytes 540672 | tf_op jit(solution)/shard_map/all_to_all | solution.py:605
  54.3 0.7 copy-start.4
  55.1 90.4 %all-to-all-start.2 = ((bf16[32,136,512]{2,1,0:T(8,128)(2,1)}), bf16[32,136,512]{2,1,0:T(8,128)(2,1)}, u32[]{:S(2)}, u32[]{:S(2)}) async-start(bf16[32,136,512]{2,1,0:T(8,128)(2,1)} %get-tuple-element.124), calls=%async_computation.2 | async-start | bytes 8912896 | tf_op jit(solution)/shard_map/all_to_all | solution.py:615
  63.9 12.6 %copy-start = (bf16[592,1024]{1,0:T(8,128)(2,1)}, bf16[592,1024]{1,0:T(8,128)(2,1)S(1)}, u32[]{:S(2)}) copy-start(bf16[592,1024]{1,0:T(8,128)(2,1)S(1)} %collective-permute-done.1.rest_11_) | copy-start | bytes 3637252
  63.9 12.6 %copy-start.1 = (bf16[592,1024]{1,0:T(8,128)(2,1)}, bf16[592,1024]{1,0:T(8,128)(2,1)S(1)}, u32[]{:S(2)}) copy-start(bf16[592,1024]{1,0:T(8,128)(2,1)S(1)} %collective-permute-done.2.rest_9_) | copy-start | bytes 3637252
  64.0 4.1 %collective-permute-start.4 = (bf16[592,1024]{1,0:T(8,128)(2,1)}, bf16[592,1024]{1,0:T(8,128)(2,1)}, u32[]{:S(2)}, u32[]{:S(2)}) collective-permute-start(bf16[592,1024]{1,0:T(8,128)(2,1)} %collective-permute-done.rest_8_), channel_id=1, source_target_pairs={{0,4},{4,0},{8,12},{12,8},{16,20},{20,16},{24,28},{28,24},{32,36},... | collective-permute-start | bytes 3637256 | tf_op jit(solution)/shard_map/ppermute | solution.py:588
  64.1 12.5 %collective-permute-start.5 = (bf16[592,1024]{1,0:T(8,128)(2,1)S(1)}, bf16[592,1024]{1,0:T(8,128)(2,1)}, u32[]{:S(2)}, u32[]{:S(2)}) collective-permute-start(bf16[592,1024]{1,0:T(8,128)(2,1)S(1)} %collective-permute-done.1.rest_11_), channel_id=1, source_target_pairs={{0,4},{4,0},{8,12},{12,8},{16,20},{20,16},{24,28},{28,24},{32,36},... | collective-permute-start | bytes 3637256 | tf_op jit(solution)/shard_map/ppermute | solution.py:588
  64.6 12.0 %collective-permute-start.6 = (bf16[592,1024]{1,0:T(8,128)(2,1)S(1)}, bf16[592,1024]{1,0:T(8,128)(2,1)}, u32[]{:S(2)}, u32[]{:S(2)}) collective-permute-start(bf16[592,1024]{1,0:T(8,128)(2,1)S(1)} %collective-permute-done.2.rest_9_), channel_id=1, source_target_pairs={{0,4},{4,0},{8,12},{12,8},{16,20},{20,16},{24,28},{28,24},{32,36},... | collective-permute-start | bytes 3637256 | tf_op jit(solution)/shard_map/ppermute | solution.py:588
  64.6 12.0 %collective-permute-start.7 = (bf16[592,1024]{1,0:T(8,128)(2,1)}, bf16[592,1024]{1,0:T(8,128)(2,1)}, u32[]{:S(2)}, u32[]{:S(2)}) collective-permute-start(bf16[592,1024]{1,0:T(8,128)(2,1)} %collective-permute-done.3.rest_10_), channel_id=1, source_target_pairs={{0,4},{4,0},{8,12},{12,8},{16,20},{20,16},{24,28},{28,24},{32,36},... | collective-permute-start | bytes 3637256 | tf_op jit(solution)/shard_map/ppermute | solution.py:588
  65.1 35.7 %collective-permute-start.11 = (bf16[592,1024]{1,0:T(8,128)(2,1)}, bf16[592,1024]{1,0:T(8,128)(2,1)}, u32[]{:S(2)}, u32[]{:S(2)}) collective-permute-start(bf16[592,1024]{1,0:T(8,128)(2,1)} %collective-permute-done.rest_8_), channel_id=1, source_target_pairs={{0,1},{1,2},{2,3},{3,0},{4,5},{5,6},{6,7},{7,4},{8,9},{9,10},{10,1... | collective-permute-start | bytes 3637256 | tf_op jit(solution)/shard_map/ppermute | solution.py:587
  68.1 32.7 %collective-permute-start.12 = (bf16[592,1024]{1,0:T(8,128)(2,1)S(1)}, bf16[592,1024]{1,0:T(8,128)(2,1)}, u32[]{:S(2)}, u32[]{:S(2)}) collective-permute-start(bf16[592,1024]{1,0:T(8,128)(2,1)S(1)} %collective-permute-done.1.rest_11_), channel_id=1, source_target_pairs={{0,3},{1,0},{2,1},{3,2},{4,7},{5,4},{6,5},{7,6},{8,11},{9,8},{10,9... | collective-permute-start | bytes 3637256 | tf_op jit(solution)/shard_map/ppermute | solution.py:587
  76.6 24.2 %collective-permute-start.8 = (bf16[256,256]{1,0:T(8,128)(2,1)}, bf16[256,256]{1,0:T(8,128)(2,1)S(1)}, u32[]{:S(2)}, u32[]{:S(2)}) collective-permute-start(bf16[256,256]{1,0:T(8,128)(2,1)} %get-tuple-element.102), channel_id=1, source_target_pairs={{0,1},{1,2},{2,3},{3,0},{4,5},{5,6},{6,7},{7,4},{8,9},{9,10},{10,1... | collective-permute-start | bytes 393224 | tf_op jit(solution)/shard_map/ppermute | solution.py:587
  77.8 22.9 %collective-permute-start.9 = (bf16[256,256]{1,0:T(8,128)(2,1)}, bf16[256,256]{1,0:T(8,128)(2,1)S(1)}, u32[]{:S(2)}, u32[]{:S(2)}) collective-permute-start(bf16[256,256]{1,0:T(8,128)(2,1)} %get-tuple-element.103), channel_id=1, source_target_pairs={{0,3},{1,0},{2,1},{3,2},{4,7},{5,4},{6,5},{7,6},{8,11},{9,8},{10,9... | collective-permute-start | bytes 393224 | tf_op jit(solution)/shard_map/ppermute | solution.py:587
  80.1 20.7 %collective-permute-start.10 = (bf16[256,256]{1,0:T(8,128)(2,1)}, bf16[256,256]{1,0:T(8,128)(2,1)S(1)}, u32[]{:S(2)}, u32[]{:S(2)}) collective-permute-start(bf16[256,256]{1,0:T(8,128)(2,1)} %get-tuple-element.104), channel_id=1, source_target_pairs={{0,2},{1,3},{2,0},{3,1},{4,6},{5,7},{6,4},{7,5},{8,10},{9,11},{10,... | collective-permute-start | bytes 393224 | tf_op jit(solution)/shard_map/ppermute | solution.py:587
  100.8 6.4 %copy-start.12 = (bf16[256,256]{1,0:T(8,128)(2,1)}, bf16[256,256]{1,0:T(8,128)(2,1)S(1)}, u32[]{:S(2)}) copy-start(bf16[256,256]{1,0:T(8,128)(2,1)S(1)} %collective-permute-done.8.rest_1_) | copy-start | bytes 393220
  100.8 6.4 %copy-start.13 = (bf16[256,256]{1,0:T(8,128)(2,1)}, bf16[256,256]{1,0:T(8,128)(2,1)S(1)}, u32[]{:S(2)}) copy-start(bf16[256,256]{1,0:T(8,128)(2,1)S(1)} %collective-permute-done.9.rest_2_) | copy-start | bytes 393220
  100.8 6.4 %copy-start.14 = (bf16[256,256]{1,0:T(8,128)(2,1)}, bf16[256,256]{1,0:T(8,128)(2,1)S(1)}, u32[]{:S(2)}) copy-start(bf16[256,256]{1,0:T(8,128)(2,1)S(1)} %collective-permute-done.10.rest_3_) | copy-start | bytes 393220
  100.8 6.3 %collective-permute-start.13 = (bf16[592,1024]{1,0:T(8,128)(2,1)}, bf16[592,1024]{1,0:T(8,128)(2,1)S(1)}, u32[]{:S(2)}, u32[]{:S(2)}) collective-permute-start(bf16[592,1024]{1,0:T(8,128)(2,1)} %collective-permute-done.11.rest_12_), channel_id=1, source_target_pairs={{0,4},{4,0},{8,12},{12,8},{16,20},{20,16},{24,28},{28,24},{32,36},... | collective-permute-start | bytes 3637256 | tf_op jit(solution)/shard_map/ppermute | solution.py:588
  100.9 6.2 %collective-permute-start.14 = (bf16[592,1024]{1,0:T(8,128)(2,1)}, bf16[592,1024]{1,0:T(8,128)(2,1)S(1)}, u32[]{:S(2)}, u32[]{:S(2)}) collective-permute-start(bf16[592,1024]{1,0:T(8,128)(2,1)} %collective-permute-done.12.rest_13_), channel_id=1, source_target_pairs={{0,4},{4,0},{8,12},{12,8},{16,20},{20,16},{24,28},{28,24},{32,36},... | collective-permute-start | bytes 3637256 | tf_op jit(solution)/shard_map/ppermute | solution.py:588
  101.4 19.3 %collective-permute-start.15 = (bf16[256,256]{1,0:T(8,128)(2,1)}, bf16[256,256]{1,0:T(8,128)(2,1)S(1)}, u32[]{:S(2)}, u32[]{:S(2)}) collective-permute-start(bf16[256,256]{1,0:T(8,128)(2,1)} %get-tuple-element.116), channel_id=1, source_target_pairs={{0,1},{1,2},{2,3},{3,0},{4,5},{5,6},{6,7},{7,4},{8,9},{9,10},{10,1... | collective-permute-start | bytes 393224 | tf_op jit(solution)/shard_map/ppermute | solution.py:587
  103.2 17.5 %collective-permute-start.16 = (bf16[256,256]{1,0:T(8,128)(2,1)}, bf16[256,256]{1,0:T(8,128)(2,1)S(1)}, u32[]{:S(2)}, u32[]{:S(2)}) collective-permute-start(bf16[256,256]{1,0:T(8,128)(2,1)} %get-tuple-element.117), channel_id=1, source_target_pairs={{0,3},{1,0},{2,1},{3,2},{4,7},{5,4},{6,5},{7,6},{8,11},{9,8},{10,9... | collective-permute-start | bytes 393224 | tf_op jit(solution)/shard_map/ppermute | solution.py:587
  105.7 15.1 %collective-permute-start.17 = (bf16[256,256]{1,0:T(8,128)(2,1)}, bf16[256,256]{1,0:T(8,128)(2,1)S(1)}, u32[]{:S(2)}, u32[]{:S(2)}) collective-permute-start(bf16[256,256]{1,0:T(8,128)(2,1)} %get-tuple-element.118), channel_id=1, source_target_pairs={{0,2},{1,3},{2,0},{3,1},{4,6},{5,7},{6,4},{7,5},{8,10},{9,11},{10,... | collective-permute-start | bytes 393224 | tf_op jit(solution)/shard_map/ppermute | solution.py:587
  107.1 1.0 copy-start.2
  108.2 1.0 copy-start.3
  120.7 3.4 %copy-start.15 = (bf16[256,256]{1,0:T(8,128)(2,1)}, bf16[256,256]{1,0:T(8,128)(2,1)S(1)}, u32[]{:S(2)}) copy-start(bf16[256,256]{1,0:T(8,128)(2,1)S(1)} %collective-permute-done.15.rest_1_) | copy-start | bytes 393220
  120.7 3.3 %copy-start.16 = (bf16[256,256]{1,0:T(8,128)(2,1)}, bf16[256,256]{1,0:T(8,128)(2,1)S(1)}, u32[]{:S(2)}) copy-start(bf16[256,256]{1,0:T(8,128)(2,1)S(1)} %collective-permute-done.16.rest_2_) | copy-start | bytes 393220
  120.7 3.3 %copy-start.17 = (bf16[256,256]{1,0:T(8,128)(2,1)}, bf16[256,256]{1,0:T(8,128)(2,1)S(1)}, u32[]{:S(2)}) copy-start(bf16[256,256]{1,0:T(8,128)(2,1)S(1)} %collective-permute-done.17.rest_3_) | copy-start | bytes 393220
  120.8 18.1 %collective-permute-start.20 = (bf16[256,1024]{1,0:T(8,128)(2,1)}, bf16[256,1024]{1,0:T(8,128)(2,1)S(1)}, u32[]{:S(2)}, u32[]{:S(2)}) collective-permute-start(bf16[256,1024]{1,0:T(8,128)(2,1)} %ffn.2.refs_0_), channel_id=1, source_target_pairs={{0,1},{1,2},{2,3},{3,0},{4,5},{5,6},{6,7},{7,4},{8,9},{9,10},{10,1... | collective-permute-start | bytes 1572872 | tf_op jit(solution)/shard_map/ppermute | solution.py:587
  122.2 16.8 %collective-permute-start.21 = (bf16[256,1024]{1,0:T(8,128)(2,1)}, bf16[256,1024]{1,0:T(8,128)(2,1)S(1)}, u32[]{:S(2)}, u32[]{:S(2)}) collective-permute-start(bf16[256,1024]{1,0:T(8,128)(2,1)} %ffn.2.refs_0_), channel_id=1, source_target_pairs={{0,3},{1,0},{2,1},{3,2},{4,7},{5,4},{6,5},{7,6},{8,11},{9,8},{10,9... | collective-permute-start | bytes 1572872 | tf_op jit(solution)/shard_map/ppermute | solution.py:587
  135.6 16.4 %collective-permute-start.18 = (bf16[256,1024]{1,0:T(8,128)(2,1)}, bf16[256,1024]{1,0:T(8,128)(2,1)S(1)}, u32[]{:S(2)}, u32[]{:S(2)}) collective-permute-start(bf16[256,1024]{1,0:T(8,128)(2,1)} %ffn.3.refs_3_), channel_id=1, source_target_pairs={{0,1},{1,2},{2,3},{3,0},{4,5},{5,6},{6,7},{7,4},{8,9},{9,10},{10,1... | collective-permute-start | bytes 1572872 | tf_op jit(solution)/shard_map/ppermute | solution.py:587
  135.8 16.1 %collective-permute-start.19 = (bf16[256,1024]{1,0:T(8,128)(2,1)}, bf16[256,1024]{1,0:T(8,128)(2,1)S(1)}, u32[]{:S(2)}, u32[]{:S(2)}) collective-permute-start(bf16[256,1024]{1,0:T(8,128)(2,1)} %ffn.3.refs_3_), channel_id=1, source_target_pairs={{0,3},{1,0},{2,1},{3,2},{4,7},{5,4},{6,5},{7,6},{8,11},{9,8},{10,9... | collective-permute-start | bytes 1572872 | tf_op jit(solution)/shard_map/ppermute | solution.py:587
  138.9 3.4 %copy-start.8 = (bf16[256,1024]{1,0:T(8,128)(2,1)}, bf16[256,1024]{1,0:T(8,128)(2,1)S(1)}, u32[]{:S(2)}) copy-start(bf16[256,1024]{1,0:T(8,128)(2,1)S(1)} %collective-permute-done.20.refs_1_) | copy-start | bytes 1572868
  138.9 18.6 %collective-permute-start.24 = (bf16[128,1024]{1,0:T(8,128)(2,1)S(1)}, bf16[128,1024]{1,0:T(8,128)(2,1)S(1)}, u32[]{:S(2)}, u32[]{:S(2)}) collective-permute-start(bf16[128,1024]{1,0:T(8,128)(2,1)S(1)} %slice.25), channel_id=1, source_target_pairs={{0,1},{1,2},{2,3},{3,0},{4,5},{5,6},{6,7},{7,4},{8,9},{9,10},{10,1... | collective-permute-start | bytes 786440 | tf_op jit(solution)/shard_map/ppermute | solution.py:587
  139.0 3.3 %copy-start.9 = (bf16[256,1024]{1,0:T(8,128)(2,1)}, bf16[256,1024]{1,0:T(8,128)(2,1)S(1)}, u32[]{:S(2)}) copy-start(bf16[256,1024]{1,0:T(8,128)(2,1)S(1)} %collective-permute-done.21.refs_2_) | copy-start | bytes 1572868
  139.0 18.5 %collective-permute-start.25 = (bf16[128,1024]{1,0:T(8,128)(2,1)S(1)}, bf16[128,1024]{1,0:T(8,128)(2,1)S(1)}, u32[]{:S(2)}, u32[]{:S(2)}) collective-permute-start(bf16[128,1024]{1,0:T(8,128)(2,1)S(1)} %slice.26), channel_id=1, source_target_pairs={{0,3},{1,0},{2,1},{3,2},{4,7},{5,4},{6,5},{7,6},{8,11},{9,8},{10,9... | collective-permute-start | bytes 786440 | tf_op jit(solution)/shard_map/ppermute | solution.py:587
  151.9 5.6 %copy-start.6 = (bf16[256,1024]{1,0:T(8,128)(2,1)}, bf16[256,1024]{1,0:T(8,128)(2,1)S(1)}, u32[]{:S(2)}) copy-start(bf16[256,1024]{1,0:T(8,128)(2,1)S(1)} %collective-permute-done.18.refs_0_) | copy-start | bytes 1572868
  151.9 5.6 %copy-start.7 = (bf16[256,1024]{1,0:T(8,128)(2,1)}, bf16[256,1024]{1,0:T(8,128)(2,1)S(1)}, u32[]{:S(2)}) copy-start(bf16[256,1024]{1,0:T(8,128)(2,1)S(1)} %collective-permute-done.19.refs_1_) | copy-start | bytes 1572868
  152.0 9.9 %collective-permute-start.22 = (bf16[128,1024]{1,0:T(8,128)(2,1)S(1)}, bf16[128,1024]{1,0:T(8,128)(2,1)S(1)}, u32[]{:S(2)}, u32[]{:S(2)}) collective-permute-start(bf16[128,1024]{1,0:T(8,128)(2,1)S(1)} %slice.20), channel_id=1, source_target_pairs={{0,1},{1,2},{2,3},{3,0},{4,5},{5,6},{6,7},{7,4},{8,9},{9,10},{10,1... | collective-permute-start | bytes 786440 | tf_op jit(solution)/shard_map/ppermute | solution.py:587
  152.1 9.8 %collective-permute-start.23 = (bf16[128,1024]{1,0:T(8,128)(2,1)S(1)}, bf16[128,1024]{1,0:T(8,128)(2,1)S(1)}, u32[]{:S(2)}, u32[]{:S(2)}) collective-permute-start(bf16[128,1024]{1,0:T(8,128)(2,1)S(1)} %slice.21), channel_id=1, source_target_pairs={{0,3},{1,0},{2,1},{3,2},{4,7},{5,4},{6,5},{7,6},{8,11},{9,8},{10,9... | collective-permute-start | bytes 786440 | tf_op jit(solution)/shard_map/ppermute | solution.py:587
  157.5 0.7 copy-start.10
  158.2 0.7 copy-start.11

commit v4 on v3

--- a/solution.py
+++ b/solution.py
@@ -546,33 +546,37 @@
     )(place, *pieces, *rest)
 
 
-def cut_kernel(place, gate, up, down, last, p, q, sem):
+def cut_kernel(first, place, *refs):
     core = place[3]
-    copies = [
-        pltpu.make_async_copy(gate.at[pl.ds(core * 352, 352), :], p.at[pl.ds(0, 352), :], sem.at[0]),
-        pltpu.make_async_copy(up.at[pl.ds(core * 352, 240), :], p.at[pl.ds(352, 240), :], sem.at[1]),
-        pltpu.make_async_copy(up.at[pl.ds(core * 352 + 240, 112), :], q.at[pl.ds(0, 112), :], sem.at[2]),
-        pltpu.make_async_copy(down.at[pl.ds(core * 352, 352), :], q.at[pl.ds(112, 352), :], sem.at[3]),
-        pltpu.make_async_copy(last.at[pl.ds(core * 128, 128), :], q.at[pl.ds(464, 128), :], sem.at[4]),
-    ]
+    if first:
+        gate, up, out, sem = refs
+        copies = [
+            pltpu.make_async_copy(gate.at[pl.ds(core * 352, 352), :], out.at[pl.ds(0, 352), :], sem.at[0]),
+            pltpu.make_async_copy(up.at[pl.ds(core * 352, 240), :], out.at[pl.ds(352, 240), :], sem.at[1]),
+        ]
+    else:
+        up, down, last, out, sem = refs
+        copies = [
+            pltpu.make_async_copy(up.at[pl.ds(core * 352 + 240, 112), :], out.at[pl.ds(0, 112), :], sem.at[0]),
+            pltpu.make_async_copy(down.at[pl.ds(core * 352, 352), :], out.at[pl.ds(112, 352), :], sem.at[1]),
+            pltpu.make_async_copy(last.at[pl.ds(core * 128, 128), :], out.at[pl.ds(464, 128), :], sem.at[2]),
+        ]
     for c in copies:
         c.start()
     for c in copies:
         c.wait()
 
 
-def cut_weights(place, gate, up, down, last):
+def cut_weights(first, place, *weights):
     anys = pl.BlockSpec(memory_space=ANY)
-    vm = pl.BlockSpec(memory_space=pltpu.VMEM)
-    shape = jax.ShapeDtypeStruct((592, gate.shape[1]), BF)
-    return pl.pallas_call(
-        cut_kernel,
-        in_specs=[pl.BlockSpec(memory_space=pltpu.SMEM)] + [anys] * 4,
-        out_specs=[vm, vm],
-        out_shape=[shape, shape],
-        scratch_shapes=[pltpu.SemaphoreType.DMA((5,))],
+    return pl.pallas_call(
+        functools.partial(cut_kernel, first),
+        in_specs=[pl.BlockSpec(memory_space=pltpu.SMEM)] + [anys] * len(weights),
+        out_specs=pl.BlockSpec(memory_space=pltpu.VMEM),
+        out_shape=jax.ShapeDtypeStruct((592, weights[0].shape[1]), BF),
+        scratch_shapes=[pltpu.SemaphoreType.DMA((3,))],
         name="cut_weights",
-    )(place, gate, up, down, last)
+    )(place, *weights)
 
 
 def on_device(
@@ -589,8 +593,10 @@
     tie = lambda *a: lax.optimization_barrier(a)
 
     gate, up = w_gate.T, w_up.T
-    p, qq = cut_weights(place, gate, up, w_down, w_out)
-    p1, q3, q1w, p3 = shift(p, 1), shift(qq, -1), shift(qq, 1), shift(p, -1)
+    p = cut_weights(True, place, gate, up)
+    p1, p3 = shift(p, 1), shift(p, -1)
+    qq = cut_weights(False, place, up, w_down, w_out)
+    q3, q1w = shift(qq, -1), shift(qq, 1)
 
     doc = doc_ids.astype(F32)
     row = jnp.concatenate([doc[None], log_forget.T, jnp.zeros((5, count), F32)])
@@ -629,8 +635,10 @@
     tied = tie(*out1, *heads0)
     p2, q2, _ = tie(p2, q2, tied[0])
     out1, heads0 = tied[:4], tied[4:]
-    heads1 = send(out1)
     p2x, q2x = swap(p2), swap(q2)
+    early = shift(out1[1], 1), shift(out1[3], 3)
+    far, p2x, q2x = tie(out1[2], p2x, q2x)
+    heads1 = [out1[0], *early, shift(far, 2)]
     mine, other = [p1, q1w, p3, q3, p2, q2], [p1x, q1x, p3x, q3x, p2x, q2x]
 
     slots = arrived[:, PAGE, 0].astype(F32)

time: 164 us -> 166 us (1.012)
  starting transfers between devices: 48 us -> 50.9 us
  Pallas kernels: 78.6 us -> 80.8 us
  waiting for transfers between devices: 23.9 us -> 21.7 us
    ppermute x20, starting transfers between devices: 30 us -> 32.8 us  [on_device(): lax.ppermute(a, 'tp', [(i, (i + d) % 4) for i in range(4)])]
    pallas_call x1 -> x2, Pallas kernels: 3.86 us -> 5.98 us  [cut_weights(): pl.pallas_call(functools.partial(cut_kernel, first), in_specs=[pl.BlockSp...]
    unnamed x44 -> x46, local copies, waits for them, and re-layouts: 4.97 us -> 3.55 us
  transfers between devices with their start and end apart: 29 -> 29, of which waited for: 7 -> 11; matrix products, arithmetic and copies ran while one was open for 3% -> 3% of each run, Pallas kernels for 46% -> 47%
where the time goes in v4:
time: 166 us; the launch traced here: 165 us
  Pallas kernels  80.8 us (49%)
  starting transfers between devices  50.9 us (31%)
  waiting for transfers between devices  21.7 us (13%)
  local copies, waits for them, and re-layouts  7.03 us (4%)
  other arithmetic  3.2 us (2%)
    ppermute x20, starting transfers between devices, on_device(): lax.ppermute(a, 'tp', [(i, (i + d) % 4) for i in range(4)])  32.8 us
    pallas_call x2, Pallas kernels, ffn(): pl.pallas_call(functools.partial(ffn_kernel, half), grid_spec=gs, out_sha...  23 us
    ppermute x20, waiting for transfers between devices, on_device(): lax.ppermute(a, 'tp', [(i, (i + d) % 4) for i in range(4)])  17.9 us
    pallas_call x2, Pallas kernels, recall(): pl.pallas_call(functools.partial(recall_kernel, half), grid_spec=gs, out_...  14.9 us
    pallas_call x1, Pallas kernels, project(): pl.pallas_call(project_kernel, grid_spec=gs, out_shape=[jax.ShapeDtypeStr...  13 us
    pallas_call x2, Pallas kernels, attend(): pl.pallas_call(attend_kernel, grid=(heads,), in_specs=[pl.BlockSpec((SEG,...  12.6 us
    all_to_all x2, starting transfers between devices, on_device(): lax.all_to_all(a, 'req', 0, 0, tiled=True, axis_index_groups=g)  9.75 us
    all_to_all x1, starting transfers between devices, on_device(): arrived = lax.all_to_all(outgoing, 'req', 0, 0, tiled=True)  6.65 us
  transfers between devices with their start and end apart: 29, of which 11 were waited for; matrix products, arithmetic and copies ran while one was open for 3% of the time, Pallas kernels for 47%

profile of v4, /device:TPU:32, one launch (start us, length us, event | category | flops | bytes accessed | tf_op | source)
XLA Modules:
  0.0 164.6 jit_solution(9389439460614270422)
XLA Ops:
  0.7 0.6 stack.23.place
  1.3 3.0 %cut_weights.2 = bf16[592,1024]{1,0:T(8,128)(2,1)} custom-call(s32[5]{0:T(128)} %stack.23.place, bf16[704,1024]{1,0:T(8,128)(2,1)} %bitcast.14, bf16[704,1024]{1,0:T(8,128)(2,1)} %bitcast.10), custom_call_target="tpu_custom_call" | custom-call | tf_op jit(solution)/shard_map/cut_weights/pallas_call | solution.py:572
  4.3 1.6 collective-permute-start
  6.0 3.0 %cut_weights.3 = bf16[592,1024]{1,0:T(8,128)(2,1)} custom-call(s32[5]{0:T(128)} %stack.23.place, bf16[704,1024]{1,0:T(8,128)(2,1)} %bitcast.11, bf16[704,1024]{1,0:T(8,128)(2,1)} %rest_6_.3, bf16[256,1024]{1,0:T(8,128)(2,1)} %rest_7_.3), custom_call_target="tpu_custom_call" | custom-call | tf_op jit(solution)/shard_map/cut_weights/pallas_call | solution.py:572
  9.0 1.7 %collective-permute-start.1 = (bf16[592,1024]{1,0:T(8,128)(2,1)}, bf16[592,1024]{1,0:T(8,128)(2,1)S(1)}, u32[]{:S(2)}, u32[]{:S(2)}) collective-permute-start(bf16[592,1024]{1,0:T(8,128)(2,1)} %cut_weights.3), channel_id=1, source_target_pairs={{0,3},{1,0},{2,1},{3,2},{4,7},{5,4},{6,5},{7,6},{8,11},{9,8},{10,9... | collective-permute-start | bytes 3637256 | tf_op jit(solution)/shard_map/ppermute | solution.py:591
  10.7 0.4 collective-permute-start.2
  11.1 2.9 %collective-permute-start.3 = (bf16[592,1024]{1,0:T(8,128)(2,1)}, bf16[592,1024]{1,0:T(8,128)(2,1)}, u32[]{:S(2)}, u32[]{:S(2)}) collective-permute-start(bf16[592,1024]{1,0:T(8,128)(2,1)} %cut_weights.2), channel_id=1, source_target_pairs={{0,3},{1,0},{2,1},{3,2},{4,7},{5,4},{6,5},{7,6},{8,11},{9,8},{10,9... | collective-permute-start | bytes 3637256 | tf_op jit(solution)/shard_map/ppermute | solution.py:591
  14.0 0.6 broadcast_in_dim.30.gain
  14.6 0.7 maximum_maximum_fusion.row
  15.3 13.0 %project.1 = (bf16[2048,256]{1,0:T(8,128)(2,1)}, bf16[2048,512]{1,0:T(8,128)(2,1)}, bf16[2048,256]{1,0:T(8,128)(2,1)}, f32[8,2,128,128]{3,2,1,0:T(8,128)}, bf16[...) custom-call(s32[16]{0:T(128)} %owner.1, s32[16]{0:T(128)} %slot.1, ...), custom_call_target="tpu_custom_call" | custom-call | tf_op jit(solution)/shard_map/project/pallas_call | solution.py:185
  28.3 5.4 %all-to-all-start = ((bf16[8,264,128]{2,1,0:T(8,128)(2,1)}), bf16[8,264,128]{2,1,0:T(8,128)(2,1)S(1)}, u32[]{:S(2)}, u32[]{:S(2)}) async-start(bf16[8,264,128]{2,1,0:T(8,128)(2,1)} %get-tuple-element.72), calls=%async_computation | async-start | bytes 1081344 | tf_op jit(solution)/shard_map/all_to_all | solution.py:611
  33.8 0.6 broadcast_in_dim.33.gain
  34.4 0.6 pad_maximum_fusion.bound
  35.1 6.3 %attend.2.at0 = f32[1024,256]{1,0:T(8,128)} custom-call(bf16[2048,256]{1,0:T(8,128)(2,1)} %get-tuple-element.82.q, bf16[2048,512]{1,0:T(8,128)(2,1)} %get-tuple-element.69.k.v.kv, bf16[2048,512]{1,0:T(8,128)(2,1)} %get-tuple-element.69.k.v.kv, bf16[16,256]{1,0:T(8,128)(2,1)} %pk.3, bf16[16,256]{1,0:T(8,128)(2,1)} %pv.3, f32[2048,8]{1,0:T(8,128)} %get-tuple-element.70.col, ...), custom_call_target="tpu_custom_call" | custom-call | flops 1400000000 | bytes 4000000 | tf_op jit(solution)/shard_map/attend/pallas_call | solution.py:270
  41.4 1.4 all-to-all-done.got
  42.8 0.8 copy-done.6
  43.6 2.0 %combine.1 = (f32[2,128,128]{2,1,0:T(8,128)}, f32[8,128]{1,0:T(8,128)}, bf16[4,264,128]{2,1,0:T(8,128)(2,1)}) custom-call(s32[5]{0:T(128)} %stack.23.place, bf16[8,264,128]{2,1,0:T(8,128)(2,1)} %copy-done.6), custom_call_target="tpu_custom_call" | custom-call | tf_op jit(solution)/shard_map/combine/pallas_call | solution.py:227
  45.7 4.3 %all-to-all-start.1 = ((bf16[4,264,128]{2,1,0:T(8,128)(2,1)}), bf16[4,264,128]{2,1,0:T(8,128)(2,1)S(1)}, u32[]{:S(2)}, u32[]{:S(2)}) async-start(bf16[4,264,128]{2,1,0:T(8,128)(2,1)} %get-tuple-element.81), calls=%async_computation.1 | async-start | bytes 540672 | tf_op jit(solution)/shard_map/all_to_all | solution.py:611
  50.0 6.3 %attend.3.at1 = f32[1024,256]{1,0:T(8,128)} custom-call(bf16[2048,256]{1,0:T(8,128)(2,1)} %get-tuple-element.82.q, bf16[2048,512]{1,0:T(8,128)(2,1)} %get-tuple-element.69.k.v.kv, bf16[2048,512]{1,0:T(8,128)(2,1)} %get-tuple-element.69.k.v.kv, bf16[16,256]{1,0:T(8,128)(2,1)} %pk.3, bf16[16,256]{1,0:T(8,128)(2,1)} %pv.3, f32[2048,8]{1,0:T(8,128)} %get-tuple-element.70.col, ...), custom_call_target="tpu_custom_call" | custom-call | flops 1400000000 | bytes 4000000 | tf_op jit(solution)/shard_map/attend/pallas_call | solution.py:270
  56.3 0.4 all-to-all-done.1.got
  56.7 0.7 copy-done.5
  57.4 6.6 %all-to-all-start.2 = ((bf16[32,136,512]{2,1,0:T(8,128)(2,1)}), bf16[32,136,512]{2,1,0:T(8,128)(2,1)}, u32[]{:S(2)}, u32[]{:S(2)}) async-start(bf16[32,136,512]{2,1,0:T(8,128)(2,1)} %get-tuple-element.126), calls=%async_computation.2 | async-start | bytes 8912896 | tf_op jit(solution)/shard_map/all_to_all | solution.py:621
  64.1 0.2 collective-permute-start.4
  64.4 0.4 collective-permute-start.5
  64.9 0.4 collective-permute-start.7
  65.2 0.8 collective-permute-start.11
  66.1 1.3 collective-permute-done.4.rest_14_
  67.3 1.0 copy-done.2
  68.4 3.7 %collective-permute-start.12 = (bf16[592,1024]{1,0:T(8,128)(2,1)S(1)}, bf16[592,1024]{1,0:T(8,128)(2,1)}, u32[]{:S(2)}, u32[]{:S(2)}) collective-permute-start(bf16[592,1024]{1,0:T(8,128)(2,1)S(1)} %collective-permute-done.1.rest_11_), channel_id=1, source_target_pairs={{0,3},{1,0},{2,1},{3,2},{4,7},{5,4},{6,5},{7,6},{8,11},{9,8},{10,9... | collective-permute-start | bytes 3637256 | tf_op jit(solution)/shard_map/ppermute | solution.py:591
  72.0 7.4 %recall.3 = (bf16[256,256]{1,0:T(8,128)(2,1)}, bf16[256,256]{1,0:T(8,128)(2,1)}, bf16[256,256]{1,0:T(8,128)(2,1)}, bf16[256,256]{1,0:T(8,128)(2,1)}) custom-call(s32[5]{0:T(128)} %stack.23.place, f32[8]{0:T(128)} %pad_maximum_fusion.bound, bf16[2048,256]{1,0:T(8,128)(2,1)} %get-tuple-element.82.q, bf16[2048,256]{1,0:T(8,128)(2,1)} %get-tuple-element.75.ku, ...), custom_call_target="tpu_custom_call" | custom-call | flops 400000000 | bytes 4000000 | tf_op jit(solution)/shard_map/recall/pallas_call | solution.py:372
  79.5 0.3 collective-permute-start.8
  79.8 3.2 %collective-permute-start.9 = (bf16[256,256]{1,0:T(8,128)(2,1)}, bf16[256,256]{1,0:T(8,128)(2,1)S(1)}, u32[]{:S(2)}, u32[]{:S(2)}) collective-permute-start(bf16[256,256]{1,0:T(8,128)(2,1)} %get-tuple-element.102), channel_id=1, source_target_pairs={{0,3},{1,0},{2,1},{3,2},{4,7},{5,4},{6,5},{7,6},{8,11},{9,8},{10,9... | collective-permute-start | bytes 393224 | tf_op jit(solution)/shard_map/ppermute | solution.py:591
  83.0 7.5 %recall.2 = (bf16[256,256]{1,0:T(8,128)(2,1)}, bf16[256,256]{1,0:T(8,128)(2,1)}, bf16[256,256]{1,0:T(8,128)(2,1)}, bf16[256,256]{1,0:T(8,128)(2,1)}) custom-call(s32[5]{0:T(128)} %stack.23.place, f32[8]{0:T(128)} %pad_maximum_fusion.bound, bf16[2048,256]{1,0:T(8,128)(2,1)} %get-tuple-element.82.q, bf16[2048,256]{1,0:T(8,128)(2,1)} %get-tuple-element.75.ku, ...), custom_call_target="tpu_custom_call" | custom-call | flops 400000000 | bytes 4000000 | tf_op jit(solution)/shard_map/recall/pallas_call | solution.py:372
  90.5 8.1 %collective-permute-done.8.rest_1_ = bf16[256,256]{1,0:T(8,128)(2,1)S(1)} collective-permute-done((bf16[256,256]{1,0:T(8,128)(2,1)}, bf16[256,256]{1,0:T(8,128)(2,1)S(1)}, u32[]{:S(2)}, u32[]{:S(2)}) %collective-permute-start.8) | collective-permute-done | bytes 131104 | tf_op jit(solution)/shard_map/ppermute | solution.py:591
  98.6 5.3 %collective-permute-done.9.rest_2_ = bf16[256,256]{1,0:T(8,128)(2,1)S(1)} collective-permute-done((bf16[256,256]{1,0:T(8,128)(2,1)}, bf16[256,256]{1,0:T(8,128)(2,1)S(1)}, u32[]{:S(2)}, u32[]{:S(2)}) %collective-permute-start.9) | collective-permute-done | bytes 131104 | tf_op jit(solution)/shard_map/ppermute | solution.py:591
  104.1 0.5 collective-permute-start.14
  104.6 1.7 %collective-permute-start.15 = (bf16[256,256]{1,0:T(8,128)(2,1)}, bf16[256,256]{1,0:T(8,128)(2,1)S(1)}, u32[]{:S(2)}, u32[]{:S(2)}) collective-permute-start(bf16[256,256]{1,0:T(8,128)(2,1)} %get-tuple-element.118), channel_id=1, source_target_pairs={{0,1},{1,2},{2,3},{3,0},{4,5},{5,6},{6,7},{7,4},{8,9},{9,10},{10,1... | collective-permute-start | bytes 393224 | tf_op jit(solution)/shard_map/ppermute | solution.py:591
  106.3 1.9 %collective-permute-start.16 = (bf16[256,256]{1,0:T(8,128)(2,1)}, bf16[256,256]{1,0:T(8,128)(2,1)S(1)}, u32[]{:S(2)}, u32[]{:S(2)}) collective-permute-start(bf16[256,256]{1,0:T(8,128)(2,1)} %get-tuple-element.119), channel_id=1, source_target_pairs={{0,3},{1,0},{2,1},{3,2},{4,7},{5,4},{6,5},{7,6},{8,11},{9,8},{10,9... | collective-permute-start | bytes 393224 | tf_op jit(solution)/shard_map/ppermute | solution.py:591
  108.2 0.7 collective-permute-done.14.rest_19_
  108.9 0.8 collective-permute-start.17
  109.8 0.2 copy-done.4
  110.0 11.5 %ffn.2.refs_0_ = bf16[256,1024]{1,0:T(8,128)(2,1)} custom-call(s32[5]{0:T(128)} %stack.23.place, bf16[1,1024]{1,0:T(2,128)(2,1)} %broadcast_in_dim.33.gain, bf16[2048,1024]{1,0:T(8,128)(2,1)} %tokens.3, bf16[256,256]{1,0:T(8,128)(2,1)} %get-tuple-element.104.rest_0_, bf16[256,256]{1,0:T(8,128)(2,1)} %copy-done.13, bf16[256,256]{1,0:T(8,128)(2,1)} %copy-done.14, ...), custom_call_target="tpu_custom_call" | custom-call | tf_op jit(solution)/shard_map/ffn/pallas_call | solution.py:481
  121.5 3.5 %collective-permute-start.20 = (bf16[256,1024]{1,0:T(8,128)(2,1)}, bf16[256,1024]{1,0:T(8,128)(2,1)S(1)}, u32[]{:S(2)}, u32[]{:S(2)}) collective-permute-start(bf16[256,1024]{1,0:T(8,128)(2,1)} %ffn.2.refs_0_), channel_id=1, source_target_pairs={{0,1},{1,2},{2,3},{3,0},{4,5},{5,6},{6,7},{7,4},{8,9},{9,10},{10,1... | collective-permute-start | bytes 1572872 | tf_op jit(solution)/shard_map/ppermute | solution.py:591
  125.0 0.2 collective-permute-start.21
  125.3 11.5 %ffn.3.refs_3_ = bf16[256,1024]{1,0:T(8,128)(2,1)} custom-call(s32[5]{0:T(128)} %stack.23.place, bf16[1,1024]{1,0:T(2,128)(2,1)} %broadcast_in_dim.33.gain, bf16[2048,1024]{1,0:T(8,128)(2,1)} %tokens.3, bf16[256,256]{1,0:T(8,128)(2,1)} %get-tuple-element.121.rest_0_, bf16[256,256]{1,0:T(8,128)(2,1)} %copy-done.16, bf16[256,256]{1,0:T(8,128)(2,1)} %copy-done.17, ...), custom_call_target="tpu_custom_call" | custom-call | tf_op jit(solution)/shard_map/ffn/pallas_call | solution.py:481
  136.8 1.9 %collective-permute-start.18 = (bf16[256,1024]{1,0:T(8,128)(2,1)}, bf16[256,1024]{1,0:T(8,128)(2,1)S(1)}, u32[]{:S(2)}, u32[]{:S(2)}) collective-permute-start(bf16[256,1024]{1,0:T(8,128)(2,1)} %ffn.3.refs_3_), channel_id=1, source_target_pairs={{0,1},{1,2},{2,3},{3,0},{4,5},{5,6},{6,7},{7,4},{8,9},{9,10},{10,1... | collective-permute-start | bytes 1572872 | tf_op jit(solution)/shard_map/ppermute | solution.py:591
  138.6 1.4 collective-permute-start.19
  140.1 0.7 collective-permute-start.24
  140.8 2.7 %collective-permute-start.25 = (bf16[128,1024]{1,0:T(8,128)(2,1)S(1)}, bf16[128,1024]{1,0:T(8,128)(2,1)S(1)}, u32[]{:S(2)}, u32[]{:S(2)}) collective-permute-start(bf16[128,1024]{1,0:T(8,128)(2,1)S(1)} %slice.26), channel_id=1, source_target_pairs={{0,3},{1,0},{2,1},{3,2},{4,7},{5,4},{6,5},{7,6},{8,11},{9,8},{10,9... | collective-permute-start | bytes 786440 | tf_op jit(solution)/shard_map/ppermute | solution.py:591
  143.5 3.1 %join.2.refs_4_ = bf16[2048,1024]{1,0:T(8,128)(2,1)} custom-call(s32[5]{0:T(128)} %stack.23.place, bf16[256,1024]{1,0:T(8,128)(2,1)} %ffn.2.refs_0_, bf16[256,1024]{1,0:T(8,128)(2,1)} %copy-done.9, bf16[256,1024]{1,0:T(8,128)(2,1)} %copy-done.10, bf16[256,1024]{1,0:T(8,128)(2,1)} %ffn.3.refs_3_), custom_call_target="tpu_custom_call" | custom-call | tf_op jit(solution)/shard_map/join/pallas_call | solution.py:538
  146.6 1.2 fusion
  147.8 0.2 select_reduce_fusion
  148.0 0.5 broadcast_clamp_fusion.source
  148.5 3.2 %place.1 = bf16[16,128,512]{2,1,0:T(8,128)(2,1)} custom-call(s32[16]{0:T(128)} %broadcast_clamp_fusion.source, bf16[32,136,512]{2,1,0:T(8,128)(2,1)} %all-to-all-done.2.got), custom_call_target="tpu_custom_call" | custom-call | tf_op jit(solution)/shard_map/place/pallas_call | solution.py:515
  151.7 1.3 collective-permute-done.18.refs_0_
  153.1 0.7 collective-permute-done.19.refs_1_
  153.9 3.2 %collective-permute-start.23 = (bf16[128,1024]{1,0:T(8,128)(2,1)S(1)}, bf16[128,1024]{1,0:T(8,128)(2,1)S(1)}, u32[]{:S(2)}, u32[]{:S(2)}) collective-permute-start(bf16[128,1024]{1,0:T(8,128)(2,1)S(1)} %slice.21), channel_id=1, source_target_pairs={{0,3},{1,0},{2,1},{3,2},{4,7},{5,4},{6,5},{7,6},{8,11},{9,8},{10,9... | collective-permute-start | bytes 786440 | tf_op jit(solution)/shard_map/ppermute | solution.py:591
  157.1 1.5 collective-permute-done.24.refs_2_
  158.7 0.7 collective-permute-done.25.refs_3_
  159.4 0.7 copy-done.12
  160.1 2.9 %join.3 = bf16[2048,1024]{1,0:T(8,128)(2,1)} custom-call(s32[5]{0:T(128)} %stack.23.place, bf16[256,1024]{1,0:T(8,128)(2,1)} %copy-done.7, bf16[256,1024]{1,0:T(8,128)(2,1)} %copy-done.8, bf16[128,1024]{1,0:T(8,128)(2,1)} %copy-done.11, bf16[128,1024]{1,0:T(8,128)(2,1)} %copy-done.12, bf16[2048,1024]{1,0:T(8,128)(2,1)} %join.2.refs_4_), custom_call_target="tpu_custom_call", output_to_operand_aliasing={{}: (5, {})} | custom-call | tf_op jit(solution)/shard_map/join/pallas_call | solution.py:538
  163.0 0.2 collective-permute-done.22
  163.2 0.7 constant_dynamic-update-slice_fusion
  163.9 0.7 constant_dynamic-update-slice_fusion.1
  (72 shorter events, 0.8 us)
Async XLA Ops:
  4.3 9.7 %copy-start.21 = (bf16[1024]{0:T(1024)(128)(2,1)S(1)}, bf16[1024]{0:T(1024)(128)(2,1)}, u32[]{:S(2)}) copy-start(bf16[1024]{0:T(1024)(128)(2,1)} %param.18) | copy-start | bytes 6148
  4.3 10.3 %copy-start.20 = (s32[2048]{0:T(1024)S(1)}, s32[2048]{0:T(1024)}, u32[]{:S(2)}) copy-start(s32[2048]{0:T(1024)} %param.31) | copy-start | bytes 24580
  4.3 10.3 %copy-start.19 = (f32[2048,2]{0,1:T(2,128)S(1)}, f32[2048,2]{0,1:T(2,128)}, u32[]{:S(2)}) copy-start(f32[2048,2]{0,1:T(2,128)} %param.24) | copy-start | bytes 49156
  4.3 59.8 %collective-permute-start = (bf16[592,1024]{1,0:T(8,128)(2,1)}, bf16[592,1024]{1,0:T(8,128)(2,1)S(1)}, u32[]{:S(2)}, u32[]{:S(2)}) collective-permute-start(bf16[592,1024]{1,0:T(8,128)(2,1)} %cut_weights.2), channel_id=1, source_target_pairs={{0,1},{1,2},{2,3},{3,0},{4,5},{5,6},{6,7},{7,4},{8,9},{9,10},{10,1... | collective-permute-start | bytes 3637256 | tf_op jit(solution)/shard_map/ppermute | solution.py:591
  9.0 55.1 %collective-permute-start.1 = (bf16[592,1024]{1,0:T(8,128)(2,1)}, bf16[592,1024]{1,0:T(8,128)(2,1)S(1)}, u32[]{:S(2)}, u32[]{:S(2)}) collective-permute-start(bf16[592,1024]{1,0:T(8,128)(2,1)} %cut_weights.3), channel_id=1, source_target_pairs={{0,3},{1,0},{2,1},{3,2},{4,7},{5,4},{6,5},{7,6},{8,11},{9,8},{10,9... | collective-permute-start | bytes 3637256 | tf_op jit(solution)/shard_map/ppermute | solution.py:591
  10.7 53.4 %collective-permute-start.2 = (bf16[592,1024]{1,0:T(8,128)(2,1)}, bf16[592,1024]{1,0:T(8,128)(2,1)}, u32[]{:S(2)}, u32[]{:S(2)}) collective-permute-start(bf16[592,1024]{1,0:T(8,128)(2,1)} %cut_weights.3), channel_id=1, source_target_pairs={{0,1},{1,2},{2,3},{3,0},{4,5},{5,6},{6,7},{7,4},{8,9},{9,10},{10,1... | collective-permute-start | bytes 3637256 | tf_op jit(solution)/shard_map/ppermute | solution.py:591
  11.1 53.0 %collective-permute-start.3 = (bf16[592,1024]{1,0:T(8,128)(2,1)}, bf16[592,1024]{1,0:T(8,128)(2,1)}, u32[]{:S(2)}, u32[]{:S(2)}) collective-permute-start(bf16[592,1024]{1,0:T(8,128)(2,1)} %cut_weights.2), channel_id=1, source_target_pairs={{0,3},{1,0},{2,1},{3,2},{4,7},{5,4},{6,5},{7,6},{8,11},{9,8},{10,9... | collective-permute-start | bytes 3637256 | tf_op jit(solution)/shard_map/ppermute | solution.py:591
  15.3 18.5 %copy-start.22 = (bf16[1024]{0:T(1024)(128)(2,1)S(1)}, bf16[1024]{0:T(1024)(128)(2,1)}, u32[]{:S(2)}) copy-start(bf16[1024]{0:T(1024)(128)(2,1)} %param.27) | copy-start | bytes 6148
  28.3 14.5 %all-to-all-start = ((bf16[8,264,128]{2,1,0:T(8,128)(2,1)}), bf16[8,264,128]{2,1,0:T(8,128)(2,1)S(1)}, u32[]{:S(2)}, u32[]{:S(2)}) async-start(bf16[8,264,128]{2,1,0:T(8,128)(2,1)} %get-tuple-element.72), calls=%async_computation | async-start | bytes 1081344 | tf_op jit(solution)/shard_map/all_to_all | solution.py:611
  42.8 0.8 copy-start.6
  45.7 11.0 %all-to-all-start.1 = ((bf16[4,264,128]{2,1,0:T(8,128)(2,1)}), bf16[4,264,128]{2,1,0:T(8,128)(2,1)S(1)}, u32[]{:S(2)}, u32[]{:S(2)}) async-start(bf16[4,264,128]{2,1,0:T(8,128)(2,1)} %get-tuple-element.81), calls=%async_computation.1 | async-start | bytes 540672 | tf_op jit(solution)/shard_map/all_to_all | solution.py:611
  56.7 0.7 copy-start.5
  57.4 89.2 %all-to-all-start.2 = ((bf16[32,136,512]{2,1,0:T(8,128)(2,1)}), bf16[32,136,512]{2,1,0:T(8,128)(2,1)}, u32[]{:S(2)}, u32[]{:S(2)}) async-start(bf16[32,136,512]{2,1,0:T(8,128)(2,1)} %get-tuple-element.126), calls=%async_computation.2 | async-start | bytes 8912896 | tf_op jit(solution)/shard_map/all_to_all | solution.py:621
  64.1 15.4 %copy-start = (bf16[592,1024]{1,0:T(8,128)(2,1)}, bf16[592,1024]{1,0:T(8,128)(2,1)S(1)}, u32[]{:S(2)}) copy-start(bf16[592,1024]{1,0:T(8,128)(2,1)S(1)} %collective-permute-done.rest_8_) | copy-start | bytes 3637252
  64.1 15.4 %copy-start.1 = (bf16[592,1024]{1,0:T(8,128)(2,1)}, bf16[592,1024]{1,0:T(8,128)(2,1)S(1)}, u32[]{:S(2)}) copy-start(bf16[592,1024]{1,0:T(8,128)(2,1)S(1)} %collective-permute-done.1.rest_11_) | copy-start | bytes 3637252
  64.1 3.2 %collective-permute-start.4 = (bf16[592,1024]{1,0:T(8,128)(2,1)S(1)}, bf16[592,1024]{1,0:T(8,128)(2,1)S(1)}, u32[]{:S(2)}, u32[]{:S(2)}) collective-permute-start(bf16[592,1024]{1,0:T(8,128)(2,1)S(1)} %collective-permute-done.rest_8_), channel_id=1, source_target_pairs={{0,4},{4,0},{8,12},{12,8},{16,20},{20,16},{24,28},{28,24},{32,36},... | collective-permute-start | bytes 3637256 | tf_op jit(solution)/shard_map/ppermute | solution.py:592
  64.4 15.1 %collective-permute-start.5 = (bf16[592,1024]{1,0:T(8,128)(2,1)S(1)}, bf16[592,1024]{1,0:T(8,128)(2,1)}, u32[]{:S(2)}, u32[]{:S(2)}) collective-permute-start(bf16[592,1024]{1,0:T(8,128)(2,1)S(1)} %collective-permute-done.1.rest_11_), channel_id=1, source_target_pairs={{0,4},{4,0},{8,12},{12,8},{16,20},{20,16},{24,28},{28,24},{32,36},... | collective-permute-start | bytes 3637256 | tf_op jit(solution)/shard_map/ppermute | solution.py:592
  64.7 14.8 %collective-permute-start.6 = (bf16[592,1024]{1,0:T(8,128)(2,1)}, bf16[592,1024]{1,0:T(8,128)(2,1)}, u32[]{:S(2)}, u32[]{:S(2)}) collective-permute-start(bf16[592,1024]{1,0:T(8,128)(2,1)} %collective-permute-done.2.rest_9_), channel_id=1, source_target_pairs={{0,4},{4,0},{8,12},{12,8},{16,20},{20,16},{24,28},{28,24},{32,36},... | collective-permute-start | bytes 3637256 | tf_op jit(solution)/shard_map/ppermute | solution.py:592
  64.9 14.6 %collective-permute-start.7 = (bf16[592,1024]{1,0:T(8,128)(2,1)}, bf16[592,1024]{1,0:T(8,128)(2,1)}, u32[]{:S(2)}, u32[]{:S(2)}) collective-permute-start(bf16[592,1024]{1,0:T(8,128)(2,1)} %collective-permute-done.3.rest_10_), channel_id=1, source_target_pairs={{0,4},{4,0},{8,12},{12,8},{16,20},{20,16},{24,28},{28,24},{32,36},... | collective-permute-start | bytes 3637256 | tf_op jit(solution)/shard_map/ppermute | solution.py:592
  65.2 38.8 %collective-permute-start.11 = (bf16[592,1024]{1,0:T(8,128)(2,1)S(1)}, bf16[592,1024]{1,0:T(8,128)(2,1)}, u32[]{:S(2)}, u32[]{:S(2)}) collective-permute-start(bf16[592,1024]{1,0:T(8,128)(2,1)S(1)} %collective-permute-done.rest_8_), channel_id=1, source_target_pairs={{0,1},{1,2},{2,3},{3,0},{4,5},{5,6},{6,7},{7,4},{8,9},{9,10},{10,1... | collective-permute-start | bytes 3637256 | tf_op jit(solution)/shard_map/ppermute | solution.py:591
  67.3 1.0 copy-start.2
  68.4 35.6 %collective-permute-start.12 = (bf16[592,1024]{1,0:T(8,128)(2,1)S(1)}, bf16[592,1024]{1,0:T(8,128)(2,1)}, u32[]{:S(2)}, u32[]{:S(2)}) collective-permute-start(bf16[592,1024]{1,0:T(8,128)(2,1)S(1)} %collective-permute-done.1.rest_11_), channel_id=1, source_target_pairs={{0,3},{1,0},{2,1},{3,2},{4,7},{5,4},{6,5},{7,6},{8,11},{9,8},{10,9... | collective-permute-start | bytes 3637256 | tf_op jit(solution)/shard_map/ppermute | solution.py:591
  79.5 19.1 %collective-permute-start.8 = (bf16[256,256]{1,0:T(8,128)(2,1)}, bf16[256,256]{1,0:T(8,128)(2,1)S(1)}, u32[]{:S(2)}, u32[]{:S(2)}) collective-permute-start(bf16[256,256]{1,0:T(8,128)(2,1)} %get-tuple-element.101), channel_id=1, source_target_pairs={{0,1},{1,2},{2,3},{3,0},{4,5},{5,6},{6,7},{7,4},{8,9},{9,10},{10,1... | collective-permute-start | bytes 393224 | tf_op jit(solution)/shard_map/ppermute | solution.py:591
  79.8 24.2 %collective-permute-start.9 = (bf16[256,256]{1,0:T(8,128)(2,1)}, bf16[256,256]{1,0:T(8,128)(2,1)S(1)}, u32[]{:S(2)}, u32[]{:S(2)}) collective-permute-start(bf16[256,256]{1,0:T(8,128)(2,1)} %get-tuple-element.102), channel_id=1, source_target_pairs={{0,3},{1,0},{2,1},{3,2},{4,7},{5,4},{6,5},{7,6},{8,11},{9,8},{10,9... | collective-permute-start | bytes 393224 | tf_op jit(solution)/shard_map/ppermute | solution.py:591
  83.0 21.0 %collective-permute-start.10 = (bf16[256,256]{1,0:T(8,128)(2,1)}, bf16[256,256]{1,0:T(8,128)(2,1)S(1)}, u32[]{:S(2)}, u32[]{:S(2)}) collective-permute-start(bf16[256,256]{1,0:T(8,128)(2,1)} %get-tuple-element.103), channel_id=1, source_target_pairs={{0,2},{1,3},{2,0},{3,1},{4,6},{5,7},{6,4},{7,5},{8,10},{9,11},{10,... | collective-permute-start | bytes 393224 | tf_op jit(solution)/shard_map/ppermute | solution.py:591
  98.6 11.1 %copy-start.13 = (bf16[256,256]{1,0:T(8,128)(2,1)}, bf16[256,256]{1,0:T(8,128)(2,1)S(1)}, u32[]{:S(2)}) copy-start(bf16[256,256]{1,0:T(8,128)(2,1)S(1)} %collective-permute-done.8.rest_1_) | copy-start | bytes 393220
  104.0 5.8 %copy-start.14 = (bf16[256,256]{1,0:T(8,128)(2,1)}, bf16[256,256]{1,0:T(8,128)(2,1)S(1)}, u32[]{:S(2)}) copy-start(bf16[256,256]{1,0:T(8,128)(2,1)S(1)} %collective-permute-done.9.rest_2_) | copy-start | bytes 393220
  104.0 5.8 %copy-start.15 = (bf16[256,256]{1,0:T(8,128)(2,1)}, bf16[256,256]{1,0:T(8,128)(2,1)S(1)}, u32[]{:S(2)}) copy-start(bf16[256,256]{1,0:T(8,128)(2,1)S(1)} %collective-permute-done.10.rest_3_) | copy-start | bytes 393220
  104.0 4.2 %collective-permute-start.13 = (bf16[592,1024]{1,0:T(8,128)(2,1)}, bf16[592,1024]{1,0:T(8,128)(2,1)S(1)}, u32[]{:S(2)}, u32[]{:S(2)}) collective-permute-start(bf16[592,1024]{1,0:T(8,128)(2,1)} %collective-permute-done.11.rest_12_), channel_id=1, source_target_pairs={{0,4},{4,0},{8,12},{12,8},{16,20},{20,16},{24,28},{28,24},{32,36},... | collective-permute-start | bytes 3637256 | tf_op jit(solution)/shard_map/ppermute | solution.py:592
  104.1 4.8 %collective-permute-start.14 = (bf16[592,1024]{1,0:T(8,128)(2,1)}, bf16[592,1024]{1,0:T(8,128)(2,1)S(1)}, u32[]{:S(2)}, u32[]{:S(2)}) collective-permute-start(bf16[592,1024]{1,0:T(8,128)(2,1)} %collective-permute-done.12.rest_13_), channel_id=1, source_target_pairs={{0,4},{4,0},{8,12},{12,8},{16,20},{20,16},{24,28},{28,24},{32,36},... | collective-permute-start | bytes 3637256 | tf_op jit(solution)/shard_map/ppermute | solution.py:592
  104.6 16.9 %collective-permute-start.15 = (bf16[256,256]{1,0:T(8,128)(2,1)}, bf16[256,256]{1,0:T(8,128)(2,1)S(1)}, u32[]{:S(2)}, u32[]{:S(2)}) collective-permute-start(bf16[256,256]{1,0:T(8,128)(2,1)} %get-tuple-element.118), channel_id=1, source_target_pairs={{0,1},{1,2},{2,3},{3,0},{4,5},{5,6},{6,7},{7,4},{8,9},{9,10},{10,1... | collective-permute-start | bytes 393224 | tf_op jit(solution)/shard_map/ppermute | solution.py:591
  106.3 15.2 %collective-permute-start.16 = (bf16[256,256]{1,0:T(8,128)(2,1)}, bf16[256,256]{1,0:T(8,128)(2,1)S(1)}, u32[]{:S(2)}, u32[]{:S(2)}) collective-permute-start(bf16[256,256]{1,0:T(8,128)(2,1)} %get-tuple-element.119), channel_id=1, source_target_pairs={{0,3},{1,0},{2,1},{3,2},{4,7},{5,4},{6,5},{7,6},{8,11},{9,8},{10,9... | collective-permute-start | bytes 393224 | tf_op jit(solution)/shard_map/ppermute | solution.py:591
  108.2 1.6 copy-start.3
  108.9 1.0 copy-start.4
  108.9 12.6 %collective-permute-start.17 = (bf16[256,256]{1,0:T(8,128)(2,1)}, bf16[256,256]{1,0:T(8,128)(2,1)S(1)}, u32[]{:S(2)}, u32[]{:S(2)}) collective-permute-start(bf16[256,256]{1,0:T(8,128)(2,1)} %get-tuple-element.120), channel_id=1, source_target_pairs={{0,2},{1,3},{2,0},{3,1},{4,6},{5,7},{6,4},{7,5},{8,10},{9,11},{10,... | collective-permute-start | bytes 393224 | tf_op jit(solution)/shard_map/ppermute | solution.py:591
  121.5 3.8 %copy-start.16 = (bf16[256,256]{1,0:T(8,128)(2,1)}, bf16[256,256]{1,0:T(8,128)(2,1)S(1)}, u32[]{:S(2)}) copy-start(bf16[256,256]{1,0:T(8,128)(2,1)S(1)} %collective-permute-done.15.rest_1_) | copy-start | bytes 393220
  121.5 3.8 %copy-start.17 = (bf16[256,256]{1,0:T(8,128)(2,1)}, bf16[256,256]{1,0:T(8,128)(2,1)S(1)}, u32[]{:S(2)}) copy-start(bf16[256,256]{1,0:T(8,128)(2,1)S(1)} %collective-permute-done.16.rest_2_) | copy-start | bytes 393220
  121.5 3.8 %copy-start.18 = (bf16[256,256]{1,0:T(8,128)(2,1)}, bf16[256,256]{1,0:T(8,128)(2,1)S(1)}, u32[]{:S(2)}) copy-start(bf16[256,256]{1,0:T(8,128)(2,1)S(1)} %collective-permute-done.17.rest_3_) | copy-start | bytes 393220
  121.5 18.6 %collective-permute-start.20 = (bf16[256,1024]{1,0:T(8,128)(2,1)}, bf16[256,1024]{1,0:T(8,128)(2,1)S(1)}, u32[]{:S(2)}, u32[]{:S(2)}) collective-permute-start(bf16[256,1024]{1,0:T(8,128)(2,1)} %ffn.2.refs_0_), channel_id=1, source_target_pairs={{0,1},{1,2},{2,3},{3,0},{4,5},{5,6},{6,7},{7,4},{8,9},{9,10},{10,1... | collective-permute-start | bytes 1572872 | tf_op jit(solution)/shard_map/ppermute | solution.py:591
  125.0 15.7 %collective-permute-start.21 = (bf16[256,1024]{1,0:T(8,128)(2,1)}, bf16[256,1024]{1,0:T(8,128)(2,1)S(1)}, u32[]{:S(2)}, u32[]{:S(2)}) collective-permute-start(bf16[256,1024]{1,0:T(8,128)(2,1)} %ffn.2.refs_0_), channel_id=1, source_target_pairs={{0,3},{1,0},{2,1},{3,2},{4,7},{5,4},{6,5},{7,6},{8,11},{9,8},{10,9... | collective-permute-start | bytes 1572872 | tf_op jit(solution)/shard_map/ppermute | solution.py:591
  136.8 16.3 %collective-permute-start.18 = (bf16[256,1024]{1,0:T(8,128)(2,1)}, bf16[256,1024]{1,0:T(8,128)(2,1)S(1)}, u32[]{:S(2)}, u32[]{:S(2)}) collective-permute-start(bf16[256,1024]{1,0:T(8,128)(2,1)} %ffn.3.refs_3_), channel_id=1, source_target_pairs={{0,1},{1,2},{2,3},{3,0},{4,5},{5,6},{6,7},{7,4},{8,9},{9,10},{10,1... | collective-permute-start | bytes 1572872 | tf_op jit(solution)/shard_map/ppermute | solution.py:591
  138.6 15.1 %collective-permute-start.19 = (bf16[256,1024]{1,0:T(8,128)(2,1)}, bf16[256,1024]{1,0:T(8,128)(2,1)S(1)}, u32[]{:S(2)}, u32[]{:S(2)}) collective-permute-start(bf16[256,1024]{1,0:T(8,128)(2,1)} %ffn.3.refs_3_), channel_id=1, source_target_pairs={{0,3},{1,0},{2,1},{3,2},{4,7},{5,4},{6,5},{7,6},{8,11},{9,8},{10,9... | collective-permute-start | bytes 1572872 | tf_op jit(solution)/shard_map/ppermute | solution.py:591
  140.1 3.4 %copy-start.9 = (bf16[256,1024]{1,0:T(8,128)(2,1)}, bf16[256,1024]{1,0:T(8,128)(2,1)S(1)}, u32[]{:S(2)}) copy-start(bf16[256,1024]{1,0:T(8,128)(2,1)S(1)} %collective-permute-done.20.refs_1_) | copy-start | bytes 1572868
  140.1 18.6 %collective-permute-start.24 = (bf16[128,1024]{1,0:T(8,128)(2,1)S(1)}, bf16[128,1024]{1,0:T(8,128)(2,1)S(1)}, u32[]{:S(2)}, u32[]{:S(2)}) collective-permute-start(bf16[128,1024]{1,0:T(8,128)(2,1)S(1)} %slice.25), channel_id=1, source_target_pairs={{0,1},{1,2},{2,3},{3,0},{4,5},{5,6},{6,7},{7,4},{8,9},{9,10},{10,1... | collective-permute-start | bytes 786440 | tf_op jit(solution)/shard_map/ppermute | solution.py:591
  140.8 2.7 %copy-start.10 = (bf16[256,1024]{1,0:T(8,128)(2,1)}, bf16[256,1024]{1,0:T(8,128)(2,1)S(1)}, u32[]{:S(2)}) copy-start(bf16[256,1024]{1,0:T(8,128)(2,1)S(1)} %collective-permute-done.21.refs_2_) | copy-start | bytes 1572868
  140.8 18.5 %collective-permute-start.25 = (bf16[128,1024]{1,0:T(8,128)(2,1)S(1)}, bf16[128,1024]{1,0:T(8,128)(2,1)S(1)}, u32[]{:S(2)}, u32[]{:S(2)}) collective-permute-start(bf16[128,1024]{1,0:T(8,128)(2,1)S(1)} %slice.26), channel_id=1, source_target_pairs={{0,3},{1,0},{2,1},{3,2},{4,7},{5,4},{6,5},{7,6},{8,11},{9,8},{10,9... | collective-permute-start | bytes 786440 | tf_op jit(solution)/shard_map/ppermute | solution.py:591
  153.1 6.3 %copy-start.7 = (bf16[256,1024]{1,0:T(8,128)(2,1)}, bf16[256,1024]{1,0:T(8,128)(2,1)S(1)}, u32[]{:S(2)}) copy-start(bf16[256,1024]{1,0:T(8,128)(2,1)S(1)} %collective-permute-done.18.refs_0_) | copy-start | bytes 1572868
  153.7 5.6 %copy-start.8 = (bf16[256,1024]{1,0:T(8,128)(2,1)}, bf16[256,1024]{1,0:T(8,128)(2,1)S(1)}, u32[]{:S(2)}) copy-start(bf16[256,1024]{1,0:T(8,128)(2,1)S(1)} %collective-permute-done.19.refs_1_) | copy-start | bytes 1572868
  153.7 9.4 %collective-permute-start.22 = (bf16[128,1024]{1,0:T(8,128)(2,1)S(1)}, bf16[128,1024]{1,0:T(8,128)(2,1)S(1)}, u32[]{:S(2)}, u32[]{:S(2)}) collective-permute-start(bf16[128,1024]{1,0:T(8,128)(2,1)S(1)} %slice.20), channel_id=1, source_target_pairs={{0,1},{1,2},{2,3},{3,0},{4,5},{5,6},{6,7},{7,4},{8,9},{9,10},{10,1... | collective-permute-start | bytes 786440 | tf_op jit(solution)/shard_map/ppermute | solution.py:591
  153.9 9.3 %collective-permute-start.23 = (bf16[128,1024]{1,0:T(8,128)(2,1)S(1)}, bf16[128,1024]{1,0:T(8,128)(2,1)S(1)}, u32[]{:S(2)}, u32[]{:S(2)}) collective-permute-start(bf16[128,1024]{1,0:T(8,128)(2,1)S(1)} %slice.21), channel_id=1, source_target_pairs={{0,3},{1,0},{2,1},{3,2},{4,7},{5,4},{6,5},{7,6},{8,11},{9,8},{10,9... | collective-permute-start | bytes 786440 | tf_op jit(solution)/shard_map/ppermute | solution.py:591
  158.7 0.7 copy-start.11
  159.4 0.7 copy-start.12

commit v5 on v3

--- a/solution.py
+++ b/solution.py
@@ -629,8 +629,10 @@
     tied = tie(*out1, *heads0)
     p2, q2, _ = tie(p2, q2, tied[0])
     out1, heads0 = tied[:4], tied[4:]
-    heads1 = send(out1)
     p2x, q2x = swap(p2), swap(q2)
+    early = shift(out1[1], 1), shift(out1[3], 3)
+    far, p2x, q2x = tie(out1[2], p2x, q2x)
+    heads1 = [out1[0], *early, shift(far, 2)]
     mine, other = [p1, q1w, p3, q3, p2, q2], [p1x, q1x, p3x, q3x, p2x, q2x]
 
     slots = arrived[:, PAGE, 0].astype(F32)

time: 164 us -> 164 us (level)
  starting transfers between devices: 48 us -> 50.9 us
  waiting for transfers between devices: 23.9 us -> 21.7 us
    ppermute x20, starting transfers between devices: 30 us -> 32.8 us  [on_device(): lax.ppermute(a, 'tp', [(i, (i + d) % 4) for i in range(4)])]
    unnamed x44 -> x46, local copies, waits for them, and re-layouts: 4.97 us -> 3.57 us
  transfers between devices with their start and end apart: 29 -> 29, of which waited for: 7 -> 11; matrix products, arithmetic and copies ran while one was open for 3% -> 3% of each run, Pallas kernels for 46% -> 46%
where the time goes in v5:
time: 164 us; the launch traced here: 163 us
  Pallas kernels  78.7 us (48%)
  starting transfers between devices  50.9 us (31%)
  waiting for transfers between devices  21.7 us (13%)
  local copies, waits for them, and re-layouts  7.11 us (4%)
  other arithmetic  3.22 us (2%)
    ppermute x20, starting transfers between devices, on_device(): lax.ppermute(a, 'tp', [(i, (i + d) % 4) for i in range(4)])  32.8 us
    pallas_call x2, Pallas kernels, ffn(): pl.pallas_call(functools.partial(ffn_kernel, half), grid_spec=gs, out_sha...  23 us
    ppermute x20, waiting for transfers between devices, on_device(): lax.ppermute(a, 'tp', [(i, (i + d) % 4) for i in range(4)])  17.8 us
    pallas_call x2, Pallas kernels, recall(): pl.pallas_call(functools.partial(recall_kernel, half), grid_spec=gs, out_...  14.9 us
    pallas_call x1, Pallas kernels, project(): pl.pallas_call(project_kernel, grid_spec=gs, out_shape=[jax.ShapeDtypeStr...  13 us
    pallas_call x2, Pallas kernels, attend(): pl.pallas_call(attend_kernel, grid=(heads,), in_specs=[pl.BlockSpec((SEG,...  12.6 us
    all_to_all x2, starting transfers between devices, on_device(): lax.all_to_all(a, 'req', 0, 0, tiled=True, axis_index_groups=g)  9.74 us
    all_to_all x1, starting transfers between devices, on_device(): arrived = lax.all_to_all(outgoing, 'req', 0, 0, tiled=True)  6.66 us
  transfers between devices with their start and end apart: 29, of which 11 were waited for; matrix products, arithmetic and copies ran while one was open for 3% of the time, Pallas kernels for 46%

profile of v5, /device:TPU:32, one launch (start us, length us, event | category | flops | bytes accessed | tf_op | source)
XLA Modules:
  0.0 162.5 jit_solution(9570224502446650499)
XLA Ops:
  0.7 0.7 stack.23.place
  1.3 3.9 %cut_weights.1 = (bf16[592,1024]{1,0:T(8,128)(2,1)}, bf16[592,1024]{1,0:T(8,128)(2,1)}) custom-call(s32[5]{0:T(128)} %stack.23.place, bf16[704,1024]{1,0:T(8,128)(2,1)} %bitcast.10, bf16[704,1024]{1,0:T(8,128)(2,1)} %bitcast.13, bf16[704,1024]{1,0:T(8,128)(2,1)} %rest_6_.3, bf16[256,1024]{1,0:T(8,128)(2,1)} %rest_7_.3), custom_call_target="tpu_custom_call" | custom-call | tf_op jit(solution)/shard_map/cut_weights/pallas_call | solution.py:568
  5.2 1.6 %collective-permute-start = (bf16[592,1024]{1,0:T(8,128)(2,1)}, bf16[592,1024]{1,0:T(8,128)(2,1)S(1)}, u32[]{:S(2)}, u32[]{:S(2)}) collective-permute-start(bf16[592,1024]{1,0:T(8,128)(2,1)} %get-tuple-element.89), channel_id=1, source_target_pairs={{0,1},{1,2},{2,3},{3,0},{4,5},{5,6},{6,7},{7,4},{8,9},{9,10},{10,1... | collective-permute-start | bytes 3637256 | tf_op jit(solution)/shard_map/ppermute | solution.py:587
  6.9 1.7 %collective-permute-start.1 = (bf16[592,1024]{1,0:T(8,128)(2,1)}, bf16[592,1024]{1,0:T(8,128)(2,1)S(1)}, u32[]{:S(2)}, u32[]{:S(2)}) collective-permute-start(bf16[592,1024]{1,0:T(8,128)(2,1)} %get-tuple-element.90), channel_id=1, source_target_pairs={{0,3},{1,0},{2,1},{3,2},{4,7},{5,4},{6,5},{7,6},{8,11},{9,8},{10,9... | collective-permute-start | bytes 3637256 | tf_op jit(solution)/shard_map/ppermute | solution.py:587
  8.5 0.4 collective-permute-start.2
  8.9 2.9 %collective-permute-start.3 = (bf16[592,1024]{1,0:T(8,128)(2,1)}, bf16[592,1024]{1,0:T(8,128)(2,1)}, u32[]{:S(2)}, u32[]{:S(2)}) collective-permute-start(bf16[592,1024]{1,0:T(8,128)(2,1)} %get-tuple-element.89), channel_id=1, source_target_pairs={{0,3},{1,0},{2,1},{3,2},{4,7},{5,4},{6,5},{7,6},{8,11},{9,8},{10,9... | collective-permute-start | bytes 3637256 | tf_op jit(solution)/shard_map/ppermute | solution.py:587
  11.8 0.6 broadcast_in_dim.30.gain
  12.5 0.7 maximum_maximum_fusion.row
  13.2 13.0 %project.1 = (bf16[2048,256]{1,0:T(8,128)(2,1)}, bf16[2048,512]{1,0:T(8,128)(2,1)}, bf16[2048,256]{1,0:T(8,128)(2,1)}, f32[8,2,128,128]{3,2,1,0:T(8,128)}, bf16[...) custom-call(s32[16]{0:T(128)} %owner.1, s32[16]{0:T(128)} %slot.1, ...), custom_call_target="tpu_custom_call" | custom-call | tf_op jit(solution)/shard_map/project/pallas_call | solution.py:185
  26.1 5.5 %all-to-all-start = ((bf16[8,264,128]{2,1,0:T(8,128)(2,1)}), bf16[8,264,128]{2,1,0:T(8,128)(2,1)S(1)}, u32[]{:S(2)}, u32[]{:S(2)}) async-start(bf16[8,264,128]{2,1,0:T(8,128)(2,1)} %get-tuple-element.74), calls=%async_computation | async-start | bytes 1081344 | tf_op jit(solution)/shard_map/all_to_all | solution.py:605
  31.7 0.6 broadcast_in_dim.33.gain
  32.3 0.6 pad_maximum_fusion.bound
  32.9 6.3 %attend.2.at0 = f32[1024,256]{1,0:T(8,128)} custom-call(bf16[2048,256]{1,0:T(8,128)(2,1)} %get-tuple-element.84.q, bf16[2048,512]{1,0:T(8,128)(2,1)} %get-tuple-element.71.k.v.kv, bf16[2048,512]{1,0:T(8,128)(2,1)} %get-tuple-element.71.k.v.kv, bf16[16,256]{1,0:T(8,128)(2,1)} %pk.3, bf16[16,256]{1,0:T(8,128)(2,1)} %pv.3, f32[2048,8]{1,0:T(8,128)} %get-tuple-element.72.col, ...), custom_call_target="tpu_custom_call" | custom-call | flops 1400000000 | bytes 4000000 | tf_op jit(solution)/shard_map/attend/pallas_call | solution.py:270
  39.2 1.5 all-to-all-done.got
  40.7 0.8 copy-done.6
  41.5 2.0 %combine.1 = (f32[2,128,128]{2,1,0:T(8,128)}, f32[8,128]{1,0:T(8,128)}, bf16[4,264,128]{2,1,0:T(8,128)(2,1)}) custom-call(s32[5]{0:T(128)} %stack.23.place, bf16[8,264,128]{2,1,0:T(8,128)(2,1)} %copy-done.6), custom_call_target="tpu_custom_call" | custom-call | tf_op jit(solution)/shard_map/combine/pallas_call | solution.py:227
  43.5 4.3 %all-to-all-start.1 = ((bf16[4,264,128]{2,1,0:T(8,128)(2,1)}), bf16[4,264,128]{2,1,0:T(8,128)(2,1)S(1)}, u32[]{:S(2)}, u32[]{:S(2)}) async-start(bf16[4,264,128]{2,1,0:T(8,128)(2,1)} %get-tuple-element.83), calls=%async_computation.1 | async-start | bytes 540672 | tf_op jit(solution)/shard_map/all_to_all | solution.py:605
  47.8 6.3 %attend.3.at1 = f32[1024,256]{1,0:T(8,128)} custom-call(bf16[2048,256]{1,0:T(8,128)(2,1)} %get-tuple-element.84.q, bf16[2048,512]{1,0:T(8,128)(2,1)} %get-tuple-element.71.k.v.kv, bf16[2048,512]{1,0:T(8,128)(2,1)} %get-tuple-element.71.k.v.kv, bf16[16,256]{1,0:T(8,128)(2,1)} %pk.3, bf16[16,256]{1,0:T(8,128)(2,1)} %pv.3, f32[2048,8]{1,0:T(8,128)} %get-tuple-element.72.col, ...), custom_call_target="tpu_custom_call" | custom-call | flops 1400000000 | bytes 4000000 | tf_op jit(solution)/shard_map/attend/pallas_call | solution.py:270
  54.1 0.4 all-to-all-done.1.got
  54.5 0.7 copy-done.5
  55.2 6.7 %all-to-all-start.2 = ((bf16[32,136,512]{2,1,0:T(8,128)(2,1)}), bf16[32,136,512]{2,1,0:T(8,128)(2,1)}, u32[]{:S(2)}, u32[]{:S(2)}) async-start(bf16[32,136,512]{2,1,0:T(8,128)(2,1)} %get-tuple-element.130), calls=%async_computation.2 | async-start | bytes 8912896 | tf_op jit(solution)/shard_map/all_to_all | solution.py:615
  62.0 0.2 collective-permute-start.4
  62.2 0.4 collective-permute-start.5
  62.7 0.4 collective-permute-start.7
  63.1 0.8 collective-permute-start.11
  63.9 1.3 collective-permute-done.4.rest_14_
  65.2 1.0 copy-done.2
  66.2 3.7 %collective-permute-start.12 = (bf16[592,1024]{1,0:T(8,128)(2,1)S(1)}, bf16[592,1024]{1,0:T(8,128)(2,1)}, u32[]{:S(2)}, u32[]{:S(2)}) collective-permute-start(bf16[592,1024]{1,0:T(8,128)(2,1)S(1)} %collective-permute-done.1.rest_11_), channel_id=1, source_target_pairs={{0,3},{1,0},{2,1},{3,2},{4,7},{5,4},{6,5},{7,6},{8,11},{9,8},{10,9... | collective-permute-start | bytes 3637256 | tf_op jit(solution)/shard_map/ppermute | solution.py:587
  69.9 7.4 %recall.3 = (bf16[256,256]{1,0:T(8,128)(2,1)}, bf16[256,256]{1,0:T(8,128)(2,1)}, bf16[256,256]{1,0:T(8,128)(2,1)}, bf16[256,256]{1,0:T(8,128)(2,1)}) custom-call(s32[5]{0:T(128)} %stack.23.place, f32[8]{0:T(128)} %pad_maximum_fusion.bound, bf16[2048,256]{1,0:T(8,128)(2,1)} %get-tuple-element.84.q, bf16[2048,256]{1,0:T(8,128)(2,1)} %get-tuple-element.77.ku, ...), custom_call_target="tpu_custom_call" | custom-call | flops 400000000 | bytes 4000000 | tf_op jit(solution)/shard_map/recall/pallas_call | solution.py:372
  77.4 0.3 collective-permute-start.8
  77.7 3.2 %collective-permute-start.9 = (bf16[256,256]{1,0:T(8,128)(2,1)}, bf16[256,256]{1,0:T(8,128)(2,1)S(1)}, u32[]{:S(2)}, u32[]{:S(2)}) collective-permute-start(bf16[256,256]{1,0:T(8,128)(2,1)} %get-tuple-element.106), channel_id=1, source_target_pairs={{0,3},{1,0},{2,1},{3,2},{4,7},{5,4},{6,5},{7,6},{8,11},{9,8},{10,9... | collective-permute-start | bytes 393224 | tf_op jit(solution)/shard_map/ppermute | solution.py:587
  80.9 7.5 %recall.2 = (bf16[256,256]{1,0:T(8,128)(2,1)}, bf16[256,256]{1,0:T(8,128)(2,1)}, bf16[256,256]{1,0:T(8,128)(2,1)}, bf16[256,256]{1,0:T(8,128)(2,1)}) custom-call(s32[5]{0:T(128)} %stack.23.place, f32[8]{0:T(128)} %pad_maximum_fusion.bound, bf16[2048,256]{1,0:T(8,128)(2,1)} %get-tuple-element.84.q, bf16[2048,256]{1,0:T(8,128)(2,1)} %get-tuple-element.77.ku, ...), custom_call_target="tpu_custom_call" | custom-call | flops 400000000 | bytes 4000000 | tf_op jit(solution)/shard_map/recall/pallas_call | solution.py:372
  88.4 8.1 %collective-permute-done.8.rest_1_ = bf16[256,256]{1,0:T(8,128)(2,1)S(1)} collective-permute-done((bf16[256,256]{1,0:T(8,128)(2,1)}, bf16[256,256]{1,0:T(8,128)(2,1)S(1)}, u32[]{:S(2)}, u32[]{:S(2)}) %collective-permute-start.8) | collective-permute-done | bytes 131104 | tf_op jit(solution)/shard_map/ppermute | solution.py:587
  96.4 5.4 %collective-permute-done.9.rest_2_ = bf16[256,256]{1,0:T(8,128)(2,1)S(1)} collective-permute-done((bf16[256,256]{1,0:T(8,128)(2,1)}, bf16[256,256]{1,0:T(8,128)(2,1)S(1)}, u32[]{:S(2)}, u32[]{:S(2)}) %collective-permute-start.9) | collective-permute-done | bytes 131104 | tf_op jit(solution)/shard_map/ppermute | solution.py:587
  102.0 0.5 collective-permute-start.14
  102.5 1.6 %collective-permute-start.15 = (bf16[256,256]{1,0:T(8,128)(2,1)}, bf16[256,256]{1,0:T(8,128)(2,1)S(1)}, u32[]{:S(2)}, u32[]{:S(2)}) collective-permute-start(bf16[256,256]{1,0:T(8,128)(2,1)} %get-tuple-element.122), channel_id=1, source_target_pairs={{0,1},{1,2},{2,3},{3,0},{4,5},{5,6},{6,7},{7,4},{8,9},{9,10},{10,1... | collective-permute-start | bytes 393224 | tf_op jit(solution)/shard_map/ppermute | solution.py:587
  104.1 1.9 %collective-permute-start.16 = (bf16[256,256]{1,0:T(8,128)(2,1)}, bf16[256,256]{1,0:T(8,128)(2,1)S(1)}, u32[]{:S(2)}, u32[]{:S(2)}) collective-permute-start(bf16[256,256]{1,0:T(8,128)(2,1)} %get-tuple-element.123), channel_id=1, source_target_pairs={{0,3},{1,0},{2,1},{3,2},{4,7},{5,4},{6,5},{7,6},{8,11},{9,8},{10,9... | collective-permute-start | bytes 393224 | tf_op jit(solution)/shard_map/ppermute | solution.py:587
  106.1 0.7 collective-permute-done.14.rest_19_
  106.8 0.8 collective-permute-start.17
  107.7 0.2 copy-done.4
  107.9 11.5 %ffn.2.refs_0_ = bf16[256,1024]{1,0:T(8,128)(2,1)} custom-call(s32[5]{0:T(128)} %stack.23.place, bf16[1,1024]{1,0:T(2,128)(2,1)} %broadcast_in_dim.33.gain, bf16[2048,1024]{1,0:T(8,128)(2,1)} %tokens.3, bf16[256,256]{1,0:T(8,128)(2,1)} %get-tuple-element.108.rest_0_, bf16[256,256]{1,0:T(8,128)(2,1)} %copy-done.13, bf16[256,256]{1,0:T(8,128)(2,1)} %copy-done.14, ...), custom_call_target="tpu_custom_call" | custom-call | tf_op jit(solution)/shard_map/ffn/pallas_call | solution.py:481
  119.4 3.5 %collective-permute-start.20 = (bf16[256,1024]{1,0:T(8,128)(2,1)}, bf16[256,1024]{1,0:T(8,128)(2,1)S(1)}, u32[]{:S(2)}, u32[]{:S(2)}) collective-permute-start(bf16[256,1024]{1,0:T(8,128)(2,1)} %ffn.2.refs_0_), channel_id=1, source_target_pairs={{0,1},{1,2},{2,3},{3,0},{4,5},{5,6},{6,7},{7,4},{8,9},{9,10},{10,1... | collective-permute-start | bytes 1572872 | tf_op jit(solution)/shard_map/ppermute | solution.py:587
  122.9 0.2 collective-permute-start.21
  123.2 11.5 %ffn.3.refs_3_ = bf16[256,1024]{1,0:T(8,128)(2,1)} custom-call(s32[5]{0:T(128)} %stack.23.place, bf16[1,1024]{1,0:T(2,128)(2,1)} %broadcast_in_dim.33.gain, bf16[2048,1024]{1,0:T(8,128)(2,1)} %tokens.3, bf16[256,256]{1,0:T(8,128)(2,1)} %get-tuple-element.125.rest_0_, bf16[256,256]{1,0:T(8,128)(2,1)} %copy-done.16, bf16[256,256]{1,0:T(8,128)(2,1)} %copy-done.17, ...), custom_call_target="tpu_custom_call" | custom-call | tf_op jit(solution)/shard_map/ffn/pallas_call | solution.py:481
  134.7 1.9 %collective-permute-start.18 = (bf16[256,1024]{1,0:T(8,128)(2,1)}, bf16[256,1024]{1,0:T(8,128)(2,1)S(1)}, u32[]{:S(2)}, u32[]{:S(2)}) collective-permute-start(bf16[256,1024]{1,0:T(8,128)(2,1)} %ffn.3.refs_3_), channel_id=1, source_target_pairs={{0,1},{1,2},{2,3},{3,0},{4,5},{5,6},{6,7},{7,4},{8,9},{9,10},{10,1... | collective-permute-start | bytes 1572872 | tf_op jit(solution)/shard_map/ppermute | solution.py:587
  136.5 1.4 collective-permute-start.19
  138.0 0.7 collective-permute-start.24
  138.7 2.7 %collective-permute-start.25 = (bf16[128,1024]{1,0:T(8,128)(2,1)S(1)}, bf16[128,1024]{1,0:T(8,128)(2,1)S(1)}, u32[]{:S(2)}, u32[]{:S(2)}) collective-permute-start(bf16[128,1024]{1,0:T(8,128)(2,1)S(1)} %slice.26), channel_id=1, source_target_pairs={{0,3},{1,0},{2,1},{3,2},{4,7},{5,4},{6,5},{7,6},{8,11},{9,8},{10,9... | collective-permute-start | bytes 786440 | tf_op jit(solution)/shard_map/ppermute | solution.py:587
  141.4 3.1 %join.2.refs_4_ = bf16[2048,1024]{1,0:T(8,128)(2,1)} custom-call(s32[5]{0:T(128)} %stack.23.place, bf16[256,1024]{1,0:T(8,128)(2,1)} %ffn.2.refs_0_, bf16[256,1024]{1,0:T(8,128)(2,1)} %copy-done.9, bf16[256,1024]{1,0:T(8,128)(2,1)} %copy-done.10, bf16[256,1024]{1,0:T(8,128)(2,1)} %ffn.3.refs_3_), custom_call_target="tpu_custom_call" | custom-call | tf_op jit(solution)/shard_map/join/pallas_call | solution.py:538
  144.5 1.2 fusion
  145.7 0.2 select_reduce_fusion
  145.9 0.6 broadcast_clamp_fusion.source
  146.5 3.2 %place.1 = bf16[16,128,512]{2,1,0:T(8,128)(2,1)} custom-call(s32[16]{0:T(128)} %broadcast_clamp_fusion.source, bf16[32,136,512]{2,1,0:T(8,128)(2,1)} %all-to-all-done.2.got), custom_call_target="tpu_custom_call" | custom-call | tf_op jit(solution)/shard_map/place/pallas_call | solution.py:515
  149.7 1.3 collective-permute-done.18.refs_0_
  151.0 0.6 collective-permute-done.19.refs_1_
  151.6 0.2 collective-permute-start.22
  151.8 3.2 %collective-permute-start.23 = (bf16[128,1024]{1,0:T(8,128)(2,1)S(1)}, bf16[128,1024]{1,0:T(8,128)(2,1)S(1)}, u32[]{:S(2)}, u32[]{:S(2)}) collective-permute-start(bf16[128,1024]{1,0:T(8,128)(2,1)S(1)} %slice.21), channel_id=1, source_target_pairs={{0,3},{1,0},{2,1},{3,2},{4,7},{5,4},{6,5},{7,6},{8,11},{9,8},{10,9... | collective-permute-start | bytes 786440 | tf_op jit(solution)/shard_map/ppermute | solution.py:587
  155.0 1.6 collective-permute-done.24.refs_2_
  156.6 0.6 collective-permute-done.25.refs_3_
  157.3 0.7 copy-done.12
  158.0 2.9 %join.3 = bf16[2048,1024]{1,0:T(8,128)(2,1)} custom-call(s32[5]{0:T(128)} %stack.23.place, bf16[256,1024]{1,0:T(8,128)(2,1)} %copy-done.7, bf16[256,1024]{1,0:T(8,128)(2,1)} %copy-done.8, bf16[128,1024]{1,0:T(8,128)(2,1)} %copy-done.11, bf16[128,1024]{1,0:T(8,128)(2,1)} %copy-done.12, bf16[2048,1024]{1,0:T(8,128)(2,1)} %join.2.refs_4_), custom_call_target="tpu_custom_call", output_to_operand_aliasing={{}: (5, {})} | custom-call | tf_op jit(solution)/shard_map/join/pallas_call | solution.py:538
  160.9 0.2 collective-permute-done.22
  161.1 0.7 constant_dynamic-update-slice_fusion
  161.8 0.7 constant_dynamic-update-slice_fusion.1
  (71 shorter events, 0.7 us)
Async XLA Ops:
  1.3 10.4 %copy-start.21 = (bf16[1024]{0:T(1024)(128)(2,1)S(1)}, bf16[1024]{0:T(1024)(128)(2,1)}, u32[]{:S(2)}) copy-start(bf16[1024]{0:T(1024)(128)(2,1)} %param.18) | copy-start | bytes 6148
  1.3 11.0 %copy-start.20 = (s32[2048]{0:T(1024)S(1)}, s32[2048]{0:T(1024)}, u32[]{:S(2)}) copy-start(s32[2048]{0:T(1024)} %param.31) | copy-start | bytes 24580
  1.3 11.1 %copy-start.19 = (f32[2048,2]{0,1:T(2,128)S(1)}, f32[2048,2]{0,1:T(2,128)}, u32[]{:S(2)}) copy-start(f32[2048,2]{0,1:T(2,128)} %param.24) | copy-start | bytes 49156
  5.2 56.7 %collective-permute-start = (bf16[592,1024]{1,0:T(8,128)(2,1)}, bf16[592,1024]{1,0:T(8,128)(2,1)S(1)}, u32[]{:S(2)}, u32[]{:S(2)}) collective-permute-start(bf16[592,1024]{1,0:T(8,128)(2,1)} %get-tuple-element.89), channel_id=1, source_target_pairs={{0,1},{1,2},{2,3},{3,0},{4,5},{5,6},{6,7},{7,4},{8,9},{9,10},{10,1... | collective-permute-start | bytes 3637256 | tf_op jit(solution)/shard_map/ppermute | solution.py:587
  6.9 55.1 %collective-permute-start.1 = (bf16[592,1024]{1,0:T(8,128)(2,1)}, bf16[592,1024]{1,0:T(8,128)(2,1)S(1)}, u32[]{:S(2)}, u32[]{:S(2)}) collective-permute-start(bf16[592,1024]{1,0:T(8,128)(2,1)} %get-tuple-element.90), channel_id=1, source_target_pairs={{0,3},{1,0},{2,1},{3,2},{4,7},{5,4},{6,5},{7,6},{8,11},{9,8},{10,9... | collective-permute-start | bytes 3637256 | tf_op jit(solution)/shard_map/ppermute | solution.py:587
  8.5 53.4 %collective-permute-start.2 = (bf16[592,1024]{1,0:T(8,128)(2,1)}, bf16[592,1024]{1,0:T(8,128)(2,1)}, u32[]{:S(2)}, u32[]{:S(2)}) collective-permute-start(bf16[592,1024]{1,0:T(8,128)(2,1)} %get-tuple-element.90), channel_id=1, source_target_pairs={{0,1},{1,2},{2,3},{3,0},{4,5},{5,6},{6,7},{7,4},{8,9},{9,10},{10,1... | collective-permute-start | bytes 3637256 | tf_op jit(solution)/shard_map/ppermute | solution.py:587
  8.9 53.1 %collective-permute-start.3 = (bf16[592,1024]{1,0:T(8,128)(2,1)}, bf16[592,1024]{1,0:T(8,128)(2,1)}, u32[]{:S(2)}, u32[]{:S(2)}) collective-permute-start(bf16[592,1024]{1,0:T(8,128)(2,1)} %get-tuple-element.89), channel_id=1, source_target_pairs={{0,3},{1,0},{2,1},{3,2},{4,7},{5,4},{6,5},{7,6},{8,11},{9,8},{10,9... | collective-permute-start | bytes 3637256 | tf_op jit(solution)/shard_map/ppermute | solution.py:587
  13.2 18.5 %copy-start.22 = (bf16[1024]{0:T(1024)(128)(2,1)S(1)}, bf16[1024]{0:T(1024)(128)(2,1)}, u32[]{:S(2)}) copy-start(bf16[1024]{0:T(1024)(128)(2,1)} %param.27) | copy-start | bytes 6148
  26.1 14.5 %all-to-all-start = ((bf16[8,264,128]{2,1,0:T(8,128)(2,1)}), bf16[8,264,128]{2,1,0:T(8,128)(2,1)S(1)}, u32[]{:S(2)}, u32[]{:S(2)}) async-start(bf16[8,264,128]{2,1,0:T(8,128)(2,1)} %get-tuple-element.74), calls=%async_computation | async-start | bytes 1081344 | tf_op jit(solution)/shard_map/all_to_all | solution.py:605
  40.7 0.8 copy-start.6
  43.5 11.0 %all-to-all-start.1 = ((bf16[4,264,128]{2,1,0:T(8,128)(2,1)}), bf16[4,264,128]{2,1,0:T(8,128)(2,1)S(1)}, u32[]{:S(2)}, u32[]{:S(2)}) async-start(bf16[4,264,128]{2,1,0:T(8,128)(2,1)} %get-tuple-element.83), calls=%async_computation.1 | async-start | bytes 540672 | tf_op jit(solution)/shard_map/all_to_all | solution.py:605
  54.5 0.7 copy-start.5
  55.2 89.3 %all-to-all-start.2 = ((bf16[32,136,512]{2,1,0:T(8,128)(2,1)}), bf16[32,136,512]{2,1,0:T(8,128)(2,1)}, u32[]{:S(2)}, u32[]{:S(2)}) async-start(bf16[32,136,512]{2,1,0:T(8,128)(2,1)} %get-tuple-element.130), calls=%async_computation.2 | async-start | bytes 8912896 | tf_op jit(solution)/shard_map/all_to_all | solution.py:615
  61.9 15.5 %copy-start = (bf16[592,1024]{1,0:T(8,128)(2,1)}, bf16[592,1024]{1,0:T(8,128)(2,1)S(1)}, u32[]{:S(2)}) copy-start(bf16[592,1024]{1,0:T(8,128)(2,1)S(1)} %collective-permute-done.rest_8_) | copy-start | bytes 3637252
  61.9 15.4 %copy-start.1 = (bf16[592,1024]{1,0:T(8,128)(2,1)}, bf16[592,1024]{1,0:T(8,128)(2,1)S(1)}, u32[]{:S(2)}) copy-start(bf16[592,1024]{1,0:T(8,128)(2,1)S(1)} %collective-permute-done.1.rest_11_) | copy-start | bytes 3637252
  62.0 3.2 %collective-permute-start.4 = (bf16[592,1024]{1,0:T(8,128)(2,1)S(1)}, bf16[592,1024]{1,0:T(8,128)(2,1)S(1)}, u32[]{:S(2)}, u32[]{:S(2)}) collective-permute-start(bf16[592,1024]{1,0:T(8,128)(2,1)S(1)} %collective-permute-done.rest_8_), channel_id=1, source_target_pairs={{0,4},{4,0},{8,12},{12,8},{16,20},{20,16},{24,28},{28,24},{32,36},... | collective-permute-start | bytes 3637256 | tf_op jit(solution)/shard_map/ppermute | solution.py:588
  62.2 15.2 %collective-permute-start.5 = (bf16[592,1024]{1,0:T(8,128)(2,1)S(1)}, bf16[592,1024]{1,0:T(8,128)(2,1)}, u32[]{:S(2)}, u32[]{:S(2)}) collective-permute-start(bf16[592,1024]{1,0:T(8,128)(2,1)S(1)} %collective-permute-done.1.rest_11_), channel_id=1, source_target_pairs={{0,4},{4,0},{8,12},{12,8},{16,20},{20,16},{24,28},{28,24},{32,36},... | collective-permute-start | bytes 3637256 | tf_op jit(solution)/shard_map/ppermute | solution.py:588
  62.6 14.8 %collective-permute-start.6 = (bf16[592,1024]{1,0:T(8,128)(2,1)}, bf16[592,1024]{1,0:T(8,128)(2,1)}, u32[]{:S(2)}, u32[]{:S(2)}) collective-permute-start(bf16[592,1024]{1,0:T(8,128)(2,1)} %collective-permute-done.2.rest_9_), channel_id=1, source_target_pairs={{0,4},{4,0},{8,12},{12,8},{16,20},{20,16},{24,28},{28,24},{32,36},... | collective-permute-start | bytes 3637256 | tf_op jit(solution)/shard_map/ppermute | solution.py:588
  62.7 14.7 %collective-permute-start.7 = (bf16[592,1024]{1,0:T(8,128)(2,1)}, bf16[592,1024]{1,0:T(8,128)(2,1)}, u32[]{:S(2)}, u32[]{:S(2)}) collective-permute-start(bf16[592,1024]{1,0:T(8,128)(2,1)} %collective-permute-done.3.rest_10_), channel_id=1, source_target_pairs={{0,4},{4,0},{8,12},{12,8},{16,20},{20,16},{24,28},{28,24},{32,36},... | collective-permute-start | bytes 3637256 | tf_op jit(solution)/shard_map/ppermute | solution.py:588
  63.1 38.8 %collective-permute-start.11 = (bf16[592,1024]{1,0:T(8,128)(2,1)S(1)}, bf16[592,1024]{1,0:T(8,128)(2,1)}, u32[]{:S(2)}, u32[]{:S(2)}) collective-permute-start(bf16[592,1024]{1,0:T(8,128)(2,1)S(1)} %collective-permute-done.rest_8_), channel_id=1, source_target_pairs={{0,1},{1,2},{2,3},{3,0},{4,5},{5,6},{6,7},{7,4},{8,9},{9,10},{10,1... | collective-permute-start | bytes 3637256 | tf_op jit(solution)/shard_map/ppermute | solution.py:587
  65.2 1.0 copy-start.2
  66.2 35.7 %collective-permute-start.12 = (bf16[592,1024]{1,0:T(8,128)(2,1)S(1)}, bf16[592,1024]{1,0:T(8,128)(2,1)}, u32[]{:S(2)}, u32[]{:S(2)}) collective-permute-start(bf16[592,1024]{1,0:T(8,128)(2,1)S(1)} %collective-permute-done.1.rest_11_), channel_id=1, source_target_pairs={{0,3},{1,0},{2,1},{3,2},{4,7},{5,4},{6,5},{7,6},{8,11},{9,8},{10,9... | collective-permute-start | bytes 3637256 | tf_op jit(solution)/shard_map/ppermute | solution.py:587
  77.4 19.0 %collective-permute-start.8 = (bf16[256,256]{1,0:T(8,128)(2,1)}, bf16[256,256]{1,0:T(8,128)(2,1)S(1)}, u32[]{:S(2)}, u32[]{:S(2)}) collective-permute-start(bf16[256,256]{1,0:T(8,128)(2,1)} %get-tuple-element.105), channel_id=1, source_target_pairs={{0,1},{1,2},{2,3},{3,0},{4,5},{5,6},{6,7},{7,4},{8,9},{9,10},{10,1... | collective-permute-start | bytes 393224 | tf_op jit(solution)/shard_map/ppermute | solution.py:587
  77.7 24.2 %collective-permute-start.9 = (bf16[256,256]{1,0:T(8,128)(2,1)}, bf16[256,256]{1,0:T(8,128)(2,1)S(1)}, u32[]{:S(2)}, u32[]{:S(2)}) collective-permute-start(bf16[256,256]{1,0:T(8,128)(2,1)} %get-tuple-element.106), channel_id=1, source_target_pairs={{0,3},{1,0},{2,1},{3,2},{4,7},{5,4},{6,5},{7,6},{8,11},{9,8},{10,9... | collective-permute-start | bytes 393224 | tf_op jit(solution)/shard_map/ppermute | solution.py:587
  80.9 21.0 %collective-permute-start.10 = (bf16[256,256]{1,0:T(8,128)(2,1)}, bf16[256,256]{1,0:T(8,128)(2,1)S(1)}, u32[]{:S(2)}, u32[]{:S(2)}) collective-permute-start(bf16[256,256]{1,0:T(8,128)(2,1)} %get-tuple-element.107), channel_id=1, source_target_pairs={{0,2},{1,3},{2,0},{3,1},{4,6},{5,7},{6,4},{7,5},{8,10},{9,11},{10,... | collective-permute-start | bytes 393224 | tf_op jit(solution)/shard_map/ppermute | solution.py:587
  96.4 11.2 %copy-start.13 = (bf16[256,256]{1,0:T(8,128)(2,1)}, bf16[256,256]{1,0:T(8,128)(2,1)S(1)}, u32[]{:S(2)}) copy-start(bf16[256,256]{1,0:T(8,128)(2,1)S(1)} %collective-permute-done.8.rest_1_) | copy-start | bytes 393220
  101.9 5.8 %copy-start.14 = (bf16[256,256]{1,0:T(8,128)(2,1)}, bf16[256,256]{1,0:T(8,128)(2,1)S(1)}, u32[]{:S(2)}) copy-start(bf16[256,256]{1,0:T(8,128)(2,1)S(1)} %collective-permute-done.9.rest_2_) | copy-start | bytes 393220
  101.9 5.8 %copy-start.15 = (bf16[256,256]{1,0:T(8,128)(2,1)}, bf16[256,256]{1,0:T(8,128)(2,1)S(1)}, u32[]{:S(2)}) copy-start(bf16[256,256]{1,0:T(8,128)(2,1)S(1)} %collective-permute-done.10.rest_3_) | copy-start | bytes 393220
  101.9 4.2 %collective-permute-start.13 = (bf16[592,1024]{1,0:T(8,128)(2,1)}, bf16[592,1024]{1,0:T(8,128)(2,1)S(1)}, u32[]{:S(2)}, u32[]{:S(2)}) collective-permute-start(bf16[592,1024]{1,0:T(8,128)(2,1)} %collective-permute-done.11.rest_12_), channel_id=1, source_target_pairs={{0,4},{4,0},{8,12},{12,8},{16,20},{20,16},{24,28},{28,24},{32,36},... | collective-permute-start | bytes 3637256 | tf_op jit(solution)/shard_map/ppermute | solution.py:588
  102.0 4.8 %collective-permute-start.14 = (bf16[592,1024]{1,0:T(8,128)(2,1)}, bf16[592,1024]{1,0:T(8,128)(2,1)S(1)}, u32[]{:S(2)}, u32[]{:S(2)}) collective-permute-start(bf16[592,1024]{1,0:T(8,128)(2,1)} %collective-permute-done.12.rest_13_), channel_id=1, source_target_pairs={{0,4},{4,0},{8,12},{12,8},{16,20},{20,16},{24,28},{28,24},{32,36},... | collective-permute-start | bytes 3637256 | tf_op jit(solution)/shard_map/ppermute | solution.py:588
  102.5 16.9 %collective-permute-start.15 = (bf16[256,256]{1,0:T(8,128)(2,1)}, bf16[256,256]{1,0:T(8,128)(2,1)S(1)}, u32[]{:S(2)}, u32[]{:S(2)}) collective-permute-start(bf16[256,256]{1,0:T(8,128)(2,1)} %get-tuple-element.122), channel_id=1, source_target_pairs={{0,1},{1,2},{2,3},{3,0},{4,5},{5,6},{6,7},{7,4},{8,9},{9,10},{10,1... | collective-permute-start | bytes 393224 | tf_op jit(solution)/shard_map/ppermute | solution.py:587
  104.1 15.2 %collective-permute-start.16 = (bf16[256,256]{1,0:T(8,128)(2,1)}, bf16[256,256]{1,0:T(8,128)(2,1)S(1)}, u32[]{:S(2)}, u32[]{:S(2)}) collective-permute-start(bf16[256,256]{1,0:T(8,128)(2,1)} %get-tuple-element.123), channel_id=1, source_target_pairs={{0,3},{1,0},{2,1},{3,2},{4,7},{5,4},{6,5},{7,6},{8,11},{9,8},{10,9... | collective-permute-start | bytes 393224 | tf_op jit(solution)/shard_map/ppermute | solution.py:587
  106.1 1.6 copy-start.3
  106.8 1.0 copy-start.4
  106.8 12.6 %collective-permute-start.17 = (bf16[256,256]{1,0:T(8,128)(2,1)}, bf16[256,256]{1,0:T(8,128)(2,1)S(1)}, u32[]{:S(2)}, u32[]{:S(2)}) collective-permute-start(bf16[256,256]{1,0:T(8,128)(2,1)} %get-tuple-element.124), channel_id=1, source_target_pairs={{0,2},{1,3},{2,0},{3,1},{4,6},{5,7},{6,4},{7,5},{8,10},{9,11},{10,... | collective-permute-start | bytes 393224 | tf_op jit(solution)/shard_map/ppermute | solution.py:587
  119.4 3.8 %copy-start.16 = (bf16[256,256]{1,0:T(8,128)(2,1)}, bf16[256,256]{1,0:T(8,128)(2,1)S(1)}, u32[]{:S(2)}) copy-start(bf16[256,256]{1,0:T(8,128)(2,1)S(1)} %collective-permute-done.15.rest_1_) | copy-start | bytes 393220
  119.4 3.8 %copy-start.17 = (bf16[256,256]{1,0:T(8,128)(2,1)}, bf16[256,256]{1,0:T(8,128)(2,1)S(1)}, u32[]{:S(2)}) copy-start(bf16[256,256]{1,0:T(8,128)(2,1)S(1)} %collective-permute-done.16.rest_2_) | copy-start | bytes 393220
  119.4 3.8 %copy-start.18 = (bf16[256,256]{1,0:T(8,128)(2,1)}, bf16[256,256]{1,0:T(8,128)(2,1)S(1)}, u32[]{:S(2)}) copy-start(bf16[256,256]{1,0:T(8,128)(2,1)S(1)} %collective-permute-done.17.rest_3_) | copy-start | bytes 393220
  119.4 18.6 %collective-permute-start.20 = (bf16[256,1024]{1,0:T(8,128)(2,1)}, bf16[256,1024]{1,0:T(8,128)(2,1)S(1)}, u32[]{:S(2)}, u32[]{:S(2)}) collective-permute-start(bf16[256,1024]{1,0:T(8,128)(2,1)} %ffn.2.refs_0_), channel_id=1, source_target_pairs={{0,1},{1,2},{2,3},{3,0},{4,5},{5,6},{6,7},{7,4},{8,9},{9,10},{10,1... | collective-permute-start | bytes 1572872 | tf_op jit(solution)/shard_map/ppermute | solution.py:587
  122.9 15.7 %collective-permute-start.21 = (bf16[256,1024]{1,0:T(8,128)(2,1)}, bf16[256,1024]{1,0:T(8,128)(2,1)S(1)}, u32[]{:S(2)}, u32[]{:S(2)}) collective-permute-start(bf16[256,1024]{1,0:T(8,128)(2,1)} %ffn.2.refs_0_), channel_id=1, source_target_pairs={{0,3},{1,0},{2,1},{3,2},{4,7},{5,4},{6,5},{7,6},{8,11},{9,8},{10,9... | collective-permute-start | bytes 1572872 | tf_op jit(solution)/shard_map/ppermute | solution.py:587
  134.7 16.3 %collective-permute-start.18 = (bf16[256,1024]{1,0:T(8,128)(2,1)}, bf16[256,1024]{1,0:T(8,128)(2,1)S(1)}, u32[]{:S(2)}, u32[]{:S(2)}) collective-permute-start(bf16[256,1024]{1,0:T(8,128)(2,1)} %ffn.3.refs_3_), channel_id=1, source_target_pairs={{0,1},{1,2},{2,3},{3,0},{4,5},{5,6},{6,7},{7,4},{8,9},{9,10},{10,1... | collective-permute-start | bytes 1572872 | tf_op jit(solution)/shard_map/ppermute | solution.py:587
  136.5 15.1 %collective-permute-start.19 = (bf16[256,1024]{1,0:T(8,128)(2,1)}, bf16[256,1024]{1,0:T(8,128)(2,1)S(1)}, u32[]{:S(2)}, u32[]{:S(2)}) collective-permute-start(bf16[256,1024]{1,0:T(8,128)(2,1)} %ffn.3.refs_3_), channel_id=1, source_target_pairs={{0,3},{1,0},{2,1},{3,2},{4,7},{5,4},{6,5},{7,6},{8,11},{9,8},{10,9... | collective-permute-start | bytes 1572872 | tf_op jit(solution)/shard_map/ppermute | solution.py:587
  138.0 3.4 %copy-start.9 = (bf16[256,1024]{1,0:T(8,128)(2,1)}, bf16[256,1024]{1,0:T(8,128)(2,1)S(1)}, u32[]{:S(2)}) copy-start(bf16[256,1024]{1,0:T(8,128)(2,1)S(1)} %collective-permute-done.20.refs_1_) | copy-start | bytes 1572868
  138.0 18.6 %collective-permute-start.24 = (bf16[128,1024]{1,0:T(8,128)(2,1)S(1)}, bf16[128,1024]{1,0:T(8,128)(2,1)S(1)}, u32[]{:S(2)}, u32[]{:S(2)}) collective-permute-start(bf16[128,1024]{1,0:T(8,128)(2,1)S(1)} %slice.25), channel_id=1, source_target_pairs={{0,1},{1,2},{2,3},{3,0},{4,5},{5,6},{6,7},{7,4},{8,9},{9,10},{10,1... | collective-permute-start | bytes 786440 | tf_op jit(solution)/shard_map/ppermute | solution.py:587
  138.7 2.7 %copy-start.10 = (bf16[256,1024]{1,0:T(8,128)(2,1)}, bf16[256,1024]{1,0:T(8,128)(2,1)S(1)}, u32[]{:S(2)}) copy-start(bf16[256,1024]{1,0:T(8,128)(2,1)S(1)} %collective-permute-done.21.refs_2_) | copy-start | bytes 1572868
  138.7 18.5 %collective-permute-start.25 = (bf16[128,1024]{1,0:T(8,128)(2,1)S(1)}, bf16[128,1024]{1,0:T(8,128)(2,1)S(1)}, u32[]{:S(2)}, u32[]{:S(2)}) collective-permute-start(bf16[128,1024]{1,0:T(8,128)(2,1)S(1)} %slice.26), channel_id=1, source_target_pairs={{0,3},{1,0},{2,1},{3,2},{4,7},{5,4},{6,5},{7,6},{8,11},{9,8},{10,9... | collective-permute-start | bytes 786440 | tf_op jit(solution)/shard_map/ppermute | solution.py:587
  151.0 6.3 %copy-start.7 = (bf16[256,1024]{1,0:T(8,128)(2,1)}, bf16[256,1024]{1,0:T(8,128)(2,1)S(1)}, u32[]{:S(2)}) copy-start(bf16[256,1024]{1,0:T(8,128)(2,1)S(1)} %collective-permute-done.18.refs_0_) | copy-start | bytes 1572868
  151.6 5.6 %copy-start.8 = (bf16[256,1024]{1,0:T(8,128)(2,1)}, bf16[256,1024]{1,0:T(8,128)(2,1)S(1)}, u32[]{:S(2)}) copy-start(bf16[256,1024]{1,0:T(8,128)(2,1)S(1)} %collective-permute-done.19.refs_1_) | copy-start | bytes 1572868
  151.6 9.5 %collective-permute-start.22 = (bf16[128,1024]{1,0:T(8,128)(2,1)S(1)}, bf16[128,1024]{1,0:T(8,128)(2,1)S(1)}, u32[]{:S(2)}, u32[]{:S(2)}) collective-permute-start(bf16[128,1024]{1,0:T(8,128)(2,1)S(1)} %slice.20), channel_id=1, source_target_pairs={{0,1},{1,2},{2,3},{3,0},{4,5},{5,6},{6,7},{7,4},{8,9},{9,10},{10,1... | collective-permute-start | bytes 786440 | tf_op jit(solution)/shard_map/ppermute | solution.py:587
  151.8 9.3 %collective-permute-start.23 = (bf16[128,1024]{1,0:T(8,128)(2,1)S(1)}, bf16[128,1024]{1,0:T(8,128)(2,1)S(1)}, u32[]{:S(2)}, u32[]{:S(2)}) collective-permute-start(bf16[128,1024]{1,0:T(8,128)(2,1)S(1)} %slice.21), channel_id=1, source_target_pairs={{0,3},{1,0},{2,1},{3,2},{4,7},{5,4},{6,5},{7,6},{8,11},{9,8},{10,9... | collective-permute-start | bytes 786440 | tf_op jit(solution)/shard_map/ppermute | solution.py:587
  156.6 0.7 copy-start.11
  157.3 0.7 copy-start.12
